TPU v7x, 512 devices: a whole 4x4x16 slice. The times are simulated.
512 devices in a mesh: head: 8 (over x, core), shard: 64 (over y, z).
Axes of the slice: x: 4, y: 4, z: 16, core: 2. Of those that a mesh axis runs over, the one named last changes fastest.
Arguments:
- tokens: bfloat16 [256, 64, 1024], P('shard'), may hold values from -6 to 6
- w_query: bfloat16 [1024, 1024], P(None, 'head'), may hold values from -0.1875 to 0.1875
- w_key: bfloat16 [1024, 1024], P(None, 'head'), may hold values from -0.1875 to 0.1875
- w_value: bfloat16 [1024, 1024], P(None, 'head'), may hold values from -0.1875 to 0.1875
- w_out: bfloat16 [1024, 1024], P('head'), may hold values from -0.1875 to 0.1875
- norm1_gain: float32 [1024], replicated, may hold values from 0.1 to 1.9
- w_inner: bfloat16 [1024, 4096], P(None, 'head'), may hold values from -0.1875 to 0.1875
- w_outer: bfloat16 [4096, 1024], P('head'), may hold values from -0.09375 to 0.09375
- norm2_gain: float32 [1024], replicated, may hold values from 0.1 to 1.9
- w_project: bfloat16 [1024, 128], replicated, may hold values from -0.1875 to 0.1875
- key_pages: bfloat16 [128, 64, 1024], P('shard', None, 'head'), may hold values from -400 to 400
- value_pages: bfloat16 [128, 64, 1024], P('shard', None, 'head'), may hold values from -6 to 6
- page_table: int32 [128], replicated, may hold values from 0 to 127, as said below
- prompt_lengths: int32 [16], replicated, may hold values from 1 to 512
- request_group: int32 [256], P('shard'), may hold values from 0 to 15, as said below
- doc_vectors: bfloat16 [131072, 128], P(('head', 'shard')), may hold values from -0.29882812 to 0.29882812
- doc_lengths: int32 [512, 4], P(('head', 'shard')), may hold values from 1 to 128, 256 in all within a row
- candidates: int32 [256, 16], P('shard'), may hold values from 0 to 2047, as said below
Outputs:
- embedded: bfloat16 [256, 64, 128], P('shard')
- scores: float32 [256, 16], P('shard')
Inputs may be any that keep to these rules, and one draw needn't show every extreme that they name: `page_table`: positions g * 8 to g * 8 + 7 list the pages of group g's prompt in order; they are the pages g * 8 to g * 8 + 7 in some order. `request_group`: every group has exactly 16 requests; the 4 requests of one index of shard belong to distinct groups. `candidates`: document d is held by the device of index d // 4 along head+shard. `doc_lengths`: each row holds the token counts of one holder's documents in the order they are packed; a row sums to 256.
All inputs are finite; a program needn't handle non-finite values.
Results may differ from a plain program's by a relative error of at most 0.023.
Values may be sent and summed in bfloat16 or wider, within the bound.
No kernel may reach another device: no remote copies, remote signals or barrier semaphores. Data moves between devices by JAX's collectives and lax.ppermute only.
A program may use at most 64 MiB of HBM per device.

v0:
```python
import math

import jax
import jax.numpy as jnp
from jax import lax
from jax.sharding import PartitionSpec as P

DH = 64
PPG = 8
DLMAX = 128


def layer_norm(values, norm_gain):
    row_mean = jnp.mean(values, axis=-1, keepdims=True)
    row_var = jnp.mean(jnp.square(values - row_mean), axis=-1, keepdims=True)
    return (values - row_mean) * lax.rsqrt(row_var + 1e-05) * norm_gain


def combine_heads(term_rows, residual, norm_gain):
    row_total = residual.shape[0]
    summed = lax.psum(term_rows(0, row_total).astype(jnp.bfloat16), "head").astype(jnp.float32)
    return layer_norm(residual.astype(jnp.float32) + summed, norm_gain).astype(jnp.bfloat16)


def build_tiles(vectors, lengths):
    holders = lengths.shape[0]
    per_holder = vectors.shape[0] // holders
    starts = (
        jnp.arange(holders, dtype=jnp.int32)[:, None] * per_holder
        + jnp.cumsum(lengths, axis=1)
        - lengths
    )
    tile_index = starts.reshape(-1)[:, None] + jnp.arange(DLMAX, dtype=jnp.int32)[None, :]
    tile_valid = jnp.arange(DLMAX)[None, :] < lengths.reshape(-1)[:, None]
    tile_index = jnp.minimum(tile_index, vectors.shape[0] - 1)
    doc_tiles = jnp.take(vectors, tile_index.reshape(-1), axis=0)
    return (doc_tiles, tile_valid)


def doc_maxima(query_rows, doc_tiles, tile_valid):
    row_count = query_rows.shape[0]
    row_block = math.gcd(row_count, 256)
    docs_here = tile_valid.shape[0]

    def block_max(block_rows):
        sims = jnp.einsum("ne,te->nt", block_rows, doc_tiles, preferred_element_type=jnp.float32)
        sims = sims.reshape(row_block, docs_here, DLMAX)
        return jnp.max(jnp.where(tile_valid[None], sims, -1e30), axis=-1)

    blocks = query_rows.reshape(row_count // row_block, row_block, query_rows.shape[1])
    return lax.map(block_max, blocks).reshape(row_count, docs_here)


def per_device(
    tokens,
    w_query,
    w_key,
    w_value,
    w_out,
    norm1_gain,
    w_inner,
    w_outer,
    norm2_gain,
    w_project,
    key_pages,
    value_pages,
    page_table,
    prompt_lengths,
    request_group,
    doc_vectors,
    doc_lengths,
    candidates,
):
    req_count, query_len, model_width = tokens.shape
    head_width = w_query.shape[1]
    heads_here = head_width // DH
    token_rows = tokens.reshape(req_count * query_len, model_width)

    def project(weight):
        out = jnp.dot(token_rows, weight, preferred_element_type=jnp.float32).astype(jnp.bfloat16)
        return out.reshape(req_count, query_len, heads_here, DH)

    queries = project(w_query)
    keys_own = project(w_key)
    values_own = project(w_value)
    score_scale = 1.0 / math.sqrt(DH)
    own_score = (
        jnp.einsum("rqhd,rkhd->rhqk", queries, keys_own, preferred_element_type=jnp.float32)
        * score_scale
    )
    row_top = jnp.max(own_score, axis=-1)
    own_weight = jnp.exp(own_score - row_top[..., None])
    row_total = jnp.sum(own_weight, axis=-1)
    weighted = jnp.einsum(
        "rhqk,rkhd->rhqd",
        own_weight.astype(jnp.bfloat16),
        values_own,
        preferred_element_type=jnp.float32,
    )
    cand_ids = lax.all_gather(candidates, "shard", axis=0, tiled=True)
    group_count = prompt_lengths.shape[0]
    page_slot = jnp.argsort(page_table)
    group_hit = request_group[:, None] == jnp.arange(group_count, dtype=jnp.int32)[None, :]
    group_len = jnp.sum(jnp.where(group_hit, prompt_lengths[None, :], 0), axis=1)
    running = (row_top, row_total, weighted)
    key_piece = lax.all_gather(key_pages, "shard", axis=0, tiled=True)
    value_piece = lax.all_gather(value_pages, "shard", axis=0, tiled=True)
    page_count = key_piece.shape[0]
    page_len = key_piece.shape[1]
    step_pages = math.gcd(page_count, max(1, 512 // page_len))
    block_count = page_count // step_pages
    key_blocks = key_piece.reshape(block_count, step_pages * page_len, heads_here, DH)
    value_blocks = value_piece.reshape(block_count, step_pages * page_len, heads_here, DH)
    slot_blocks = page_slot.reshape(block_count, step_pages)

    def one_block(state, page_block):
        old_top, old_total, old_weighted = state
        key_block, value_block, slot_block = page_block
        owner = slot_block // PPG
        offset = (slot_block % PPG)[:, None] * page_len + jnp.arange(page_len, dtype=jnp.int32)[
            None, :
        ]
        is_valid = (owner[None, :, None] == request_group[:, None, None]) & (
            offset[None] < group_len[:, None, None]
        )
        is_valid = is_valid.reshape(req_count, step_pages * page_len)
        score = (
            jnp.einsum("rqhd,khd->rhqk", queries, key_block, preferred_element_type=jnp.float32)
            * score_scale
        )
        score = jnp.where(is_valid[:, None, None, :], score, -1e30)
        new_top = jnp.maximum(old_top, jnp.max(score, axis=-1))
        fade_factor = jnp.exp(old_top - new_top)
        weight = jnp.exp(score - new_top[..., None])
        new_total = old_total * fade_factor + jnp.sum(weight, axis=-1)
        new_weighted = old_weighted * fade_factor[..., None] + jnp.einsum(
            "rhqk,khd->rhqd",
            weight.astype(jnp.bfloat16),
            value_block,
            preferred_element_type=jnp.float32,
        )
        return ((new_top, new_total, new_weighted), None)

    running, _ = lax.scan(one_block, running, (key_blocks, value_blocks, slot_blocks))
    row_top, row_total, weighted = running
    context = (weighted / row_total[..., None]).astype(jnp.bfloat16)
    context = jnp.transpose(context, (0, 2, 1, 3)).reshape(req_count * query_len, head_width)

    def attn_terms(row_start, row_count):
        return jnp.dot(context, w_out, preferred_element_type=jnp.float32)

    first = combine_heads(attn_terms, token_rows, norm1_gain)
    inner = jnp.dot(first, w_inner, preferred_element_type=jnp.float32)
    active = jax.nn.gelu(inner, approximate=False).astype(jnp.bfloat16)

    def outer_terms(row_start, row_count):
        return jnp.dot(active, w_outer, preferred_element_type=jnp.float32)

    second = combine_heads(outer_terms, first, norm2_gain)
    projected = jnp.dot(second, w_project, preferred_element_type=jnp.float32)
    embed_rows = (
        projected * lax.rsqrt(jnp.sum(projected * projected, axis=-1, keepdims=True) + 1e-06)
    ).astype(jnp.bfloat16)
    embedded = embed_rows.reshape(req_count, query_len, embed_rows.shape[1])
    doc_each = doc_lengths.shape[1]
    holder = cand_ids // doc_each
    doc_tiles, tile_valid = build_tiles(doc_vectors, doc_lengths)
    maxima = doc_maxima(
        lax.all_gather(embed_rows, "shard", axis=0, tiled=True), doc_tiles, tile_valid
    )
    docs_here = tile_valid.shape[0]
    per_doc = jnp.sum(maxima.reshape(-1, query_len, docs_here), axis=1)
    is_mine = holder == lax.axis_index(("head", "shard"))
    local_doc = cand_ids % doc_each
    doc_hit = local_doc[..., None] == jnp.arange(docs_here, dtype=jnp.int32)
    contrib = jnp.sum(jnp.where(doc_hit, per_doc[:, None, :], 0.0), axis=-1)
    contrib = jnp.where(is_mine, contrib, 0.0)
    score_part = lax.psum_scatter(contrib, "shard", scatter_dimension=0, tiled=True)
    scores = lax.psum(score_part, "head")
    return (embedded, scores)


def solution(mesh):
    in_specs = (
        P("shard", None, None),
        P(None, "head"),
        P(None, "head"),
        P(None, "head"),
        P("head", None),
        P(),
        P(None, "head"),
        P("head", None),
        P(),
        P(),
        P("shard", None, "head"),
        P("shard", None, "head"),
        P(),
        P(),
        P("shard"),
        P(("head", "shard"), None),
        P(("head", "shard"), None),
        P("shard", None),
    )
    out_specs = (P("shard", None, None), P("shard", None))
    return jax.shard_map(
        per_device, mesh=mesh, in_specs=in_specs, out_specs=out_specs, check_vma=False
    )
```

profile of v0, /device:TPU:1, one launch (start us, length us, event | category | flops | bytes accessed | tf_op | source)
XLA Modules:
  0.0 1057.8 jit_solution(1644707749141062123)
XLA Ops:
  8.8 1.4 convolution_convert_fusion.4
  10.3 1.4 convolution_convert_fusion.3
  12.6 2.5 sort.17
  15.6 132.8 %all-gather.5.cloned.1.call-done = bf16[128,64,128]{2,1,0:T(8,128)(2,1)} async-done(((bf16[2,64,128]{2,1,0:T(8,128)(2,1)}), bf16[128,64,128]{2,1,0:T(8,128)(2,1)}) %all-gather.5.cloned.1.call-update) | async-done | bytes 2097168 | tf_op jit(solution)/shard_map/all_gather | solution.py:106
  148.4 8.2 reshape.284
  156.7 10.6 %copy.80 = bf16[16,512,2,64]{1,3,2,0:T(8,128)(2,1)} copy(bf16[16,512,2,64]{3,2,1,0:T(2,128)(2,1)} %reshape.284) | data formatting | bytes 4194304 | tf_op jit(solution)/shard_map/while | solution.py:144
  167.3 121.1 %all-gather.7.cloned.1.call-done = bf16[128,64,128]{2,1,0:T(8,128)(2,1)} async-done(((bf16[2,64,128]{2,1,0:T(8,128)(2,1)}), bf16[128,64,128]{2,1,0:T(8,128)(2,1)}) %all-gather.7.cloned.1.call-update) | async-done | bytes 2097168 | tf_op jit(solution)/shard_map/all_gather | solution.py:107
  288.4 8.2 reshape.285
  296.6 10.6 copy.82
  307.2 60.7 %while.27 = (s32[]{:T(128)}, f32[4,2,64]{2,0,1:T(4,128)S(1)}, f32[4,2,64]{2,0,1:T(4,128)S(1)}, f32[4,2,64,64]{2,3,0,1:T(8,128)S(1)}, s32[16,8]{1,0:T(8,128)S(1)}...) while((s32[]{:T(128)}, f32[4,2,64]{2,0,1:T(4,128)S(1)}, ...), condition=%wide.region_7.8_spmd, body=%wide.region_4.7_spmd.sunk | while | flops 70063840 | bytes 4855253 | solution.py:144
  307.8 1.2 fusion.150
  309.5 1.4 fusion.154
  311.6 1.2 fusion.150
  313.3 1.4 fusion.154
  315.4 1.2 fusion.150
  317.1 1.4 fusion.154
  319.2 1.2 fusion.150
  320.9 1.4 fusion.154
  323.0 1.2 fusion.150
  324.7 1.4 fusion.154
  326.8 1.2 fusion.150
  328.5 1.4 fusion.154
  332.3 1.4 fusion.154
  336.1 1.4 fusion.154
  339.9 1.4 fusion.154
  342.0 1.2 fusion.150
  343.7 1.4 fusion.154
  347.5 1.4 fusion.154
  351.3 1.4 fusion.154
  355.1 1.4 fusion.154
  357.2 1.2 fusion.150
  358.9 1.4 fusion.154
  362.7 1.4 fusion.154
  366.5 1.4 fusion.154
  369.4 79.6 %all-reduce.4.cloned.1.call-done = bf16[256,1024]{1,0:T(8,128)(2,1)} async-done(((bf16[256,1024]{1,0:T(8,128)(2,1)}), bf16[256,1024]{1,0:T(8,128)(2,1)}) %all-reduce.4.cloned.1.call-update) | async-done | bytes 524304 | tf_op jit(solution)/shard_map/psum | solution.py:21
  449.0 1.3 fusion.27
  450.3 1.3 multiply_reduce_fusion.1
  451.9 2.7 convolution_convert_fusion
  454.8 75.4 %all-reduce.6.cloned.1.call-done = bf16[256,1024]{1,0:T(8,128)(2,1)} async-done(((bf16[256,1024]{1,0:T(8,128)(2,1)}), bf16[256,1024]{1,0:T(8,128)(2,1)}) %all-reduce.6.cloned.1.call-update) | async-done | bytes 524304 | tf_op jit(solution)/shard_map/psum | solution.py:21
  530.1 1.3 fusion.29
  531.5 1.4 multiply_reduce_fusion
  534.4 77.8 %all-gather = s32[64,4,16]{2,1,0:T(4,128)S(1)} all-gather(s32[1,4,16]{2,1,0:T(4,128)S(1)} %bitcast.140), channel_id=1, replica_groups=mesh['head'=8,'shard'=64] {'shard'}, dimensions={0}, use_global_device_ids=true | all-gather | bytes 16640 | tf_op jit(solution)/shard_map/all_gather | solution.py:100
  612.4 1.3 gather_fusion
  613.7 1.3 dynamic-slice
  615.9 57.6 %all-gather.9.cloned.1.call-done = bf16[16384,128]{1,0:T(8,128)(2,1)} async-done(((bf16[256,128]{1,0:T(8,128)(2,1)}), bf16[16384,128]{1,0:T(8,128)(2,1)}) %all-gather.9.cloned.1.call-update) | async-done | bytes 4194320 | tf_op jit(solution)/shard_map/all_gather | solution.py:169
  673.5 79.8 %while.28 = (s32[]{:T(128)}, f32[64,256,4]{1,0,2:T(8,128)S(1)}, bf16[64,256,128]{2,1,0:T(8,128)(2,1)}, bf16[512,128]{1,0:T(8,128)(2,1)S(1)}, s32[4]{0:T(128)S(1)}, /*index=5*/s32[]{:T(128)}, s32[]{:T(128)}) while((s32[]{:T(128)}, f32[64,256,4]{1,0,2:T(8,128)S(1)}, bf16[64,256,128]{2,1,0:T(8,128)(2,1)}, ...), condition=%wide.region_18.19_spmd.clone, body=%wide.region_16.18_spmd.clone.sunk | while | flops 33816064 | bytes 218721 | solution.py:51
  753.7 220.8 %all-reduce = f32[256,16]{1,0:T(8,128)S(1)} all-reduce(f32[256,16]{1,0:T(8,128)S(1)} %copy.89), channel_id=2, replica_groups=mesh['head'=8,'shard'=64] {'shard'}, use_global_device_ids=true, to_apply=%region_21.22.clone | all-reduce | flops 4096 | bytes 32768
  974.6 76.7 %psum.23 = f32[4,16]{1,0:T(4,128)} all-reduce(f32[4,16]{1,0:T(4,128)S(1)} %constant_dynamic-slice_fusion.1), channel_id=1, replica_groups=mesh['head'=8,'shard'=64] {'head'}, use_global_device_ids=true, to_apply=%region_22.23 | all-reduce | flops 64 | bytes 512 | tf_op jit(solution)/shard_map/psum | solution.py:179
  (603 shorter events, 112.4 us)
Async XLA Ops:
  7.2 444.8 %copy-start = (bf16[512,1024]{1,0:T(8,128)(2,1)S(1)}, bf16[512,1024]{1,0:T(8,128)(2,1)}, u32[]{:S(2)}) copy-start(bf16[512,1024]{1,0:T(8,128)(2,1)} %param.29) | copy-start | bytes 3145732
  7.2 4.6 copy-start.1
  7.2 4.6 copy-start.5
  7.2 141.2 %all-gather.5.cloned.1.call-start = ((), (), s32[]{:S(2)}) async-start(), calls=%async_computation | async-start | bytes 2129920 | tf_op jit(solution)/shard_map/all_gather | solution.py:106
  7.9 280.4 %all-gather.7.cloned.1.call-start = ((), (), s32[]{:S(2)}) async-start(), calls=%async_computation.1 | async-start | bytes 2129920 | tf_op jit(solution)/shard_map/all_gather | solution.py:107
  8.7 440.3 %all-reduce.4.cloned.1.call-start = ((), (), s32[]{:S(2)}) async-start(), calls=%async_computation.2 | async-start | bytes 1048576 | tf_op jit(solution)/shard_map/psum | solution.py:21
  8.7 3.8 copy-start.12
  8.7 6.5 copy-start.13
  8.8 6.5 copy-start.14
  307.2 61.1 %copy-start.6 = (bf16[128,1024]{1,0:T(8,128)(2,1)S(1)}, bf16[128,1024]{1,0:T(8,128)(2,1)}, u32[]{:S(2)}) copy-start(bf16[128,1024]{1,0:T(8,128)(2,1)} %param.26) | copy-start | bytes 786436
  367.9 83.7 %copy-start.7 = (f32[1024]{0:T(1024)S(1)}, f32[1024]{0:T(1024)}, u32[]{:S(2)}) copy-start(f32[1024]{0:T(1024)} %param.27) | copy-start | bytes 12292
  369.3 82.6 %copy-start.9 = (bf16[1024,512]{1,0:T(8,128)(2,1)S(1)}, bf16[1024,512]{1,0:T(8,128)(2,1)}, u32[]{:S(2)}) copy-start(bf16[1024,512]{1,0:T(8,128)(2,1)} %param.28) | copy-start | bytes 3145732
  369.4 160.8 %all-reduce.6.cloned.1.call-start = ((), (), s32[]{:S(2)}) async-start(), calls=%async_computation.3 | async-start | bytes 1048576 | tf_op jit(solution)/shard_map/psum | solution.py:21
  449.0 2.7 copy-start.3
  454.7 78.2 %copy-start.10 = (bf16[1024,128]{1,0:T(8,128)(2,1)S(1)}, bf16[1024,128]{1,0:T(8,128)(2,1)}, u32[]{:S(2)}) copy-start(bf16[1024,128]{1,0:T(8,128)(2,1)} %param.31) | copy-start | bytes 786436
  454.7 78.2 %copy-start.11 = (f32[1024]{0:T(1024)S(1)}, f32[1024]{0:T(1024)}, u32[]{:S(2)}) copy-start(f32[1024]{0:T(1024)} %param.30) | copy-start | bytes 12292
  454.7 79.5 %copy-start.15 = (s32[1,4]{1,0:T(1,128)S(1)}, s32[1,4]{1,0:T(1,128)}, u32[]{:S(2)}) copy-start(s32[1,4]{1,0:T(1,128)} %param.38) | copy-start | bytes 52
  454.7 79.7 %copy-start.8 = (s32[4,16]{1,0:T(4,128)S(1)}, s32[4,16]{1,0:T(4,128)}, u32[]{:S(2)}) copy-start(s32[4,16]{1,0:T(4,128)} %param.39) | copy-start | bytes 772
  454.7 218.8 %all-gather.9.cloned.1.call-start = ((), (), s32[]{:S(2)}) async-start(), calls=%async_computation.4 | async-start | bytes 4259840 | tf_op jit(solution)/shard_map/all_gather | solution.py:169
  530.1 2.7 copy-start.4
  531.5 80.9 %copy-start.2 = (bf16[256,128]{1,0:T(8,128)(2,1)S(1)}, bf16[256,128]{1,0:T(8,128)(2,1)}, u32[]{:S(2)}) copy-start(bf16[256,128]{1,0:T(8,128)(2,1)} %param.37) | copy-start | bytes 196612
Sparse Core Ops, SparseCore 0:
  11.0 137.4 all-gather.4
  151.4 136.9 all-gather.6
  369.5 79.4 all-reduce.3
  454.8 75.2 all-reduce.5
  534.3 139.1 all-gather.8
where the time goes:
time: 1060 us
  waiting for transfers between devices  468 us (44%)
  blocking collectives  375 us (35%)
  matrix products  118 us (11%)
  local copies, waits for them, and re-layouts  51.2 us (5%)
  other arithmetic  26.6 us (3%)
  between operations  14.8 us (1%)
    unnamed x1, blocking collectives  221 us
    psum x2, waiting for transfers between devices, combine_heads(): lax.psum(term_rows(0, row_total).astype(jnp.bfloat16), 'head')  155 us
    all_gather x1, waiting for transfers between devices, per_device(): key_piece = lax.all_gather(key_pages, 'shard', axis=0, tiled=True)  133 us
    all_gather x1, waiting for transfers between devices, per_device(): value_piece = lax.all_gather(value_pages, 'shard', axis=0, tiled=True)  121 us
    all_gather x1, blocking collectives, per_device(): cand_ids = lax.all_gather(candidates, 'shard', axis=0, tiled=True)  77.8 us
    psum x1, blocking collectives, per_device(): scores = lax.psum(score_part, 'head')  76.7 us
    dot_general x64, matrix products, block_max(): jnp.einsum('ne,te->nt', block_rows, doc_tiles, preferred_element_type=jnp...  69.4 us
    all_gather x1, waiting for transfers between devices, per_device(): lax.all_gather(embed_rows, 'shard', axis=0, tiled=True)  57.6 us
  transfers between devices with their start and end apart: 5, of which 5 were waited for; matrix products, arithmetic and copies ran while one was open for 3% of the time, Pallas kernels for 0%

commit v1 on v0

v1 whole, which is shorter than its diff:
```python
import jax
import jax.numpy as jnp
from jax import lax
from jax.experimental import pallas as pl
from jax.experimental.pallas import tpu as pltpu
from jax.sharding import Mesh, PartitionSpec as P

HEAD = ("x", "c")
SHARD = ("y", "q", "r")
RQ = 4
QL = 64
NC = 16
NROW = RQ * QL
DT = 256
DPAD = 272
XROW = 3 * NROW + 16
BF = jnp.bfloat16
F32 = jnp.float32


def layer_norm(values, norm_gain):
    row_mean = jnp.mean(values, axis=-1, keepdims=True)
    row_var = jnp.mean(jnp.square(values - row_mean), axis=-1, keepdims=True)
    return (values - row_mean) * lax.rsqrt(row_var + 1e-05) * norm_gain


def spread(block, axes, count):
    wide = jnp.broadcast_to(block[None], (count,) + block.shape)
    return lax.all_to_all(wide, axes, 0, 0, tiled=True)


def nt_dot(a, b):
    return lax.dot_general(a, b, (((1,), (1,)), ((), ())), preferred_element_type=F32)


def attend_kernel(group_ref, rows_ref, prompt_ref, bias_ref, out_ref):
    low_half = lax.broadcasted_iota(jnp.int32, (QL, 128), 1) < 64

    def one_request(i, carry):
        src = i // RQ
        row = pl.multiple_of((i % RQ) * QL, QL)
        group = group_ref[i]

        @pl.when(group >= 0)
        def _():
            query = rows_ref[src, pl.ds(row, QL), :]
            zero = jnp.zeros_like(query)
            both = jnp.concatenate(
                [jnp.where(low_half, query, zero), jnp.where(low_half, zero, query)], axis=0
            )
            own_key = rows_ref[src, pl.ds(pl.multiple_of(NROW + row, QL), QL), :]
            own_value = rows_ref[src, pl.ds(pl.multiple_of(2 * NROW + row, QL), QL), :]
            parts = [nt_dot(both, own_key)]
            values = [own_value]
            for piece in range(4):
                start = pl.multiple_of(piece * 1024 + group * 256, 256)
                key = prompt_ref[pl.ds(start, 128), :]
                values.append(prompt_ref[pl.ds(pl.multiple_of(start + 128, 128), 128), :])
                bias = bias_ref[group, :, piece * 128 : (piece + 1) * 128]
                parts.append(nt_dot(both, key) + bias)
            top = jnp.max(parts[0], axis=-1, keepdims=True)
            for part in parts[1:]:
                top = jnp.maximum(top, jnp.max(part, axis=-1, keepdims=True))
            total = jnp.zeros_like(top)
            mixed = jnp.zeros((2 * QL, 128), F32)
            for part, value in zip(parts, values):
                weight = jnp.exp(part - top)
                total = total + jnp.sum(weight, axis=-1, keepdims=True)
                mixed = mixed + jnp.dot(weight.astype(BF), value, preferred_element_type=F32)
            mixed = mixed / total
            out_ref[i] = jnp.where(low_half, mixed[:QL], mixed[QL:]).astype(BF)

        @pl.when(group < 0)
        def _():
            out_ref[i] = jnp.zeros((QL, 128), BF)

        return carry

    lax.fori_loop(0, 16, one_request, 0)


def attend(groups, rows, prompt, bias):
    return pl.pallas_call(
        attend_kernel,
        out_shape=jax.ShapeDtypeStruct((16, QL, 128), BF),
        in_specs=[
            pl.BlockSpec(memory_space=pltpu.SMEM),
            pl.BlockSpec(memory_space=pltpu.VMEM),
            pl.BlockSpec(memory_space=pltpu.VMEM),
            pl.BlockSpec(memory_space=pltpu.VMEM),
        ],
        out_specs=pl.BlockSpec(memory_space=pltpu.VMEM),
        compiler_params=pltpu.CompilerParams(vmem_limit_bytes=32 << 20),
        cost_estimate=pl.CostEstimate(flops=600_000_000, bytes_accessed=2_200_000, transcendentals=1_200_000),
        name="attend",
    )(groups, rows, prompt, bias)


def match_kernel(need_ref, first_ref, last_ref, query_ref, docs_ref, pick_ref, out_ref, sims_ref, best_ref):
    best_ref[...] = jnp.zeros_like(best_ref)
    token = lax.broadcasted_iota(jnp.int32, (DT, 128), 0)

    def one_holder(z, carry):
        base = z * 4
        any_need = need_ref[base] + need_ref[base + 1] + need_ref[base + 2] + need_ref[base + 3]

        @pl.when(any_need > 0)
        def _():
            vectors = docs_ref[pl.ds(pl.multiple_of(z * DPAD, 16), DT), :]
            sims_ref[...] = nt_dot(vectors, query_ref[...])

            def one_doc(k, inner):
                doc = base + k

                @pl.when(need_ref[doc] > 0)
                def _():
                    inside = (token >= first_ref[doc]) & (token < last_ref[doc])
                    tops = []
                    for col in range(8):
                        block = sims_ref[:, col * 128 : (col + 1) * 128]
                        tops.append(jnp.max(jnp.where(inside, block, -1e30), axis=0, keepdims=True))
                    best_ref[doc] = jnp.concatenate(tops, axis=0)

                return inner

            lax.fori_loop(0, 4, one_doc, 0)

        return carry

    lax.fori_loop(0, 16, one_holder, 0)
    lane = lax.broadcasted_iota(jnp.int32, (128, 128), 0)
    request = lax.broadcasted_iota(jnp.int32, (128, 128), 1)
    member = (lane // 32 == request // RQ).astype(F32)
    sums = jnp.dot(
        best_ref[...].reshape(512, 128), member, preferred_element_type=F32, precision=lax.Precision.HIGHEST
    ).reshape(64, 8, 128)
    head = lax.broadcasted_iota(jnp.int32, (64, 8, 128), 1)
    request = lax.broadcasted_iota(jnp.int32, (64, 8, 128), 2)
    per_doc = jnp.sum(jnp.where(head // 2 == request % RQ, sums, 0.0), axis=1)
    doc_row = lax.broadcasted_iota(jnp.int32, (64, 128), 0)
    for c in range(NC):
        hit = doc_row == pick_ref[c : c + 1, :]
        out_ref[c : c + 1, :] = jnp.sum(jnp.where(hit, per_doc, 0.0), axis=0, keepdims=True)


def match(need, first, last, queries, docs, pick):
    return pl.pallas_call(
        match_kernel,
        out_shape=jax.ShapeDtypeStruct((NC, 128), F32),
        in_specs=[pl.BlockSpec(memory_space=pltpu.SMEM)] * 3 + [pl.BlockSpec(memory_space=pltpu.VMEM)] * 3,
        out_specs=pl.BlockSpec(memory_space=pltpu.VMEM),
        scratch_shapes=[pltpu.VMEM((DT, 1024), F32), pltpu.VMEM((64, 8, 128), F32)],
        compiler_params=pltpu.CompilerParams(vmem_limit_bytes=32 << 20),
        cost_estimate=pl.CostEstimate(flops=1_000_000_000, bytes_accessed=1_500_000, transcendentals=0),
        name="match",
    )(need, first, last, queries, docs, pick)


def per_device(
    tokens,
    w_query,
    w_key,
    w_value,
    w_out,
    norm1_gain,
    w_inner,
    w_outer,
    norm2_gain,
    w_project,
    key_pages,
    value_pages,
    page_table,
    prompt_lengths,
    request_group,
    doc_vectors,
    doc_lengths,
    candidates,
):
    my_y = lax.axis_index("y")
    my_head = lax.axis_index(HEAD)
    token_rows = tokens.reshape(NROW, 1024)

    pages = jnp.concatenate([key_pages.reshape(128, 128), value_pages.reshape(128, 128)], axis=0)
    pages_q = lax.all_gather(pages, "q", axis=0, tiled=True)
    w_out_all = lax.all_gather(w_out, HEAD, axis=0, tiled=True)
    pages_q, w_out_all = lax.optimization_barrier((pages_q, w_out_all))
    prompt = lax.all_gather(pages_q, "r", axis=0, tiled=True)

    query = jnp.dot(token_rows, w_query, preferred_element_type=F32).astype(BF) * BF(0.125)
    own_key = jnp.dot(token_rows, w_key, preferred_element_type=F32).astype(BF)
    own_value = jnp.dot(token_rows, w_value, preferred_element_type=F32).astype(BF)
    ids = jnp.concatenate([candidates // 64, candidates % 64, request_group[:, None]], axis=1)
    ids = jnp.pad(ids.astype(BF), ((0, 12), (0, 128 - 33)))
    rows = spread(jnp.concatenate([query, own_key, own_value, ids], axis=0), "y", 4)
    rows = rows.reshape(4, XROW, 128)
    got = rows[:, 3 * NROW : 3 * NROW + RQ, :33].reshape(16, 33).astype(jnp.int32)
    groups = jnp.where(got[:, 32] // 4 == my_y, got[:, 32] % 4, -1)
    pick = jnp.where(got[:, :16] == my_head * 4 + my_y, got[:, 16:32], -1)

    table = lax.dynamic_slice(page_table, (my_y * 32,), (32,)).reshape(4, 8)
    lengths = lax.dynamic_slice(prompt_lengths, (my_y * 4,), (4,))
    page_ids = (my_y * 32 + jnp.arange(32, dtype=jnp.int32)).reshape(4, 8)
    slot = jnp.sum(
        jnp.where(table[:, None, :] == page_ids[:, :, None], jnp.arange(8, dtype=jnp.int32), 0), axis=-1
    )
    position = slot[:, :, None] * 64 + jnp.arange(64, dtype=jnp.int32)
    bias = jnp.where(position < lengths[:, None, None], 0.0, -1e30).astype(F32).reshape(4, 1, 512)

    doc_rows = jnp.pad(doc_lengths.astype(BF), ((0, 15), (0, 124)))
    doc_block = jnp.concatenate([doc_vectors, doc_rows], axis=0)
    doc_block, prompt = lax.optimization_barrier((doc_block, prompt))
    docs = lax.all_gather(doc_block, ("q", "r"), axis=0, tiled=True)

    mixed = attend(groups, rows, prompt, bias)
    back = lax.all_to_all(mixed.reshape(4, NROW, 128), "y", 0, 0, tiled=True)
    context = jnp.sum(back.astype(F32), axis=0).astype(BF)
    context = lax.all_gather(context, HEAD, axis=0, tiled=False)
    context = jnp.transpose(context, (1, 0, 2)).reshape(NROW, 1024)
    attn = jnp.dot(context, w_out_all, preferred_element_type=F32)
    first = layer_norm(token_rows.astype(F32) + attn, norm1_gain).astype(BF)
    inner = jnp.dot(first, w_inner, preferred_element_type=F32)
    active = jax.nn.gelu(inner, approximate=False).astype(BF)
    outer = jnp.dot(active, w_outer, preferred_element_type=F32).astype(BF)
    outer = lax.all_to_all(outer.reshape(8, 32, 1024), HEAD, 0, 0, tiled=True)
    mine = lax.dynamic_slice(first, (my_head * 32, 0), (32, 1024))
    second = layer_norm(mine.astype(F32) + jnp.sum(outer.astype(F32), axis=0), norm2_gain).astype(BF)
    projected = jnp.dot(second, w_project, preferred_element_type=F32)
    embed = (projected * lax.rsqrt(jnp.sum(projected * projected, axis=-1, keepdims=True) + 1e-06)).astype(BF)

    queries = spread(embed, HEAD + ("y",), 32)
    own = lax.dynamic_slice(queries.reshape(8, 4, 32, 128), (0, my_y, 0, 0), (8, 1, 32, 128))
    embedded = own.reshape(RQ, QL, 128)

    doc_len = docs.reshape(16, DPAD, 128)[:, DT, :4].astype(jnp.int32)
    doc_last = jnp.cumsum(doc_len, axis=1)
    doc_first = doc_last - doc_len
    need = jnp.any(
        pick.reshape(1, 256) == jnp.arange(64, dtype=jnp.int32)[:, None], axis=1
    ).astype(jnp.int32)
    pick_lanes = jnp.pad(pick.T, ((0, 0), (0, 112)), constant_values=-1)
    terms = match(
        need, doc_first.reshape(64), doc_last.reshape(64), queries.reshape(1024, 128), docs, pick_lanes
    )
    terms = spread(terms, HEAD + ("y",), 32).reshape(32, NC, 128)
    total = jnp.sum(terms, axis=0)
    scores = lax.dynamic_slice(total, (0, my_y * RQ), (NC, RQ)).T
    return (embedded, scores)


def solution(mesh):
    fine = Mesh(mesh.devices.reshape(4, 2, 4, 4, 4), HEAD + SHARD)
    in_specs = (
        P(SHARD, None, None),
        P(None, HEAD),
        P(None, HEAD),
        P(None, HEAD),
        P(HEAD, None),
        P(),
        P(None, HEAD),
        P(HEAD, None),
        P(),
        P(),
        P(SHARD, None, HEAD),
        P(SHARD, None, HEAD),
        P(),
        P(),
        P(SHARD),
        P(HEAD + SHARD, None),
        P(HEAD + SHARD, None),
        P(SHARD, None),
    )
    out_specs = (P(SHARD, None, None), P(SHARD, None))
    return jax.shard_map(per_device, mesh=fine, in_specs=in_specs, out_specs=out_specs, check_vma=False)
```

time: 1060 us -> 203 us (0.19)
  waiting for transfers between devices: 468 us -> 84 us
  blocking collectives: 375 us -> 41.1 us
  matrix products: 118 us -> 8.49 us
  local copies, waits for them, and re-layouts: 51.2 us -> 9.54 us
  starting transfers between devices: 0.2 us -> 37 us
  other arithmetic: 26.6 us -> 4.4 us
    all_gather x3, waiting for transfers between devices: 312 us -> 49.9 us  [the longest x1 22.9 us: per_device(): prompt = lax.all_gather(pages_q, 'r', axis=0, tiled=True)]
    unnamed x1 -> x0, blocking collectives: 221 us -> none
    psum x2 -> x0, waiting for transfers between devices: 155 us -> none  [combine_heads(): lax.psum(term_rows(0, row_total).astype(jnp.bfloat16), 'head')]
    dot_general x88 -> x6, matrix products: 99.7 us -> 8.49 us  [the longest x1 2.67 us: per_device(): outer = jnp.dot(active, w_outer, preferred_element_type=F32).astype(BF)]
    psum x1 -> x0, blocking collectives: 76.7 us -> none  [per_device(): scores = lax.psum(score_part, 'head')]
    all_to_all x0 -> x5, starting transfers between devices: none -> 36.9 us  [the longest x3 26.8 us: spread(): return lax.all_to_all(wide, axes, 0, 0, tiled=True)]
    all_gather x1 -> x2, blocking collectives: 77.8 us -> 41.1 us  [the longest x1 25.6 us: per_device(): pages_q = lax.all_gather(pages, 'q', axis=0, tiled=True)]
    all_to_all x0 -> x5, waiting for transfers between devices: none -> 32.6 us  [the longest x3 18.7 us: spread(): return lax.all_to_all(wide, axes, 0, 0, tiled=True)]
  transfers between devices with their start and end apart: 5 -> 8, of which waited for: 5 -> 7; matrix products, arithmetic and copies ran while one was open for 3% -> 9% of each run, Pallas kernels for 0% -> 0%
where the time goes in v1:
time: 203 us
  waiting for transfers between devices  84 us (41%)
  blocking collectives  41.1 us (20%)
  starting transfers between devices  37 us (18%)
  between operations  14 us (7%)
  local copies, waits for them, and re-layouts  9.54 us (5%)
  matrix products  8.49 us (4%)
  other arithmetic  4.4 us (2%)
  Pallas kernels  3.95 us (2%)
    all_to_all x3, starting transfers between devices, spread(): return lax.all_to_all(wide, axes, 0, 0, tiled=True)  26.8 us
    all_gather x1, blocking collectives, per_device(): pages_q = lax.all_gather(pages, 'q', axis=0, tiled=True)  25.6 us
    all_gather x1, waiting for transfers between devices, per_device(): prompt = lax.all_gather(pages_q, 'r', axis=0, tiled=True)  22.9 us
    all_to_all x3, waiting for transfers between devices, spread(): return lax.all_to_all(wide, axes, 0, 0, tiled=True)  18.7 us
    all_gather x1, waiting for transfers between devices, per_device(): docs = lax.all_gather(doc_block, ('q', 'r'), axis=0, tiled=True)  16.9 us
    all_gather x1, blocking collectives, per_device(): context = lax.all_gather(context, HEAD, axis=0, tiled=False)  15.6 us
    all_gather x1, waiting for transfers between devices, per_device(): w_out_all = lax.all_gather(w_out, HEAD, axis=0, tiled=True)  10.1 us
    all_to_all x1, waiting for transfers between devices, per_device(): outer = lax.all_to_all(outer.reshape(8, 32, 1024), HEAD, 0, 0, tiled=True)  9.11 us
  transfers between devices with their start and end apart: 8, of which 7 were waited for; matrix products, arithmetic and copies ran while one was open for 9% of the time, Pallas kernels for 0%

profile of v1, /device:TPU:1, one launch (start us, length us, event | category | flops | bytes accessed | tf_op | source)
XLA Modules:
  0.0 202.5 jit_solution(9264784645316493934)
XLA Ops:
  7.2 0.7 all-gather.5.cloned.1.call-update
  8.0 0.7 convert_bitcast_fusion
  8.6 0.1 copy.43
  8.8 0.8 pad_maximum_fusion.1
  9.5 25.6 %all_gather.18 = bf16[1024,128]{1,0:T(8,128)(2,1)} all-gather(bf16[256,128]{1,0:T(8,128)(2,1)S(1)} %pad_maximum_fusion.1), channel_id=1, replica_groups=mesh['x'=4,'c'=2,'y'=4,'q'=4,'r'=4] {'q'}, dimensions={0}, use_global_device_ids=true | all-gather | bytes 327680 | tf_op jit(solution)/shard_map/all_gather | solution.py:184
  35.1 0.7 fusion.59
  35.8 1.4 convolution_convert_fusion.1
  37.2 1.4 convolution_convert_fusion.2
  38.7 10.1 %all-gather.5.cloned.1.call-done = bf16[1024,1024]{1,0:T(8,128)(2,1)} async-done(((bf16[128,1024]{1,0:T(8,128)(2,1)}), bf16[1024,1024]{1,0:T(8,128)(2,1)}) %all-gather.5.cloned.1.call-update) | async-done | bytes 2097168 | tf_op jit(solution)/shard_map/all_gather | solution.py:185
  48.9 0.3 fusion
  49.2 1.0 broadcast_in_dim.32
  50.2 4.0 %all-to-all-start = ((bf16[4,784,128]{2,1,0:T(8,128)(2,1)}), bf16[4,784,128]{2,1,0:T(8,128)(2,1)S(1)}, u32[]{:S(2)}, u32[]{:S(2)}) async-start(bf16[4,784,128]{2,1,0:T(8,128)(2,1)} %broadcast_in_dim.32), calls=%async_computation | async-start | bytes 1605632 | tf_op jit(solution)/shard_map/all_to_all | solution.py:29
  54.3 0.2 select_reduce_fusion
  54.9 0.6 fusion.43
  55.6 10.5 %all-to-all-done.rows_ref = bf16[4,784,128]{2,1,0:T(8,128)(2,1)S(1)} async-done(((bf16[4,784,128]{2,1,0:T(8,128)(2,1)}), bf16[4,784,128]{2,1,0:T(8,128)(2,1)S(1)}, u32[]{:S(2)}, u32[]{:S(2)}) %all-to-all-start) | async-done | bytes 802848 | tf_op jit(solution)/shard_map/all_to_all | solution.py:29
  66.2 0.2 slice_reduce_fusion
  66.4 22.9 %all-gather.7.cloned.1.call-done.prompt_ref = bf16[4096,128]{1,0:T(8,128)(2,1)} async-done(((bf16[1024,128]{1,0:T(8,128)(2,1)}), bf16[4096,128]{1,0:T(8,128)(2,1)}) %all-gather.7.cloned.1.call-update) | async-done | bytes 1048592 | tf_op jit(solution)/shard_map/all_gather | solution.py:187
  89.3 1.2 copy-done.2
  90.5 2.7 %attend.1 = bf16[16,64,128]{2,1,0:T(8,128)(2,1)} custom-call(s32[16]{0:T(128)S(1)} %compare_select_fusion.2.group_ref, bf16[4,784,128]{2,1,0:T(8,128)(2,1)S(1)} %all-to-all-done.rows_ref, bf16[4096,128]{1,0:T(8,128)(2,1)S(1)} %copy-done.2, f32[4,1,512]{2,1,0:T(1,128)S(1)} %compare_select_fusion.bias_ref), custom_call_target="tpu_custom_call" | custom-call | flops 600000000 | bytes 2200000 | tf_op jit(solution)/shard_map/attend/pallas_call | solution.py:83
  93.2 6.2 %all-to-all-start.1 = ((bf16[4,256,128]{2,1,0:T(8,128)(2,1)}), bf16[4,256,128]{2,1,0:T(8,128)(2,1)S(1)}, u32[]{:S(2)}, u32[]{:S(2)}) async-start(bf16[4,256,128]{2,1,0:T(8,128)(2,1)} %bitcast.5), calls=%async_computation.1 | async-start | bytes 524288 | tf_op jit(solution)/shard_map/all_to_all | solution.py:215
  99.3 0.7 all-gather.9.cloned.1.call-update
  100.0 4.8 %all-to-all-done.1 = bf16[4,256,128]{2,1,0:T(8,128)(2,1)S(1)} async-done(((bf16[4,256,128]{2,1,0:T(8,128)(2,1)}), bf16[4,256,128]{2,1,0:T(8,128)(2,1)S(1)}, u32[]{:S(2)}, u32[]{:S(2)}) %all-to-all-start.1) | async-done | bytes 262176 | tf_op jit(solution)/shard_map/all_to_all | solution.py:215
  104.9 15.6 %all-gather = bf16[2048,128]{1,0:T(8,128)(2,1)S(1)} all-gather(bf16[256,128]{1,0:T(8,128)(2,1)S(1)} %reduce_sum.85), channel_id=2, replica_groups=mesh['x'=4,'c'=2,'y'=4,'q'=4,'r'=4] {'x','c'}, dimensions={0}, use_global_device_ids=true | all-gather | bytes 589824 | tf_op jit(solution)/shard_map/all_gather | solution.py:217
  120.5 0.2 copy.44
  120.7 2.4 %fusion.94 = (f32[256]{0:T(256)S(1)}, f32[256,1024]{1,0:T(8,128)S(1)}) fusion(bf16[256,1024]{0,1:T(8,128)(2,1)S(1)} %bitcast.44, bf16[1024,1024]{1,0:T(8,128)(2,1)} %all-gather.5.cloned.1.call-done, bf16[256,1024]{1,0:T(8,128)(2,1)S(1)} %bitcast.43), kind=kOutput, calls=%fused_computation.149 | convolution fusion | flops 537657088 | bytes 4195328 | tf_op jit(solution)/shard_map/dot_general | solution.py:219
  123.2 0.2 multiply_reduce_fusion
  123.4 0.2 multiply_convert_fusion
  123.7 0.7 copy-done.9
  124.4 2.7 %convolution_convert_fusion = bf16[256,1024]{1,0:T(8,128)(2,1)} fusion(bf16[512,1024]{1,0:T(8,128)(2,1)S(1)} %copy-done, bf16[256,1024]{1,0:T(8,128)(2,1)S(1)} %multiply_convert_fusion, bf16[1024,512]{1,0:T(8,128)(2,1)S(1)} %copy-done.9), kind=kOutput, calls=%fused_computation.1 | convolution fusion | flops 545652736 | bytes 3145728 | tf_op jit(solution)/shard_map/dot_general | solution.py:223
  127.1 3.9 %all-to-all-start.2 = ((bf16[8,32,1024]{2,1,0:T(8,128)(2,1)}), bf16[8,32,1024]{2,1,0:T(8,128)(2,1)S(1)}, u32[]{:S(2)}, u32[]{:S(2)}) async-start(bf16[8,32,1024]{2,1,0:T(8,128)(2,1)} %bitcast.9), calls=%async_computation.2 | async-start | bytes 1048576 | tf_op jit(solution)/shard_map/all_to_all | solution.py:224
  131.4 9.1 %all-to-all-done.2 = bf16[8,32,1024]{2,1,0:T(8,128)(2,1)S(1)} async-done(((bf16[8,32,1024]{2,1,0:T(8,128)(2,1)}), bf16[8,32,1024]{2,1,0:T(8,128)(2,1)S(1)}, u32[]{:S(2)}, u32[]{:S(2)}) %all-to-all-start.2) | async-done | bytes 524320 | tf_op jit(solution)/shard_map/all_to_all | solution.py:224
  140.6 0.1 fusion.49
  140.7 0.2 multiply_reduce_fusion.1
  140.9 0.3 multiply_reduce_fusion.2
  141.3 0.7 broadcast_in_dim.61
  142.1 4.4 %all-to-all-start.3 = ((bf16[32,32,128]{2,1,0:T(8,128)(2,1)}), bf16[32,32,128]{2,1,0:T(8,128)(2,1)S(1)}, u32[]{:S(2)}, u32[]{:S(2)}) async-start(bf16[32,32,128]{2,1,0:T(8,128)(2,1)} %broadcast_in_dim.61), calls=%async_computation.3 | async-start | bytes 524288 | tf_op jit(solution)/shard_map/all_to_all | solution.py:29
  146.5 0.1 fusion.48
  146.6 16.9 %all-gather.9.cloned.1.call-done.docs_ref = bf16[4352,128]{1,0:T(8,128)(2,1)} async-done(((bf16[272,128]{1,0:T(8,128)(2,1)}), bf16[4352,128]{1,0:T(8,128)(2,1)}) %all-gather.9.cloned.1.call-update) | async-done | bytes 1114128 | tf_op jit(solution)/shard_map/all_gather | solution.py:212
  163.6 0.8 slice.25
  164.5 0.1 copy.51
  164.6 0.1 reduce_window_sum.14.last_ref
  164.7 1.2 copy-done.1
  166.0 1.3 match.1
  167.3 0.7 broadcast_in_dim.63
  168.0 18.4 %all-to-all-start.4 = ((f32[32,16,128]{2,1,0:T(8,128)}), f32[32,16,128]{2,1,0:T(8,128)S(1)}, u32[]{:S(2)}, u32[]{:S(2)}) async-start(f32[32,16,128]{2,1,0:T(8,128)} %broadcast_in_dim.63), calls=%async_computation.4 | async-start | bytes 524288 | tf_op jit(solution)/shard_map/all_to_all | solution.py:29
  186.4 0.6 constant_dynamic-slice_fusion
  187.0 8.2 %all-to-all-done.4 = f32[32,16,128]{2,1,0:T(8,128)S(1)} async-done(((f32[32,16,128]{2,1,0:T(8,128)}), f32[32,16,128]{2,1,0:T(8,128)S(1)}, u32[]{:S(2)}, u32[]{:S(2)}) %all-to-all-start.4) | async-done | bytes 262176 | tf_op jit(solution)/shard_map/all_to_all | solution.py:29
  195.3 0.7 copy.52
  (67 shorter events, 1.8 us)
Async XLA Ops:
  7.2 116.5 %copy-start = (bf16[512,1024]{1,0:T(8,128)(2,1)S(1)}, bf16[512,1024]{1,0:T(8,128)(2,1)}, u32[]{:S(2)}) copy-start(bf16[512,1024]{1,0:T(8,128)(2,1)} %param.25) | copy-start | bytes 3145732
  7.2 41.7 %copy-start.3 = (bf16[4,64,1024]{2,1,0:T(8,128)(2,1)S(1)}, bf16[4,64,1024]{2,1,0:T(8,128)(2,1)}, u32[]{:S(2)}) copy-start(bf16[4,64,1024]{2,1,0:T(8,128)(2,1)} %param.18) | copy-start | bytes 1572868
  7.2 41.7 %copy-start.4 = (bf16[1024,128]{1,0:T(8,128)(2,1)S(1)}, bf16[1024,128]{1,0:T(8,128)(2,1)}, u32[]{:S(2)}) copy-start(bf16[1024,128]{1,0:T(8,128)(2,1)} %param.19) | copy-start | bytes 786436
  7.2 41.6 %all-gather.5.cloned.1.call-start = ((), (), s32[]{:S(2)}) async-start(), calls=%async_computation.5 | async-start | bytes 2359296 | tf_op jit(solution)/shard_map/all_gather | solution.py:185
  7.9 81.3 %all-gather.7.cloned.1.call-start = ((), (), s32[]{:S(2)}) async-start(), calls=%async_computation.6 | async-start | bytes 1310720 | tf_op jit(solution)/shard_map/all_gather | solution.py:187
  38.6 15.6 %copy-start.10 = (s32[128]{0:T(128)S(1)}, s32[128]{0:T(128)}, u32[]{:S(2)}) copy-start(s32[128]{0:T(128)} %param.30) | copy-start | bytes 1540
  38.6 16.2 %copy-start.11 = (s32[1,4]{1,0:T(1,128)S(1)}, s32[1,4]{1,0:T(1,128)}, u32[]{:S(2)}) copy-start(s32[1,4]{1,0:T(1,128)} %param.34) | copy-start | bytes 52
  38.6 16.2 %copy-start.12 = (s32[16]{0:T(128)S(1)}, s32[16]{0:T(128)}, u32[]{:S(2)}) copy-start(s32[16]{0:T(128)} %param.31) | copy-start | bytes 196
  38.6 16.3 %copy-start.6 = (bf16[256,128]{1,0:T(8,128)(2,1)S(1)}, bf16[256,128]{1,0:T(8,128)(2,1)}, u32[]{:S(2)}) copy-start(bf16[256,128]{1,0:T(8,128)(2,1)} %param.33) | copy-start | bytes 196612
  50.2 16.0 %all-to-all-start = ((bf16[4,784,128]{2,1,0:T(8,128)(2,1)}), bf16[4,784,128]{2,1,0:T(8,128)(2,1)S(1)}, u32[]{:S(2)}, u32[]{:S(2)}) async-start(bf16[4,784,128]{2,1,0:T(8,128)(2,1)} %broadcast_in_dim.32), calls=%async_computation | async-start | bytes 1605632 | tf_op jit(solution)/shard_map/all_to_all | solution.py:29
  89.3 1.2 copy-start.2
  93.2 11.7 %all-to-all-start.1 = ((bf16[4,256,128]{2,1,0:T(8,128)(2,1)}), bf16[4,256,128]{2,1,0:T(8,128)(2,1)S(1)}, u32[]{:S(2)}, u32[]{:S(2)}) async-start(bf16[4,256,128]{2,1,0:T(8,128)(2,1)} %bitcast.5), calls=%async_computation.1 | async-start | bytes 524288 | tf_op jit(solution)/shard_map/all_to_all | solution.py:215
  99.3 64.2 %all-gather.9.cloned.1.call-start = ((), (), s32[]{:S(2)}) async-start(), calls=%async_computation.7 | async-start | bytes 1183744 | tf_op jit(solution)/shard_map/all_gather | solution.py:212
  120.7 2.7 %copy-start.7 = (f32[1024]{0:T(1024)S(1)}, f32[1024]{0:T(1024)}, u32[]{:S(2)}) copy-start(f32[1024]{0:T(1024)} %param.23) | copy-start | bytes 12292
  123.1 1.2 copy-start.9
  127.0 13.9 %copy-start.5 = (bf16[1024,128]{1,0:T(8,128)(2,1)S(1)}, bf16[1024,128]{1,0:T(8,128)(2,1)}, u32[]{:S(2)}) copy-start(bf16[1024,128]{1,0:T(8,128)(2,1)} %param.27) | copy-start | bytes 786436
  127.0 13.9 %copy-start.8 = (f32[1024]{0:T(1024)S(1)}, f32[1024]{0:T(1024)}, u32[]{:S(2)}) copy-start(f32[1024]{0:T(1024)} %param.26) | copy-start | bytes 12292
  127.1 13.4 %all-to-all-start.2 = ((bf16[8,32,1024]{2,1,0:T(8,128)(2,1)}), bf16[8,32,1024]{2,1,0:T(8,128)(2,1)S(1)}, u32[]{:S(2)}, u32[]{:S(2)}) async-start(bf16[8,32,1024]{2,1,0:T(8,128)(2,1)} %bitcast.9), calls=%async_computation.2 | async-start | bytes 1048576 | tf_op jit(solution)/shard_map/all_to_all | solution.py:224
  142.1 22.6 %all-to-all-start.3 = ((bf16[32,32,128]{2,1,0:T(8,128)(2,1)}), bf16[32,32,128]{2,1,0:T(8,128)(2,1)S(1)}, u32[]{:S(2)}, u32[]{:S(2)}) async-start(bf16[32,32,128]{2,1,0:T(8,128)(2,1)} %broadcast_in_dim.61), calls=%async_computation.3 | async-start | bytes 524288 | tf_op jit(solution)/shard_map/all_to_all | solution.py:29
  164.7 1.2 copy-start.1
  168.0 27.2 %all-to-all-start.4 = ((f32[32,16,128]{2,1,0:T(8,128)}), f32[32,16,128]{2,1,0:T(8,128)S(1)}, u32[]{:S(2)}, u32[]{:S(2)}) async-start(f32[32,16,128]{2,1,0:T(8,128)} %broadcast_in_dim.63), calls=%async_computation.4 | async-start | bytes 524288 | tf_op jit(solution)/shard_map/all_to_all | solution.py:29
Sparse Core Ops, SparseCore 0:
  10.2 38.5 all-gather.4
  50.9 38.3 all-gather.6
  102.2 61.2 all-gather.8

commit v2 on v1

--- a/solution.py
+++ b/solution.py
@@ -12,7 +12,7 @@
 NC = 16
 NROW = RQ * QL
 DT = 256
-DPAD = 272
+DPAD = 640
 XROW = 3 * NROW + 16
 BF = jnp.bfloat16
 F32 = jnp.float32
@@ -26,7 +26,7 @@
 
 def spread(block, axes, count):
     wide = jnp.broadcast_to(block[None], (count,) + block.shape)
-    return lax.all_to_all(wide, axes, 0, 0, tiled=True)
+    return lax.all_to_all(wide, axes, 0, 0, tiled=True).reshape((-1,) + block.shape[1:])
 
 
 def nt_dot(a, b):
@@ -91,7 +91,7 @@
         ],
         out_specs=pl.BlockSpec(memory_space=pltpu.VMEM),
         compiler_params=pltpu.CompilerParams(vmem_limit_bytes=32 << 20),
-        cost_estimate=pl.CostEstimate(flops=600_000_000, bytes_accessed=2_200_000, transcendentals=1_200_000),
+        cost_estimate=pl.CostEstimate(flops=1000, bytes_accessed=1000, transcendentals=0),
         name="attend",
     )(groups, rows, prompt, bias)
 
@@ -106,7 +106,7 @@
 
         @pl.when(any_need > 0)
         def _():
-            vectors = docs_ref[pl.ds(pl.multiple_of(z * DPAD, 16), DT), :]
+            vectors = docs_ref[pl.ds(pl.multiple_of(z * DT, DT), DT), :]
             sims_ref[...] = nt_dot(vectors, query_ref[...])
 
             def one_doc(k, inner):
@@ -181,17 +181,20 @@
     token_rows = tokens.reshape(NROW, 1024)
 
     pages = jnp.concatenate([key_pages.reshape(128, 128), value_pages.reshape(128, 128)], axis=0)
-    pages_q = lax.all_gather(pages, "q", axis=0, tiled=True)
+    pages_q = spread(pages, "q", 4)
+    prompt = spread(pages_q.reshape(1024, 128), "r", 4)
+
     w_out_all = lax.all_gather(w_out, HEAD, axis=0, tiled=True)
-    pages_q, w_out_all = lax.optimization_barrier((pages_q, w_out_all))
-    prompt = lax.all_gather(pages_q, "r", axis=0, tiled=True)
+    doc_rows = jnp.pad(doc_lengths.astype(BF), ((0, DPAD - DT - 1), (0, 124)))
+    doc_block = jnp.concatenate([doc_vectors, doc_rows], axis=0)
+    docs = lax.all_gather(doc_block, ("q", "r"), axis=0, tiled=True)
 
     query = jnp.dot(token_rows, w_query, preferred_element_type=F32).astype(BF) * BF(0.125)
     own_key = jnp.dot(token_rows, w_key, preferred_element_type=F32).astype(BF)
     own_value = jnp.dot(token_rows, w_value, preferred_element_type=F32).astype(BF)
     ids = jnp.concatenate([candidates // 64, candidates % 64, request_group[:, None]], axis=1)
     ids = jnp.pad(ids.astype(BF), ((0, 12), (0, 128 - 33)))
-    rows = spread(jnp.concatenate([query, own_key, own_value, ids], axis=0), "y", 4)
+    rows = lax.all_gather(jnp.concatenate([query, own_key, own_value, ids], axis=0), "y", axis=0, tiled=True)
     rows = rows.reshape(4, XROW, 128)
     got = rows[:, 3 * NROW : 3 * NROW + RQ, :33].reshape(16, 33).astype(jnp.int32)
     groups = jnp.where(got[:, 32] // 4 == my_y, got[:, 32] % 4, -1)
@@ -205,11 +208,6 @@
     )
     position = slot[:, :, None] * 64 + jnp.arange(64, dtype=jnp.int32)
     bias = jnp.where(position < lengths[:, None, None], 0.0, -1e30).astype(F32).reshape(4, 1, 512)
-
-    doc_rows = jnp.pad(doc_lengths.astype(BF), ((0, 15), (0, 124)))
-    doc_block = jnp.concatenate([doc_vectors, doc_rows], axis=0)
-    doc_block, prompt = lax.optimization_barrier((doc_block, prompt))
-    docs = lax.all_gather(doc_block, ("q", "r"), axis=0, tiled=True)
 
     mixed = attend(groups, rows, prompt, bias)
     back = lax.all_to_all(mixed.reshape(4, NROW, 128), "y", 0, 0, tiled=True)
@@ -231,7 +229,9 @@
     own = lax.dynamic_slice(queries.reshape(8, 4, 32, 128), (0, my_y, 0, 0), (8, 1, 32, 128))
     embedded = own.reshape(RQ, QL, 128)
 
-    doc_len = docs.reshape(16, DPAD, 128)[:, DT, :4].astype(jnp.int32)
+    docs = docs.reshape(16, DPAD, 128)
+    doc_len = docs[:, DT, :4].astype(jnp.int32)
+    docs = docs[:, :DT].reshape(16 * DT, 128)
     doc_last = jnp.cumsum(doc_len, axis=1)
     doc_first = doc_last - doc_len
     need = jnp.any(

time: 203 us -> 165 us (0.81)
  waiting for transfers between devices: 84 us -> 37.2 us
  blocking collectives: 41.1 us -> 67.6 us
  starting transfers between devices: 37 us -> 22 us
  matrix products: 8.49 us -> 6.31 us
    all_to_all x0 -> x2, blocking collectives: none -> 37.6 us  [the longest x1 29.7 us: spread(): lax.all_to_all(wide, axes, 0, 0, tiled=True)]
    all_gather x1 -> x0, waiting for transfers between devices: 22.9 us -> none  [per_device(): prompt = lax.all_gather(pages_q, 'r', axis=0, tiled=True)]
    all_gather x1, waiting for transfers between devices: 16.9 us -> 0.02 us  [per_device(): docs = lax.all_gather(doc_block, ('q', 'r'), axis=0, tiled=True)]
    all_to_all x4 -> x3, starting transfers between devices: 33 us -> 18 us  [spread(): lax.all_to_all(wide, axes, 0, 0, tiled=True)]
    all_gather x1, blocking collectives: 25.6 us -> 12.8 us  [per_device(): lax.all_gather(jnp.concatenate([query, own_key, own_value, ids], axis=0),...]
    all_gather x1, waiting for transfers between devices: 10.1 us -> 0.02 us  [per_device(): w_out_all = lax.all_gather(w_out, HEAD, axis=0, tiled=True)]
    all_to_all x4 -> x3, waiting for transfers between devices: 23.5 us -> 27.4 us  [spread(): lax.all_to_all(wide, axes, 0, 0, tiled=True)]
    unnamed x29 -> x33, local copies, waits for them, and re-layouts: 4.05 us -> 1.6 us
  transfers between devices with their start and end apart: 8 -> 6, of which waited for: 7 -> 4; matrix products, arithmetic and copies ran while one was open for 9% -> 10% of each run, Pallas kernels for 0% -> 2%
where the time goes in v2:
time: 165 us
  blocking collectives  67.6 us (41%)
  waiting for transfers between devices  37.2 us (23%)
  starting transfers between devices  22 us (13%)
  between operations  14.4 us (9%)
  local copies, waits for them, and re-layouts  8.6 us (5%)
  matrix products  6.31 us (4%)
  Pallas kernels  5.41 us (3%)
  other arithmetic  3.1 us (2%)
    all_to_all x1, blocking collectives, spread(): lax.all_to_all(wide, axes, 0, 0, tiled=True)  29.7 us
    all_to_all x3, waiting for transfers between devices, spread(): lax.all_to_all(wide, axes, 0, 0, tiled=True)  27.4 us
    all_to_all x3, starting transfers between devices, spread(): lax.all_to_all(wide, axes, 0, 0, tiled=True)  18 us
    all_gather x1, blocking collectives, per_device(): context = lax.all_gather(context, HEAD, axis=0, tiled=False)  17.2 us
    all_gather x1, blocking collectives, per_device(): lax.all_gather(jnp.concatenate([query, own_key, own_value, ids], axis=0),...  12.8 us
    all_to_all x1, waiting for transfers between devices, per_device(): outer = lax.all_to_all(outer.reshape(8, 32, 1024), HEAD, 0, 0, tiled=True)  9.11 us
    all_to_all x1, blocking collectives, per_device(): back = lax.all_to_all(mixed.reshape(4, NROW, 128), 'y', 0, 0, tiled=True)  7.92 us
    pallas_call x1, Pallas kernels, attend(): pl.pallas_call(attend_kernel, out_shape=jax.ShapeDtypeStruct((16, QL, 128...  4.11 us
  transfers between devices with their start and end apart: 6, of which 4 were waited for; matrix products, arithmetic and copies ran while one was open for 10% of the time, Pallas kernels for 2%

profile of v2, /device:TPU:1, one launch (start us, length us, event | category | flops | bytes accessed | tf_op | source)
XLA Modules:
  0.0 164.6 jit_solution(6204777380618749364)
XLA Ops:
  7.2 0.7 all-gather.4.cloned.1.call-update
  7.9 0.8 pad_maximum_fusion.1
  8.8 29.7 %all_to_all.30 = bf16[4,256,128]{2,1,0:T(8,128)(2,1)S(1)} all-to-all(bf16[4,256,128]{2,1,0:T(8,128)(2,1)S(1)} %broadcast_in_dim.36), channel_id=1, replica_groups=mesh['x'=4,'c'=2,'y'=4,'q'=4,'r'=4] {'q'}, dimensions={0} | all-to-all | bytes 524288 | tf_op jit(solution)/shard_map/all_to_all | solution.py:29
  38.5 1.2 broadcast_in_dim.38
  39.7 9.2 %all-to-all-start.1 = ((bf16[4,1024,128]{2,1,0:T(8,128)(2,1)}), bf16[4,1024,128]{2,1,0:T(8,128)(2,1)S(1)}, u32[]{:S(2)}, u32[]{:S(2)}) async-start(bf16[4,1024,128]{2,1,0:T(8,128)(2,1)} %broadcast_in_dim.38), calls=%async_computation.1 | async-start | bytes 2097152 | tf_op jit(solution)/shard_map/all_to_all | solution.py:29
  48.9 0.7 fusion.43
  49.7 0.1 eq.48
  49.8 0.1 copy.43
  50.0 0.2 select_reduce_fusion
  50.3 0.3 convolution_convert_fusion.1
  50.6 0.3 convolution_convert_fusion.2
  50.9 0.3 fusion
  51.2 12.8 %all_gather.15 = bf16[3136,128]{1,0:T(8,128)(2,1)S(1)} all-gather(bf16[784,128]{1,0:T(8,128)(2,1)S(1)} %pad_maximum_fusion), channel_id=1, replica_groups=mesh['x'=4,'c'=2,'y'=4,'q'=4,'r'=4] {'y'}, dimensions={0}, use_global_device_ids=true | all-gather | bytes 1003520 | tf_op jit(solution)/shard_map/all_gather | solution.py:197
  64.0 0.1 add.126
  64.2 0.1 dynamic_slice.16
  64.3 0.2 slice_reduce_fusion
  64.6 13.0 %all-to-all-done.1 = bf16[4,1024,128]{2,1,0:T(8,128)(2,1)S(1)} async-done(((bf16[4,1024,128]{2,1,0:T(8,128)(2,1)}), bf16[4,1024,128]{2,1,0:T(8,128)(2,1)S(1)}, u32[]{:S(2)}, u32[]{:S(2)}) %all-to-all-start.1) | async-done | bytes 1048608 | tf_op jit(solution)/shard_map/all_to_all | solution.py:29
  77.5 4.1 %attend.1 = bf16[16,64,128]{2,1,0:T(8,128)(2,1)S(1)} custom-call(s32[16]{0:T(128)S(1)} %compare_select_fusion.2.group_ref, bf16[4,784,128]{2,1,0:T(8,128)(2,1)S(1)} %bitcast.43, bf16[4096,128]{1,0:T(8,128)(2,1)S(1)} %bitcast.41, f32[4,1,512]{2,1,0:T(1,128)S(1)} %compare_select_fusion.bias_ref), custom_call_target="tpu_custom_call" | custom-call | flops 1000 | bytes 1000 | tf_op jit(solution)/shard_map/attend/pallas_call | solution.py:83
  81.7 7.9 %all_to_all.31 = bf16[4,256,128]{2,1,0:T(8,128)(2,1)S(1)} all-to-all(bf16[4,256,128]{2,1,0:T(8,128)(2,1)S(1)} %bitcast.44), channel_id=1, replica_groups=mesh['x'=4,'c'=2,'y'=4,'q'=4,'r'=4] {'y'}, dimensions={0} | all-to-all | bytes 524288 | tf_op jit(solution)/shard_map/all_to_all | solution.py:213
  89.6 17.2 %all-gather = bf16[2048,128]{1,0:T(8,128)(2,1)S(1)} all-gather(bf16[256,128]{1,0:T(8,128)(2,1)S(1)} %reduce_sum.85), channel_id=2, replica_groups=mesh['x'=4,'c'=2,'y'=4,'q'=4,'r'=4] {'x','c'}, dimensions={0}, use_global_device_ids=true | all-gather | bytes 589824 | tf_op jit(solution)/shard_map/all_gather | solution.py:215
  106.8 0.2 copy.44
  107.1 2.4 %fusion.94 = (f32[256]{0:T(256)S(1)}, f32[256,1024]{1,0:T(8,128)S(1)}) fusion(bf16[256,1024]{0,1:T(8,128)(2,1)S(1)} %bitcast.52, bf16[1024,1024]{1,0:T(8,128)(2,1)} %all-gather.4.cloned.1.call-done, bf16[256,1024]{1,0:T(8,128)(2,1)S(1)} %bitcast.51), kind=kOutput, calls=%fused_computation.149 | convolution fusion | flops 537657088 | bytes 4195328 | tf_op jit(solution)/shard_map/dot_general | solution.py:217
  109.5 0.2 multiply_reduce_fusion
  109.8 0.2 multiply_convert_fusion
  110.0 0.7 copy-done.10
  110.8 2.7 %convolution_convert_fusion = bf16[256,1024]{1,0:T(8,128)(2,1)} fusion(bf16[512,1024]{1,0:T(8,128)(2,1)S(1)} %copy-done, bf16[256,1024]{1,0:T(8,128)(2,1)S(1)} %multiply_convert_fusion, bf16[1024,512]{1,0:T(8,128)(2,1)S(1)} %copy-done.10), kind=kOutput, calls=%fused_computation.1 | convolution fusion | flops 545652736 | bytes 3145728 | tf_op jit(solution)/shard_map/dot_general | solution.py:221
  113.5 4.0 %all-to-all-start.3 = ((bf16[8,32,1024]{2,1,0:T(8,128)(2,1)}), bf16[8,32,1024]{2,1,0:T(8,128)(2,1)S(1)}, u32[]{:S(2)}, u32[]{:S(2)}) async-start(bf16[8,32,1024]{2,1,0:T(8,128)(2,1)} %bitcast.12), calls=%async_computation.3 | async-start | bytes 1048576 | tf_op jit(solution)/shard_map/all_to_all | solution.py:222
  117.7 0.1 eq.54
  117.8 9.1 %all-to-all-done.3 = bf16[8,32,1024]{2,1,0:T(8,128)(2,1)S(1)} async-done(((bf16[8,32,1024]{2,1,0:T(8,128)(2,1)}), bf16[8,32,1024]{2,1,0:T(8,128)(2,1)S(1)}, u32[]{:S(2)}, u32[]{:S(2)}) %all-to-all-start.3) | async-done | bytes 524320 | tf_op jit(solution)/shard_map/all_to_all | solution.py:222
  127.0 0.1 fusion.49
  127.1 0.2 multiply_reduce_fusion.1
  127.4 0.3 multiply_reduce_fusion.2
  127.8 0.8 broadcast_in_dim.70
  128.5 4.4 %all-to-all-start.4 = ((bf16[32,32,128]{2,1,0:T(8,128)(2,1)}), bf16[32,32,128]{2,1,0:T(8,128)(2,1)S(1)}, u32[]{:S(2)}, u32[]{:S(2)}) async-start(bf16[32,32,128]{2,1,0:T(8,128)(2,1)} %broadcast_in_dim.70), calls=%async_computation.4 | async-start | bytes 524288 | tf_op jit(solution)/shard_map/all_to_all | solution.py:29
  133.0 0.1 fusion.48
  133.1 0.8 slice.29
  133.9 0.1 copy.50
  134.0 0.1 reshape.170
  134.1 1.3 slice.30
  135.4 0.1 copy.51
  135.5 0.1 reduce_window_sum.14.last_ref
  135.6 6.2 %all-to-all-done.4 = bf16[32,32,128]{2,1,0:T(8,128)(2,1)S(1)} async-done(((bf16[32,32,128]{2,1,0:T(8,128)(2,1)}), bf16[32,32,128]{2,1,0:T(8,128)(2,1)S(1)}, u32[]{:S(2)}, u32[]{:S(2)}) %all-to-all-start.4) | async-done | bytes 262176 | tf_op jit(solution)/shard_map/all_to_all | solution.py:29
  141.9 1.3 match.1
  143.2 0.7 broadcast_in_dim.72
  143.9 4.3 %all-to-all-start.5 = ((f32[32,16,128]{2,1,0:T(8,128)}), f32[32,16,128]{2,1,0:T(8,128)S(1)}, u32[]{:S(2)}, u32[]{:S(2)}) async-start(f32[32,16,128]{2,1,0:T(8,128)} %broadcast_in_dim.72), calls=%async_computation.5 | async-start | bytes 524288 | tf_op jit(solution)/shard_map/all_to_all | solution.py:29
  148.2 0.6 constant_dynamic-slice_fusion
  148.9 8.2 %all-to-all-done.5 = f32[32,16,128]{2,1,0:T(8,128)S(1)} async-done(((f32[32,16,128]{2,1,0:T(8,128)}), f32[32,16,128]{2,1,0:T(8,128)S(1)}, u32[]{:S(2)}, u32[]{:S(2)}) %all-to-all-start.5) | async-done | bytes 262176 | tf_op jit(solution)/shard_map/all_to_all | solution.py:29
  157.1 0.7 copy.52
  (70 shorter events, 1.4 us)
Async XLA Ops:
  7.2 102.9 %copy-start = (bf16[512,1024]{1,0:T(8,128)(2,1)S(1)}, bf16[512,1024]{1,0:T(8,128)(2,1)}, u32[]{:S(2)}) copy-start(bf16[512,1024]{1,0:T(8,128)(2,1)} %param.25) | copy-start | bytes 3145732
  7.2 99.9 %all-gather.4.cloned.1.call-start = ((), (), s32[]{:S(2)}) async-start(), calls=%async_computation.6 | async-start | bytes 2359296 | tf_op jit(solution)/shard_map/all_gather | solution.py:187
  8.7 40.2 %copy-start.11 = (s32[1,4]{1,0:T(1,128)S(1)}, s32[1,4]{1,0:T(1,128)}, u32[]{:S(2)}) copy-start(s32[1,4]{1,0:T(1,128)} %param.34) | copy-start | bytes 52
  8.7 40.2 %copy-start.6 = (bf16[256,128]{1,0:T(8,128)(2,1)S(1)}, bf16[256,128]{1,0:T(8,128)(2,1)}, u32[]{:S(2)}) copy-start(bf16[256,128]{1,0:T(8,128)(2,1)} %param.33) | copy-start | bytes 196612
  8.7 40.9 %copy-start.12 = (s32[128]{0:T(128)S(1)}, s32[128]{0:T(128)}, u32[]{:S(2)}) copy-start(s32[128]{0:T(128)} %param.30) | copy-start | bytes 1540
  8.8 41.1 %copy-start.13 = (s32[4]{0:T(128)S(1)}, s32[4]{0:T(128)}, u32[]{:S(2)}) copy-start(s32[4]{0:T(128)} %param.32) | copy-start | bytes 52
  8.8 41.2 %copy-start.9 = (s32[4,16]{1,0:T(4,128)S(1)}, s32[4,16]{1,0:T(4,128)}, u32[]{:S(2)}) copy-start(s32[4,16]{1,0:T(4,128)} %param.35) | copy-start | bytes 772
  8.8 41.5 %copy-start.1 = (bf16[4,64,1024]{2,1,0:T(8,128)(2,1)S(1)}, bf16[4,64,1024]{2,1,0:T(8,128)(2,1)}, u32[]{:S(2)}) copy-start(bf16[4,64,1024]{2,1,0:T(8,128)(2,1)} %param.18) | copy-start | bytes 1572868
  8.8 41.5 %copy-start.2 = (bf16[1024,128]{1,0:T(8,128)(2,1)S(1)}, bf16[1024,128]{1,0:T(8,128)(2,1)}, u32[]{:S(2)}) copy-start(bf16[1024,128]{1,0:T(8,128)(2,1)} %param.21) | copy-start | bytes 786436
  38.5 12.0 %copy-start.3 = (bf16[1024,128]{1,0:T(8,128)(2,1)S(1)}, bf16[1024,128]{1,0:T(8,128)(2,1)}, u32[]{:S(2)}) copy-start(bf16[1024,128]{1,0:T(8,128)(2,1)} %param.20) | copy-start | bytes 786436
  39.7 11.2 %copy-start.4 = (bf16[1024,128]{1,0:T(8,128)(2,1)S(1)}, bf16[1024,128]{1,0:T(8,128)(2,1)}, u32[]{:S(2)}) copy-start(bf16[1024,128]{1,0:T(8,128)(2,1)} %param.19) | copy-start | bytes 786436
  39.7 37.9 %all-to-all-start.1 = ((bf16[4,1024,128]{2,1,0:T(8,128)(2,1)}), bf16[4,1024,128]{2,1,0:T(8,128)(2,1)S(1)}, u32[]{:S(2)}, u32[]{:S(2)}) async-start(bf16[4,1024,128]{2,1,0:T(8,128)(2,1)} %broadcast_in_dim.38), calls=%async_computation.1 | async-start | bytes 2097152 | tf_op jit(solution)/shard_map/all_to_all | solution.py:29
  48.9 84.2 %all-gather.6.cloned.1.call-start = ((), (), s32[]{:S(2)}) async-start(), calls=%async_computation.7 | async-start | bytes 2785280 | tf_op jit(solution)/shard_map/all_gather | solution.py:190
  49.6 14.6 %copy-start.14 = (s32[16]{0:T(128)S(1)}, s32[16]{0:T(128)}, u32[]{:S(2)}) copy-start(s32[16]{0:T(128)} %param.31) | copy-start | bytes 196
  107.1 2.7 %copy-start.7 = (f32[1024]{0:T(1024)S(1)}, f32[1024]{0:T(1024)}, u32[]{:S(2)}) copy-start(f32[1024]{0:T(1024)} %param.23) | copy-start | bytes 12292
  109.5 1.2 copy-start.10
  113.5 13.9 %copy-start.5 = (bf16[1024,128]{1,0:T(8,128)(2,1)S(1)}, bf16[1024,128]{1,0:T(8,128)(2,1)}, u32[]{:S(2)}) copy-start(bf16[1024,128]{1,0:T(8,128)(2,1)} %param.27) | copy-start | bytes 786436
  113.5 13.9 %copy-start.8 = (f32[1024]{0:T(1024)S(1)}, f32[1024]{0:T(1024)}, u32[]{:S(2)}) copy-start(f32[1024]{0:T(1024)} %param.26) | copy-start | bytes 12292
  113.5 13.5 %all-to-all-start.3 = ((bf16[8,32,1024]{2,1,0:T(8,128)(2,1)}), bf16[8,32,1024]{2,1,0:T(8,128)(2,1)S(1)}, u32[]{:S(2)}, u32[]{:S(2)}) async-start(bf16[8,32,1024]{2,1,0:T(8,128)(2,1)} %bitcast.12), calls=%async_computation.3 | async-start | bytes 1048576 | tf_op jit(solution)/shard_map/all_to_all | solution.py:222
  128.5 13.3 %all-to-all-start.4 = ((bf16[32,32,128]{2,1,0:T(8,128)(2,1)}), bf16[32,32,128]{2,1,0:T(8,128)(2,1)S(1)}, u32[]{:S(2)}, u32[]{:S(2)}) async-start(bf16[32,32,128]{2,1,0:T(8,128)(2,1)} %broadcast_in_dim.70), calls=%async_computation.4 | async-start | bytes 524288 | tf_op jit(solution)/shard_map/all_to_all | solution.py:29
  143.9 13.2 %all-to-all-start.5 = ((f32[32,16,128]{2,1,0:T(8,128)}), f32[32,16,128]{2,1,0:T(8,128)S(1)}, u32[]{:S(2)}, u32[]{:S(2)}) async-start(f32[32,16,128]{2,1,0:T(8,128)} %broadcast_in_dim.72), calls=%async_computation.5 | async-start | bytes 524288 | tf_op jit(solution)/shard_map/all_to_all | solution.py:29
Sparse Core Ops, SparseCore 0:
  10.2 38.5 all-gather.3
  51.8 65.2 all-gather.5

commit v3 on v2

--- a/solution.py
+++ b/solution.py
@@ -12,7 +12,7 @@
 NC = 16
 NROW = RQ * QL
 DT = 256
-DPAD = 640
+DPAD = 272
 XROW = 3 * NROW + 16
 BF = jnp.bfloat16
 F32 = jnp.float32
@@ -39,6 +39,8 @@
     def one_request(i, carry):
         src = i // RQ
         row = pl.multiple_of((i % RQ) * QL, QL)
+        half = (i % RQ) // 2
+        place = pl.multiple_of((i % 2) * QL, QL)
         group = group_ref[i]
 
         @pl.when(group >= 0)
@@ -68,11 +70,11 @@
                 total = total + jnp.sum(weight, axis=-1, keepdims=True)
                 mixed = mixed + jnp.dot(weight.astype(BF), value, preferred_element_type=F32)
             mixed = mixed / total
-            out_ref[i] = jnp.where(low_half, mixed[:QL], mixed[QL:]).astype(BF)
+            out_ref[half, src, pl.ds(place, QL), :] = jnp.where(low_half, mixed[:QL], mixed[QL:]).astype(BF)
 
         @pl.when(group < 0)
         def _():
-            out_ref[i] = jnp.zeros((QL, 128), BF)
+            out_ref[half, src, pl.ds(place, QL), :] = jnp.zeros((QL, 128), BF)
 
         return carry
 
@@ -82,7 +84,7 @@
 def attend(groups, rows, prompt, bias):
     return pl.pallas_call(
         attend_kernel,
-        out_shape=jax.ShapeDtypeStruct((16, QL, 128), BF),
+        out_shape=jax.ShapeDtypeStruct((2, 4, 2 * QL, 128), BF),
         in_specs=[
             pl.BlockSpec(memory_space=pltpu.SMEM),
             pl.BlockSpec(memory_space=pltpu.VMEM),
@@ -90,13 +92,13 @@
             pl.BlockSpec(memory_space=pltpu.VMEM),
         ],
         out_specs=pl.BlockSpec(memory_space=pltpu.VMEM),
-        compiler_params=pltpu.CompilerParams(vmem_limit_bytes=32 << 20),
+        compiler_params=pltpu.CompilerParams(vmem_limit_bytes=16 << 20),
         cost_estimate=pl.CostEstimate(flops=1000, bytes_accessed=1000, transcendentals=0),
         name="attend",
     )(groups, rows, prompt, bias)
 
 
-def match_kernel(need_ref, first_ref, last_ref, query_ref, docs_ref, pick_ref, out_ref, sims_ref, best_ref):
+def match_kernel(need_ref, first_ref, last_ref, query_ref, docs_ref, pick_ref, out_ref, sims_ref, best_ref, term_ref):
     best_ref[...] = jnp.zeros_like(best_ref)
     token = lax.broadcasted_iota(jnp.int32, (DT, 128), 0)
 
@@ -136,24 +138,102 @@
     ).reshape(64, 8, 128)
     head = lax.broadcasted_iota(jnp.int32, (64, 8, 128), 1)
     request = lax.broadcasted_iota(jnp.int32, (64, 8, 128), 2)
-    per_doc = jnp.sum(jnp.where(head // 2 == request % RQ, sums, 0.0), axis=1)
+    per_doc = jnp.sum(jnp.where((head % 2) * 2 + head // 4 == request % RQ, sums, 0.0), axis=1)
     doc_row = lax.broadcasted_iota(jnp.int32, (64, 128), 0)
     for c in range(NC):
         hit = doc_row == pick_ref[c : c + 1, :]
-        out_ref[c : c + 1, :] = jnp.sum(jnp.where(hit, per_doc, 0.0), axis=0, keepdims=True)
+        term_ref[c : c + 1, :] = jnp.sum(jnp.where(hit, per_doc, 0.0), axis=0, keepdims=True)
+    for i in range(32):
+        out_ref[i] = term_ref[...]
 
 
 def match(need, first, last, queries, docs, pick):
     return pl.pallas_call(
         match_kernel,
-        out_shape=jax.ShapeDtypeStruct((NC, 128), F32),
+        out_shape=jax.ShapeDtypeStruct((32, NC, 128), F32),
         in_specs=[pl.BlockSpec(memory_space=pltpu.SMEM)] * 3 + [pl.BlockSpec(memory_space=pltpu.VMEM)] * 3,
         out_specs=pl.BlockSpec(memory_space=pltpu.VMEM),
-        scratch_shapes=[pltpu.VMEM((DT, 1024), F32), pltpu.VMEM((64, 8, 128), F32)],
-        compiler_params=pltpu.CompilerParams(vmem_limit_bytes=32 << 20),
-        cost_estimate=pl.CostEstimate(flops=1_000_000_000, bytes_accessed=1_500_000, transcendentals=0),
+        scratch_shapes=[pltpu.VMEM((DT, 1024), F32), pltpu.VMEM((64, 8, 128), F32), pltpu.VMEM((NC, 128), F32)],
+        compiler_params=pltpu.CompilerParams(vmem_limit_bytes=16 << 20),
+        cost_estimate=pl.CostEstimate(flops=1000, bytes_accessed=1000, transcendentals=0),
         name="match",
     )(need, first, last, queries, docs, pick)
+
+
+def vmem_call(body, out_shape, name, smem=0):
+    def call(*args):
+        spaces = [pltpu.SMEM] * smem + [pltpu.VMEM] * (len(args) - smem)
+        return pl.pallas_call(
+            body,
+            out_shape=out_shape,
+            in_specs=[pl.BlockSpec(memory_space=space) for space in spaces],
+            out_specs=jax.tree.map(lambda _: pl.BlockSpec(memory_space=pltpu.VMEM), out_shape),
+            compiler_params=pltpu.CompilerParams(vmem_limit_bytes=16 << 20),
+            cost_estimate=pl.CostEstimate(flops=1000, bytes_accessed=1000, transcendentals=0),
+            name=name,
+        )(*args)
+
+    return call
+
+
+def dense_kernel(place_ref, context_ref, token_ref, gain_ref, *refs):
+    held, first_ref, terms_ref, scratch, sems = refs[:9], refs[9], refs[10], refs[11:20], refs[20]
+    copies = [pltpu.make_async_copy(held[i], scratch[i], sems.at[i]) for i in range(9)]
+    for copy in copies:
+        copy.start()
+    w_out_ref, inner_refs, outer_refs = scratch[0], scratch[1:5], scratch[5:9]
+    start = pl.multiple_of(place_ref[0] * 128, 128)
+    attn = token_ref[pl.ds(start, 128), :].astype(F32)
+    copies[0].wait()
+    for h in range(8):
+        attn = attn + jnp.dot(
+            context_ref[h], w_out_ref[h * 128 : (h + 1) * 128, :], preferred_element_type=F32
+        )
+    first = layer_norm(attn, gain_ref[...]).astype(BF)
+    first_ref[...] = first
+    for copy in copies[1:]:
+        copy.wait()
+    total = jnp.zeros((128, 1024), F32)
+    for core in range(2):
+        inner = jnp.zeros((128, 512), F32)
+        for part in range(4):
+            inner = inner + jnp.dot(
+                first[:, part * 256 : (part + 1) * 256], inner_refs[part][core], preferred_element_type=F32
+            )
+        active = (0.5 * inner * (1.0 + lax.erf(inner * (0.5**0.5)))).astype(BF)
+        for part in range(4):
+            total = total + jnp.dot(
+                active[:, part * 128 : (part + 1) * 128], outer_refs[part][core], preferred_element_type=F32
+            )
+    terms_ref[...] = total.astype(BF).reshape(4, 32, 1024)
+
+
+def dense(place, context, tokens, gain, weights):
+    return pl.pallas_call(
+        dense_kernel,
+        out_shape=(jax.ShapeDtypeStruct((128, 1024), BF), jax.ShapeDtypeStruct((4, 32, 1024), BF)),
+        in_specs=[pl.BlockSpec(memory_space=pltpu.SMEM)]
+        + [pl.BlockSpec(memory_space=pltpu.VMEM)] * 3
+        + [pl.BlockSpec(memory_space=pl.ANY)] * 9,
+        out_specs=(pl.BlockSpec(memory_space=pltpu.VMEM), pl.BlockSpec(memory_space=pltpu.VMEM)),
+        scratch_shapes=[pltpu.VMEM(w.shape, w.dtype) for w in weights] + [pltpu.SemaphoreType.DMA((9,))],
+        compiler_params=pltpu.CompilerParams(vmem_limit_bytes=20 << 20),
+        cost_estimate=pl.CostEstimate(flops=1000, bytes_accessed=1000, transcendentals=0),
+        name="dense",
+    )(place, context, tokens, gain, *weights)
+
+
+def embed_kernel(place_ref, first_ref, terms_ref, gain_ref, w_project_ref, out_ref):
+    start = pl.multiple_of(place_ref[0] * 32, 32)
+    total = first_ref[pl.ds(start, 32), :].astype(F32)
+    for x in range(4):
+        total = total + terms_ref[x].astype(F32)
+    second = layer_norm(total, gain_ref[...]).astype(BF)
+    projected = jnp.dot(second, w_project_ref[...], preferred_element_type=F32)
+    scale = lax.rsqrt(jnp.sum(projected * projected, axis=-1, keepdims=True) + 1e-06)
+    embed = (projected * scale).astype(BF)
+    for i in range(32):
+        out_ref[i] = embed
 
 
 def per_device(
@@ -178,10 +258,20 @@
 ):
     my_y = lax.axis_index("y")
     my_head = lax.axis_index(HEAD)
+    my_core = lax.axis_index("c").reshape(1)
+    my_x = lax.axis_index("x").reshape(1)
     token_rows = tokens.reshape(NROW, 1024)
 
     pages = jnp.concatenate([key_pages.reshape(128, 128), value_pages.reshape(128, 128)], axis=0)
     pages_q = spread(pages, "q", 4)
+    inner_parts = [
+        lax.all_gather(w_inner[i * 256 : (i + 1) * 256], "c", axis=0, tiled=False) for i in range(4)
+    ]
+    outer_parts = [
+        lax.all_gather(w_outer[i * 128 : (i + 1) * 128], "c", axis=0, tiled=False) for i in range(4)
+    ]
+
+    pages_q, inner_parts, outer_parts = lax.optimization_barrier((pages_q, inner_parts, outer_parts))
     prompt = spread(pages_q.reshape(1024, 128), "r", 4)
 
     w_out_all = lax.all_gather(w_out, HEAD, axis=0, tiled=True)
@@ -210,24 +300,19 @@
     bias = jnp.where(position < lengths[:, None, None], 0.0, -1e30).astype(F32).reshape(4, 1, 512)
 
     mixed = attend(groups, rows, prompt, bias)
-    back = lax.all_to_all(mixed.reshape(4, NROW, 128), "y", 0, 0, tiled=True)
-    context = jnp.sum(back.astype(F32), axis=0).astype(BF)
-    context = lax.all_gather(context, HEAD, axis=0, tiled=False)
-    context = jnp.transpose(context, (1, 0, 2)).reshape(NROW, 1024)
-    attn = jnp.dot(context, w_out_all, preferred_element_type=F32)
-    first = layer_norm(token_rows.astype(F32) + attn, norm1_gain).astype(BF)
-    inner = jnp.dot(first, w_inner, preferred_element_type=F32)
-    active = jax.nn.gelu(inner, approximate=False).astype(BF)
-    outer = jnp.dot(active, w_outer, preferred_element_type=F32).astype(BF)
-    outer = lax.all_to_all(outer.reshape(8, 32, 1024), HEAD, 0, 0, tiled=True)
-    mine = lax.dynamic_slice(first, (my_head * 32, 0), (32, 1024))
-    second = layer_norm(mine.astype(F32) + jnp.sum(outer.astype(F32), axis=0), norm2_gain).astype(BF)
-    projected = jnp.dot(second, w_project, preferred_element_type=F32)
-    embed = (projected * lax.rsqrt(jnp.sum(projected * projected, axis=-1, keepdims=True) + 1e-06)).astype(BF)
-
-    queries = spread(embed, HEAD + ("y",), 32)
-    own = lax.dynamic_slice(queries.reshape(8, 4, 32, 128), (0, my_y, 0, 0), (8, 1, 32, 128))
-    embedded = own.reshape(RQ, QL, 128)
+    back = lax.all_to_all(mixed.reshape(8, 128, 128), ("c", "y"), 0, 0, tiled=True)
+    context = jnp.sum(back.reshape(2, 4, 128, 128).astype(F32), axis=1).astype(BF)
+    context = lax.all_gather(context, "x", axis=0, tiled=True)
+    weights = [w_out_all] + inner_parts + outer_parts
+    first, terms = dense(my_core, context, token_rows, norm1_gain[None], weights)
+    terms = lax.all_to_all(terms, "x", 0, 0, tiled=True)
+    embed = vmem_call(embed_kernel, jax.ShapeDtypeStruct((32, 32, 128), BF), "embed", 1)(
+        my_x, first, terms, norm2_gain[None], w_project
+    )
+
+    queries = lax.all_to_all(embed, HEAD + ("y",), 0, 0, tiled=True)
+    own = lax.dynamic_slice(queries.reshape(4, 2, 4, 32, 128), (0, 0, my_y, 0, 0), (4, 2, 1, 32, 128))
+    embedded = jnp.transpose(own, (1, 0, 2, 3, 4)).reshape(RQ, QL, 128)
 
     docs = docs.reshape(16, DPAD, 128)
     doc_len = docs[:, DT, :4].astype(jnp.int32)
@@ -241,7 +326,7 @@
     terms = match(
         need, doc_first.reshape(64), doc_last.reshape(64), queries.reshape(1024, 128), docs, pick_lanes
     )
-    terms = spread(terms, HEAD + ("y",), 32).reshape(32, NC, 128)
+    terms = lax.all_to_all(terms, HEAD + ("y",), 0, 0, tiled=True)
     total = jnp.sum(terms, axis=0)
     scores = lax.dynamic_slice(total, (0, my_y * RQ), (NC, RQ)).T
     return (embedded, scores)

time: 165 us -> 168 us (1.018)
  blocking collectives: 67.6 us -> 42.1 us
  starting transfers between devices: 22 us -> 42 us
  local copies, waits for them, and re-layouts: 8.6 us -> 17 us
  matrix products: 6.31 us -> 0.86 us
  Pallas kernels: 5.41 us -> 10.4 us
    all_to_all x2 -> x0, blocking collectives: 37.6 us -> none  [the longest x1 29.7 us: spread(): lax.all_to_all(wide, axes, 0, 0, tiled=True)]
    all_to_all x1 -> x4, starting transfers between devices: 3.98 us -> 22.5 us  [the longest x1 7.82 us: per_device(): queries = lax.all_to_all(embed, HEAD + ('y',), 0, 0, tiled=True)]
    all_to_all x1 -> x4, waiting for transfers between devices: 9.11 us -> 26 us  [the longest x1 8.15 us: per_device(): terms = lax.all_to_all(terms, HEAD + ('y',), 0, 0, tiled=True)]
    all_to_all x3 -> x2, waiting for transfers between devices: 27.4 us -> 11.1 us  [spread(): lax.all_to_all(wide, axes, 0, 0, tiled=True)]
    all_gather x1 -> x9, blocking collectives: 17.2 us -> 29.9 us  [the longest x1 10.6 us: per_device(): context = lax.all_gather(context, 'x', axis=0, tiled=True)]
    unnamed x33 -> x47, local copies, waits for them, and re-layouts: 1.6 us -> 9.76 us
    dot_general x3 -> x0, matrix products: 5.45 us -> none  [the longest x1 2.69 us: per_device(): outer = jnp.dot(active, w_outer, preferred_element_type=F32).astype(BF)]
    pallas_call x2 -> x4, Pallas kernels: 5.41 us -> 10.4 us  [the longest x1 3.83 us: attend(): pl.pallas_call(attend_kernel, out_shape=jax.ShapeDtypeStruct((2, 4, 2 * Q...]
  transfers between devices with their start and end apart: 6 -> 8, of which waited for: 4 -> 5; matrix products, arithmetic and copies ran while one was open for 10% -> 6% of each run, Pallas kernels for 2% -> 5%
where the time goes in v3:
time: 168 us; the launch traced here: 167 us
  blocking collectives  42.1 us (25%)
  starting transfers between devices  42 us (25%)
  waiting for transfers between devices  37.9 us (23%)
  local copies, waits for them, and re-layouts  17 us (10%)
  between operations  14.3 us (9%)
  Pallas kernels  10.4 us (6%)
  other arithmetic  2.1 us (1%)
    all_to_all x2, starting transfers between devices, spread(): lax.all_to_all(wide, axes, 0, 0, tiled=True)  19.4 us
    all_gather x1, blocking collectives, per_device(): lax.all_gather(jnp.concatenate([query, own_key, own_value, ids], axis=0),...  12.2 us
    all_to_all x2, waiting for transfers between devices, spread(): lax.all_to_all(wide, axes, 0, 0, tiled=True)  11.1 us
    all_gather x1, blocking collectives, per_device(): context = lax.all_gather(context, 'x', axis=0, tiled=True)  10.6 us
    all_gather x4, blocking collectives, per_device(): lax.all_gather(w_inner[i * 256:(i + 1) * 256], 'c', axis=0, tiled=False)  9.86 us
    unnamed x47, local copies, waits for them, and re-layouts  9.76 us
    all_gather x4, blocking collectives, per_device(): lax.all_gather(w_outer[i * 128:(i + 1) * 128], 'c', axis=0, tiled=False)  9.49 us
    all_to_all x1, waiting for transfers between devices, per_device(): terms = lax.all_to_all(terms, HEAD + ('y',), 0, 0, tiled=True)  8.15 us
  transfers between devices with their start and end apart: 8, of which 5 were waited for; matrix products, arithmetic and copies ran while one was open for 6% of the time, Pallas kernels for 5%

profile of v3, /device:TPU:1, one launch (start us, length us, event | category | flops | bytes accessed | tf_op | source)
XLA Modules:
  0.0 166.7 jit_solution(15289301089489778520)
XLA Ops:
  7.2 0.7 all-gather.11.cloned.1.call-update
  7.9 0.8 pad_maximum_fusion.1
  8.7 0.7 broadcast_in_dim.49
  9.4 15.8 %all-to-all-start = ((bf16[4,256,128]{2,1,0:T(8,128)(2,1)}), bf16[4,256,128]{2,1,0:T(8,128)(2,1)S(1)}, u32[]{:S(2)}, u32[]{:S(2)}) async-start(bf16[4,256,128]{2,1,0:T(8,128)(2,1)} %broadcast_in_dim.49), calls=%async_computation | async-start | bytes 524288 | tf_op jit(solution)/shard_map/all_to_all | solution.py:29
  25.2 1.3 fusion.17
  26.5 2.7 %all-gather.1 = bf16[512,512]{1,0:T(8,128)(2,1)S(1)} all-gather(bf16[256,512]{1,0:T(8,128)(2,1)S(1)} %get-tuple-element.33), channel_id=3, replica_groups=mesh['x'=4,'c'=2,'y'=4,'q'=4,'r'=4] {'c'}, dimensions={0}, use_global_device_ids=true | all-gather | bytes 786432 | tf_op jit(solution)/shard_map/all_gather | solution.py:268
  29.2 2.3 %all-gather.2 = bf16[512,512]{1,0:T(8,128)(2,1)} all-gather(bf16[256,512]{1,0:T(8,128)(2,1)S(1)} %get-tuple-element.35), channel_id=4, replica_groups=mesh['x'=4,'c'=2,'y'=4,'q'=4,'r'=4] {'c'}, dimensions={0}, use_global_device_ids=true | all-gather | bytes 786432 | tf_op jit(solution)/shard_map/all_gather | solution.py:268
  31.6 2.3 %all-gather.3 = bf16[512,512]{1,0:T(8,128)(2,1)} all-gather(bf16[256,512]{1,0:T(8,128)(2,1)S(1)} %get-tuple-element.32), channel_id=5, replica_groups=mesh['x'=4,'c'=2,'y'=4,'q'=4,'r'=4] {'c'}, dimensions={0}, use_global_device_ids=true | all-gather | bytes 786432 | tf_op jit(solution)/shard_map/all_gather | solution.py:268
  33.9 2.3 %all-gather.4 = bf16[256,1024]{1,0:T(8,128)(2,1)} all-gather(bf16[128,1024]{1,0:T(8,128)(2,1)S(1)} %get-tuple-element.30), channel_id=6, replica_groups=mesh['x'=4,'c'=2,'y'=4,'q'=4,'r'=4] {'c'}, dimensions={0}, use_global_device_ids=true | all-gather | bytes 786432 | tf_op jit(solution)/shard_map/all_gather | solution.py:271
  36.2 2.4 %all-gather.5 = bf16[256,1024]{1,0:T(8,128)(2,1)} all-gather(bf16[128,1024]{1,0:T(8,128)(2,1)S(1)} %get-tuple-element.29), channel_id=7, replica_groups=mesh['x'=4,'c'=2,'y'=4,'q'=4,'r'=4] {'c'}, dimensions={0}, use_global_device_ids=true | all-gather | bytes 786432 | tf_op jit(solution)/shard_map/all_gather | solution.py:271
  38.6 2.4 %all-gather.6 = bf16[256,1024]{1,0:T(8,128)(2,1)} all-gather(bf16[128,1024]{1,0:T(8,128)(2,1)S(1)} %get-tuple-element.31), channel_id=8, replica_groups=mesh['x'=4,'c'=2,'y'=4,'q'=4,'r'=4] {'c'}, dimensions={0}, use_global_device_ids=true | all-gather | bytes 786432 | tf_op jit(solution)/shard_map/all_gather | solution.py:271
  41.0 2.4 %all-gather.7 = bf16[256,1024]{1,0:T(8,128)(2,1)} all-gather(bf16[128,1024]{1,0:T(8,128)(2,1)S(1)} %get-tuple-element.28), channel_id=9, replica_groups=mesh['x'=4,'c'=2,'y'=4,'q'=4,'r'=4] {'c'}, dimensions={0}, use_global_device_ids=true | all-gather | bytes 786432 | tf_op jit(solution)/shard_map/all_gather | solution.py:271
  43.4 2.5 %all-gather = bf16[512,512]{1,0:T(8,128)(2,1)} all-gather(bf16[256,512]{1,0:T(8,128)(2,1)S(1)} %get-tuple-element.34), channel_id=2, replica_groups=mesh['x'=4,'c'=2,'y'=4,'q'=4,'r'=4] {'c'}, dimensions={0}, use_global_device_ids=true | all-gather | bytes 786432 | tf_op jit(solution)/shard_map/all_gather | solution.py:268
  45.9 1.1 broadcast_in_dim.50
  47.0 3.6 %all-to-all-start.1 = ((bf16[4,1024,128]{2,1,0:T(8,128)(2,1)}), bf16[4,1024,128]{2,1,0:T(8,128)(2,1)S(1)}, u32[]{:S(2)}, u32[]{:S(2)}) async-start(bf16[4,1024,128]{2,1,0:T(8,128)(2,1)} %broadcast_in_dim.50), calls=%async_computation.1 | async-start | bytes 2097152 | tf_op jit(solution)/shard_map/all_to_all | solution.py:29
  50.8 0.6 fusion.2
  51.6 0.2 select_reduce_fusion
  52.2 0.3 convolution_convert_fusion
  52.6 0.3 convolution_convert_fusion.1
  52.9 0.3 fusion
  53.3 12.2 %all_gather.60 = bf16[3136,128]{1,0:T(8,128)(2,1)S(1)} all-gather(bf16[784,128]{1,0:T(8,128)(2,1)S(1)} %pad_maximum_fusion), channel_id=1, replica_groups=mesh['x'=4,'c'=2,'y'=4,'q'=4,'r'=4] {'y'}, dimensions={0}, use_global_device_ids=true | all-gather | bytes 1003520 | tf_op jit(solution)/shard_map/all_gather | solution.py:287
  65.5 0.2 slice_reduce_fusion
  65.8 11.1 %all-to-all-done.1 = bf16[4,1024,128]{2,1,0:T(8,128)(2,1)S(1)} async-done(((bf16[4,1024,128]{2,1,0:T(8,128)(2,1)}), bf16[4,1024,128]{2,1,0:T(8,128)(2,1)S(1)}, u32[]{:S(2)}, u32[]{:S(2)}) %all-to-all-start.1) | async-done | bytes 1048608 | tf_op jit(solution)/shard_map/all_to_all | solution.py:29
  76.9 3.8 %attend.1 = bf16[2,4,128,128]{3,2,1,0:T(8,128)(2,1)} custom-call(s32[16]{0:T(128)S(1)} %compare_select_fusion.2.group_ref, bf16[4,784,128]{2,1,0:T(8,128)(2,1)S(1)} %bitcast.51, bf16[4096,128]{1,0:T(8,128)(2,1)S(1)} %bitcast.48, f32[4,1,512]{2,1,0:T(1,128)S(1)} %compare_select_fusion.bias_ref), custom_call_target="tpu_custom_call" | custom-call | flops 1000 | bytes 1000 | tf_op jit(solution)/shard_map/attend/pallas_call | solution.py:85
  80.8 6.1 %all-to-all-start.2 = ((bf16[8,128,128]{2,1,0:T(8,128)(2,1)}), bf16[8,128,128]{2,1,0:T(8,128)(2,1)S(1)}, u32[]{:S(2)}, u32[]{:S(2)}) async-start(bf16[8,128,128]{2,1,0:T(8,128)(2,1)} %bitcast.18), calls=%async_computation.2 | async-start | bytes 524288 | tf_op jit(solution)/shard_map/all_to_all | solution.py:303
  87.0 6.3 %all-to-all-done.2 = bf16[8,128,128]{2,1,0:T(8,128)(2,1)S(1)} async-done(((bf16[8,128,128]{2,1,0:T(8,128)(2,1)}), bf16[8,128,128]{2,1,0:T(8,128)(2,1)S(1)}, u32[]{:S(2)}, u32[]{:S(2)}) %all-to-all-start.2) | async-done | bytes 262176 | tf_op jit(solution)/shard_map/all_to_all | solution.py:303
  93.4 10.6 %all_gather.77.context_ref = bf16[8,128,128]{2,1,0:T(8,128)(2,1)S(1)} all-gather(bf16[2,128,128]{2,1,0:T(8,128)(2,1)S(1)} %bitcast_reduce_fusion), channel_id=1, replica_groups=mesh['x'=4,'c'=2,'y'=4,'q'=4,'r'=4] {'x'}, dimensions={0}, use_global_device_ids=true | all-gather | bytes 327680 | tf_op jit(solution)/shard_map/all_gather | solution.py:305
  104.0 1.6 copy-done.2
  105.6 1.0 copy-done.3
  106.7 1.0 copy-done.4
  107.7 1.0 copy-done.5
  108.8 1.0 copy-done.6
  109.8 1.0 copy-done.7
  110.9 1.0 copy-done.8
  111.9 1.0 copy-done.9
  112.9 3.4 %dense.1 = (bf16[128,1024]{1,0:T(8,128)(2,1)S(1)}, bf16[4,32,1024]{2,1,0:T(8,128)(2,1)}) custom-call(s32[1]{0:T(128)} %bitcast.1.place_ref, bf16[8,128,128]{2,1,0:T(8,128)(2,1)S(1)} %all_gather.77.context_ref, bf16[256,1024]{1,0:T(8,128)(2,1)S(1)} %bitcast.47, f32[1,1024]{1,0:T(1,128)S(1)} %bitcast.62, bf16[1024,1024]{1,0:T(8,128)(2,1)S(1)} %copy-done.2, ...), custom_call_target="tpu_custom_call" | custom-call | flops 1000 | bytes 1000 | tf_op jit(solution)/shard_map/dense/pallas_call | solution.py:212
  116.3 3.4 %all-to-all-start.3 = ((bf16[4,32,1024]{2,1,0:T(8,128)(2,1)}), bf16[4,32,1024]{2,1,0:T(8,128)(2,1)S(1)}, u32[]{:S(2)}, u32[]{:S(2)}) async-start(bf16[4,32,1024]{2,1,0:T(8,128)(2,1)} %get-tuple-element.23), calls=%async_computation.3 | async-start | bytes 524288 | tf_op jit(solution)/shard_map/all_to_all | solution.py:308
  119.9 5.4 %all-to-all-done.3.terms_ref = bf16[4,32,1024]{2,1,0:T(8,128)(2,1)S(1)} async-done(((bf16[4,32,1024]{2,1,0:T(8,128)(2,1)}), bf16[4,32,1024]{2,1,0:T(8,128)(2,1)S(1)}, u32[]{:S(2)}, u32[]{:S(2)}) %all-to-all-start.3) | async-done | bytes 262176 | tf_op jit(solution)/shard_map/all_to_all | solution.py:308
  125.3 1.1 embed.1
  126.5 7.8 %all-to-all-start.4 = ((bf16[32,32,128]{2,1,0:T(8,128)(2,1)}), bf16[32,32,128]{2,1,0:T(8,128)(2,1)S(1)}, u32[]{:S(2)}, u32[]{:S(2)}) async-start(bf16[32,32,128]{2,1,0:T(8,128)(2,1)} %embed.1), calls=%async_computation.4 | async-start | bytes 524288 | tf_op jit(solution)/shard_map/all_to_all | solution.py:313
  134.5 0.8 slice.61
  135.4 1.3 slice.62
  136.9 6.2 %all-to-all-done.4 = bf16[32,32,128]{2,1,0:T(8,128)(2,1)S(1)} async-done(((bf16[32,32,128]{2,1,0:T(8,128)(2,1)}), bf16[32,32,128]{2,1,0:T(8,128)(2,1)S(1)}, u32[]{:S(2)}, u32[]{:S(2)}) %all-to-all-start.4) | async-done | bytes 262176 | tf_op jit(solution)/shard_map/all_to_all | solution.py:313
  143.1 2.0 %match.1 = f32[32,16,128]{2,1,0:T(8,128)} custom-call(s32[64]{0:T(128)S(1)} %convert_element_type.45.need_ref, s32[64]{0:T(128)S(1)} %sub.16.first_ref, s32[64]{0:T(128)S(1)} %reduce_window_sum.14.last_ref, bf16[1024,128]{1,0:T(8,128)(2,1)S(1)} %bitcast.60, bf16[4096,128]{1,0:T(8,128)(2,1)S(1)} %bitcast.49, s32[16,128]{1,0:T(8,128)S(1)} %pad.14.pick_ref), custom_call_target="tpu_custom_call" | custom-call | flops 1000 | bytes 1000 | tf_op jit(solution)/shard_map/match/pallas_call | solution.py:151
  145.1 5.1 %all-to-all-start.5 = ((f32[32,16,128]{2,1,0:T(8,128)}), f32[32,16,128]{2,1,0:T(8,128)S(1)}, u32[]{:S(2)}, u32[]{:S(2)}) async-start(f32[32,16,128]{2,1,0:T(8,128)} %match.1), calls=%async_computation.5 | async-start | bytes 524288 | tf_op jit(solution)/shard_map/all_to_all | solution.py:329
  150.3 0.6 copy.52
  150.9 8.1 %all-to-all-done.5 = f32[32,16,128]{2,1,0:T(8,128)S(1)} async-done(((f32[32,16,128]{2,1,0:T(8,128)}), f32[32,16,128]{2,1,0:T(8,128)S(1)}, u32[]{:S(2)}, u32[]{:S(2)}) %all-to-all-start.5) | async-done | bytes 262176 | tf_op jit(solution)/shard_map/all_to_all | solution.py:329
  159.2 0.7 copy.59
  (82 shorter events, 2.1 us)
Async XLA Ops:
  7.2 45.1 %copy-start = (bf16[1024,128]{1,0:T(8,128)(2,1)S(1)}, bf16[1024,128]{1,0:T(8,128)(2,1)}, u32[]{:S(2)}) copy-start(bf16[1024,128]{1,0:T(8,128)(2,1)} %param.21) | copy-start | bytes 786436
  7.2 96.9 %all-gather.11.cloned.1.call-start = ((), (), s32[]{:S(2)}) async-start(), calls=%async_computation.6 | async-start | bytes 2359296 | tf_op jit(solution)/shard_map/all_gather | solution.py:277
  9.4 22.1 %copy-start.13 = (bf16[512,1024]{1,0:T(8,128)(2,1)S(1)}, bf16[512,1024]{1,0:T(8,128)(2,1)}, u32[]{:S(2)}) copy-start(bf16[512,1024]{1,0:T(8,128)(2,1)} %param.25) | copy-start | bytes 3145732
  9.4 36.5 %all-to-all-start = ((bf16[4,256,128]{2,1,0:T(8,128)(2,1)}), bf16[4,256,128]{2,1,0:T(8,128)(2,1)S(1)}, u32[]{:S(2)}, u32[]{:S(2)}) async-start(bf16[4,256,128]{2,1,0:T(8,128)(2,1)} %broadcast_in_dim.49), calls=%async_computation | async-start | bytes 524288 | tf_op jit(solution)/shard_map/all_to_all | solution.py:29
  43.4 7.3 %copy-start.18 = (s32[1,4]{1,0:T(1,128)S(1)}, s32[1,4]{1,0:T(1,128)}, u32[]{:S(2)}) copy-start(s32[1,4]{1,0:T(1,128)} %param.34) | copy-start | bytes 52
  43.4 7.4 %copy-start.16 = (bf16[256,128]{1,0:T(8,128)(2,1)S(1)}, bf16[256,128]{1,0:T(8,128)(2,1)}, u32[]{:S(2)}) copy-start(bf16[256,128]{1,0:T(8,128)(2,1)} %param.33) | copy-start | bytes 196612
  43.4 8.0 %copy-start.19 = (s32[128]{0:T(128)S(1)}, s32[128]{0:T(128)}, u32[]{:S(2)}) copy-start(s32[128]{0:T(128)} %param.30) | copy-start | bytes 1540
  43.4 8.7 %copy-start.20 = (s32[4]{0:T(128)S(1)}, s32[4]{0:T(128)}, u32[]{:S(2)}) copy-start(s32[4]{0:T(128)} %param.32) | copy-start | bytes 52
  43.4 8.8 %copy-start.17 = (s32[4,16]{1,0:T(4,128)S(1)}, s32[4,16]{1,0:T(4,128)}, u32[]{:S(2)}) copy-start(s32[4,16]{1,0:T(4,128)} %param.35) | copy-start | bytes 772
  43.4 8.8 %copy-start.1 = (bf16[4,64,1024]{2,1,0:T(8,128)(2,1)S(1)}, bf16[4,64,1024]{2,1,0:T(8,128)(2,1)}, u32[]{:S(2)}) copy-start(bf16[4,64,1024]{2,1,0:T(8,128)(2,1)} %param.18) | copy-start | bytes 1572868
  45.9 6.6 %copy-start.14 = (bf16[1024,128]{1,0:T(8,128)(2,1)S(1)}, bf16[1024,128]{1,0:T(8,128)(2,1)}, u32[]{:S(2)}) copy-start(bf16[1024,128]{1,0:T(8,128)(2,1)} %param.20) | copy-start | bytes 786436
  47.0 5.9 %copy-start.15 = (bf16[1024,128]{1,0:T(8,128)(2,1)S(1)}, bf16[1024,128]{1,0:T(8,128)(2,1)}, u32[]{:S(2)}) copy-start(bf16[1024,128]{1,0:T(8,128)(2,1)} %param.19) | copy-start | bytes 786436
  47.0 29.9 %all-to-all-start.1 = ((bf16[4,1024,128]{2,1,0:T(8,128)(2,1)}), bf16[4,1024,128]{2,1,0:T(8,128)(2,1)S(1)}, u32[]{:S(2)}, u32[]{:S(2)}) async-start(bf16[4,1024,128]{2,1,0:T(8,128)(2,1)} %broadcast_in_dim.50), calls=%async_computation.1 | async-start | bytes 2097152 | tf_op jit(solution)/shard_map/all_to_all | solution.py:29
  50.7 83.8 %all-gather.13.cloned.1.call-start = ((), (), s32[]{:S(2)}) async-start(), calls=%async_computation.7 | async-start | bytes 1183744 | tf_op jit(solution)/shard_map/all_gather | solution.py:280
  51.4 14.0 %copy-start.21 = (s32[16]{0:T(128)S(1)}, s32[16]{0:T(128)}, u32[]{:S(2)}) copy-start(s32[16]{0:T(128)} %param.31) | copy-start | bytes 196
  53.2 50.8 %copy-start.11 = (f32[1024]{0:T(1024)S(1)}, f32[1024]{0:T(1024)}, u32[]{:S(2)}) copy-start(f32[1024]{0:T(1024)} %param.23) | copy-start | bytes 12292
  80.8 12.6 %all-to-all-start.2 = ((bf16[8,128,128]{2,1,0:T(8,128)(2,1)}), bf16[8,128,128]{2,1,0:T(8,128)(2,1)S(1)}, u32[]{:S(2)}, u32[]{:S(2)}) async-start(bf16[8,128,128]{2,1,0:T(8,128)(2,1)} %bitcast.18), calls=%async_computation.2 | async-start | bytes 524288 | tf_op jit(solution)/shard_map/all_to_all | solution.py:303
  104.0 1.6 copy-start.2
  105.6 1.0 copy-start.3
  106.7 1.0 copy-start.4
  107.7 1.0 copy-start.5
  108.8 1.0 copy-start.6
  109.8 1.0 copy-start.7
  110.9 1.0 copy-start.8
  111.9 1.0 copy-start.9
  112.9 12.4 %copy-start.10 = (bf16[1024,128]{1,0:T(8,128)(2,1)S(1)}, bf16[1024,128]{1,0:T(8,128)(2,1)}, u32[]{:S(2)}) copy-start(bf16[1024,128]{1,0:T(8,128)(2,1)} %w_project_ref.1) | copy-start | bytes 786436
  112.9 12.4 %copy-start.12 = (f32[1024]{0:T(1024)S(1)}, f32[1024]{0:T(1024)}, u32[]{:S(2)}) copy-start(f32[1024]{0:T(1024)} %param.26) | copy-start | bytes 12292
  116.3 9.0 %all-to-all-start.3 = ((bf16[4,32,1024]{2,1,0:T(8,128)(2,1)}), bf16[4,32,1024]{2,1,0:T(8,128)(2,1)S(1)}, u32[]{:S(2)}, u32[]{:S(2)}) async-start(bf16[4,32,1024]{2,1,0:T(8,128)(2,1)} %get-tuple-element.23), calls=%async_computation.3 | async-start | bytes 524288 | tf_op jit(solution)/shard_map/all_to_all | solution.py:308
  126.5 16.6 %all-to-all-start.4 = ((bf16[32,32,128]{2,1,0:T(8,128)(2,1)}), bf16[32,32,128]{2,1,0:T(8,128)(2,1)S(1)}, u32[]{:S(2)}, u32[]{:S(2)}) async-start(bf16[32,32,128]{2,1,0:T(8,128)(2,1)} %embed.1), calls=%async_computation.4 | async-start | bytes 524288 | tf_op jit(solution)/shard_map/all_to_all | solution.py:313
  145.1 14.0 %all-to-all-start.5 = ((f32[32,16,128]{2,1,0:T(8,128)}), f32[32,16,128]{2,1,0:T(8,128)S(1)}, u32[]{:S(2)}, u32[]{:S(2)}) async-start(f32[32,16,128]{2,1,0:T(8,128)} %match.1), calls=%async_computation.5 | async-start | bytes 524288 | tf_op jit(solution)/shard_map/all_to_all | solution.py:329
Sparse Core Ops, SparseCore 0:
  10.2 38.5 all-gather.10
  53.6 64.5 all-gather.12

commit v4 on v3

--- a/solution.py
+++ b/solution.py
@@ -217,7 +217,7 @@
         + [pl.BlockSpec(memory_space=pl.ANY)] * 9,
         out_specs=(pl.BlockSpec(memory_space=pltpu.VMEM), pl.BlockSpec(memory_space=pltpu.VMEM)),
         scratch_shapes=[pltpu.VMEM(w.shape, w.dtype) for w in weights] + [pltpu.SemaphoreType.DMA((9,))],
-        compiler_params=pltpu.CompilerParams(vmem_limit_bytes=20 << 20),
+        compiler_params=pltpu.CompilerParams(vmem_limit_bytes=52 << 20),
         cost_estimate=pl.CostEstimate(flops=1000, bytes_accessed=1000, transcendentals=0),
         name="dense",
     )(place, context, tokens, gain, *weights)
@@ -264,6 +264,21 @@
 
     pages = jnp.concatenate([key_pages.reshape(128, 128), value_pages.reshape(128, 128)], axis=0)
     pages_q = spread(pages, "q", 4)
+    w_out_all = lax.all_gather(w_out, HEAD, axis=0, tiled=True)
+    doc_rows = jnp.pad(doc_lengths.astype(BF), ((0, DPAD - DT - 1), (0, 124)))
+    doc_block = jnp.concatenate([doc_vectors, doc_rows], axis=0)
+    docs = lax.all_gather(doc_block, ("q", "r"), axis=0, tiled=True)
+
+    query = jnp.dot(token_rows, w_query, preferred_element_type=F32).astype(BF) * BF(0.125)
+    own_key = jnp.dot(token_rows, w_key, preferred_element_type=F32).astype(BF)
+    own_value = jnp.dot(token_rows, w_value, preferred_element_type=F32).astype(BF)
+    ids = jnp.concatenate([candidates // 64, candidates % 64, request_group[:, None]], axis=1)
+    ids = jnp.pad(ids.astype(BF), ((0, 12), (0, 128 - 33)))
+    rows = lax.all_gather(jnp.concatenate([query, own_key, own_value, ids], axis=0), "y", axis=0, tiled=True)
+    pages_q, rows = lax.optimization_barrier((pages_q, rows))
+    prompt = spread(pages_q.reshape(1024, 128), "r", 4)
+
+    w_inner, w_outer, pages_q = lax.optimization_barrier((w_inner, w_outer, pages_q))
     inner_parts = [
         lax.all_gather(w_inner[i * 256 : (i + 1) * 256], "c", axis=0, tiled=False) for i in range(4)
     ]
@@ -271,20 +286,6 @@
         lax.all_gather(w_outer[i * 128 : (i + 1) * 128], "c", axis=0, tiled=False) for i in range(4)
     ]
 
-    pages_q, inner_parts, outer_parts = lax.optimization_barrier((pages_q, inner_parts, outer_parts))
-    prompt = spread(pages_q.reshape(1024, 128), "r", 4)
-
-    w_out_all = lax.all_gather(w_out, HEAD, axis=0, tiled=True)
-    doc_rows = jnp.pad(doc_lengths.astype(BF), ((0, DPAD - DT - 1), (0, 124)))
-    doc_block = jnp.concatenate([doc_vectors, doc_rows], axis=0)
-    docs = lax.all_gather(doc_block, ("q", "r"), axis=0, tiled=True)
-
-    query = jnp.dot(token_rows, w_query, preferred_element_type=F32).astype(BF) * BF(0.125)
-    own_key = jnp.dot(token_rows, w_key, preferred_element_type=F32).astype(BF)
-    own_value = jnp.dot(token_rows, w_value, preferred_element_type=F32).astype(BF)
-    ids = jnp.concatenate([candidates // 64, candidates % 64, request_group[:, None]], axis=1)
-    ids = jnp.pad(ids.astype(BF), ((0, 12), (0, 128 - 33)))
-    rows = lax.all_gather(jnp.concatenate([query, own_key, own_value, ids], axis=0), "y", axis=0, tiled=True)
     rows = rows.reshape(4, XROW, 128)
     got = rows[:, 3 * NROW : 3 * NROW + RQ, :33].reshape(16, 33).astype(jnp.int32)
     groups = jnp.where(got[:, 32] // 4 == my_y, got[:, 32] % 4, -1)
@@ -299,6 +300,7 @@
     position = slot[:, :, None] * 64 + jnp.arange(64, dtype=jnp.int32)
     bias = jnp.where(position < lengths[:, None, None], 0.0, -1e30).astype(F32).reshape(4, 1, 512)
 
+    rows, inner_parts, outer_parts = lax.optimization_barrier((rows, inner_parts, outer_parts))
     mixed = attend(groups, rows, prompt, bias)
     back = lax.all_to_all(mixed.reshape(8, 128, 128), ("c", "y"), 0, 0, tiled=True)
     context = jnp.sum(back.reshape(2, 4, 128, 128).astype(F32), axis=1).astype(BF)

time: 168 us -> 157 us (0.935)
  waiting for transfers between devices: 37.9 us -> 28.6 us
  local copies, waits for them, and re-layouts: 17 us -> 8.17 us
  Pallas kernels: 10.4 us -> 12.6 us
  blocking collectives: 42.1 us -> 44.2 us
  starting transfers between devices: 42 us -> 43.7 us
    all_to_all x2, waiting for transfers between devices: 11.1 us -> 1.98 us  [spread(): lax.all_to_all(wide, axes, 0, 0, tiled=True)]
    unnamed x47 -> x29, local copies, waits for them, and re-layouts: 9.76 us -> 0.87 us
    all_to_all x2, starting transfers between devices: 19.4 us -> 21.6 us  [spread(): lax.all_to_all(wide, axes, 0, 0, tiled=True)]
  transfers between devices with their start and end apart: 8 -> 8, of which waited for: 5 -> 5; matrix products, arithmetic and copies ran while one was open for 6% -> 8% of each run, Pallas kernels for 5% -> 6%
where the time goes in v4:
time: 157 us; the launch traced here: 156 us
  blocking collectives  44.2 us (28%)
  starting transfers between devices  43.7 us (28%)
  waiting for transfers between devices  28.6 us (18%)
  between operations  14.3 us (9%)
  Pallas kernels  12.6 us (8%)
  local copies, waits for them, and re-layouts  8.17 us (5%)
  other arithmetic  2.78 us (2%)
  matrix products  1.9 us (1%)
    all_to_all x2, starting transfers between devices, spread(): lax.all_to_all(wide, axes, 0, 0, tiled=True)  21.6 us
    all_gather x1, blocking collectives, per_device(): lax.all_gather(jnp.concatenate([query, own_key, own_value, ids], axis=0),...  13.1 us
    all_gather x4, blocking collectives, per_device(): lax.all_gather(w_inner[i * 256:(i + 1) * 256], 'c', axis=0, tiled=False)  11.5 us
    all_gather x1, blocking collectives, per_device(): context = lax.all_gather(context, 'x', axis=0, tiled=True)  10.3 us
    all_gather x4, blocking collectives, per_device(): lax.all_gather(w_outer[i * 128:(i + 1) * 128], 'c', axis=0, tiled=False)  9.35 us
    all_to_all x1, starting transfers between devices, per_device(): queries = lax.all_to_all(embed, HEAD + ('y',), 0, 0, tiled=True)  8.09 us
    all_to_all x1, waiting for transfers between devices, per_device(): terms = lax.all_to_all(terms, HEAD + ('y',), 0, 0, tiled=True)  8.05 us
    all_to_all x1, starting transfers between devices, per_device(): lax.all_to_all(mixed.reshape(8, 128, 128), ('c', 'y'), 0, 0, tiled=True)  6.92 us
  transfers between devices with their start and end apart: 8, of which 5 were waited for; matrix products, arithmetic and copies ran while one was open for 8% of the time, Pallas kernels for 6%

profile of v4, /device:TPU:1, one launch (start us, length us, event | category | flops | bytes accessed | tf_op | source)
XLA Modules:
  0.0 156.4 jit_solution(2328599136594578299)
XLA Ops:
  7.3 0.7 all-gather.11.cloned.1.call-update
  8.0 0.8 pad_maximum_fusion.1
  8.7 0.7 broadcast_in_dim.48
  9.5 15.6 %all-to-all-start = ((bf16[4,256,128]{2,1,0:T(8,128)(2,1)}), bf16[4,256,128]{2,1,0:T(8,128)(2,1)S(1)}, u32[]{:S(2)}, u32[]{:S(2)}) async-start(bf16[4,256,128]{2,1,0:T(8,128)(2,1)} %broadcast_in_dim.48), calls=%async_computation | async-start | bytes 524288 | tf_op jit(solution)/shard_map/all_to_all | solution.py:29
  25.1 0.7 fusion.13
  25.8 1.3 convolution_convert_fusion
  27.2 0.3 convolution_convert_fusion.1
  27.5 0.1 copy.51
  27.7 0.3 fusion
  28.0 13.1 %all_gather.60 = bf16[3136,128]{1,0:T(8,128)(2,1)S(1)} all-gather(bf16[784,128]{1,0:T(8,128)(2,1)S(1)} %pad_maximum_fusion), channel_id=1, replica_groups=mesh['x'=4,'c'=2,'y'=4,'q'=4,'r'=4] {'y'}, dimensions={0}, use_global_device_ids=true | all-gather | bytes 1003520 | tf_op jit(solution)/shard_map/all_gather | solution.py:277
  41.1 1.1 broadcast_in_dim.50
  42.2 6.0 %all-to-all-start.1 = ((bf16[4,1024,128]{2,1,0:T(8,128)(2,1)}), bf16[4,1024,128]{2,1,0:T(8,128)(2,1)S(1)}, u32[]{:S(2)}, u32[]{:S(2)}) async-start(bf16[4,1024,128]{2,1,0:T(8,128)(2,1)} %broadcast_in_dim.50), calls=%async_computation.1 | async-start | bytes 2097152 | tf_op jit(solution)/shard_map/all_to_all | solution.py:29
  48.2 0.6 fusion.2
  49.0 0.1 eq.48
  49.1 0.2 select_reduce_fusion
  49.4 0.1 add.84
  49.8 1.3 fusion.17
  51.0 4.6 %all-gather = bf16[512,512]{1,0:T(8,128)(2,1)S(1)} all-gather(bf16[256,512]{1,0:T(8,128)(2,1)S(1)} %get-tuple-element.43), channel_id=2, replica_groups=mesh['x'=4,'c'=2,'y'=4,'q'=4,'r'=4] {'c'}, dimensions={0}, use_global_device_ids=true | all-gather | bytes 786432 | tf_op jit(solution)/shard_map/all_gather | solution.py:283
  55.6 2.3 %all-gather.1 = bf16[512,512]{1,0:T(8,128)(2,1)} all-gather(bf16[256,512]{1,0:T(8,128)(2,1)S(1)} %get-tuple-element.42), channel_id=3, replica_groups=mesh['x'=4,'c'=2,'y'=4,'q'=4,'r'=4] {'c'}, dimensions={0}, use_global_device_ids=true | all-gather | bytes 786432 | tf_op jit(solution)/shard_map/all_gather | solution.py:283
  57.9 2.3 %all-gather.2 = bf16[512,512]{1,0:T(8,128)(2,1)} all-gather(bf16[256,512]{1,0:T(8,128)(2,1)S(1)} %get-tuple-element.41), channel_id=4, replica_groups=mesh['x'=4,'c'=2,'y'=4,'q'=4,'r'=4] {'c'}, dimensions={0}, use_global_device_ids=true | all-gather | bytes 786432 | tf_op jit(solution)/shard_map/all_gather | solution.py:283
  60.3 2.3 %all-gather.3 = bf16[512,512]{1,0:T(8,128)(2,1)} all-gather(bf16[256,512]{1,0:T(8,128)(2,1)S(1)} %get-tuple-element.40), channel_id=5, replica_groups=mesh['x'=4,'c'=2,'y'=4,'q'=4,'r'=4] {'c'}, dimensions={0}, use_global_device_ids=true | all-gather | bytes 786432 | tf_op jit(solution)/shard_map/all_gather | solution.py:283
  62.6 2.3 %all-gather.4 = bf16[256,1024]{1,0:T(8,128)(2,1)} all-gather(bf16[128,1024]{1,0:T(8,128)(2,1)S(1)} %get-tuple-element.39), channel_id=6, replica_groups=mesh['x'=4,'c'=2,'y'=4,'q'=4,'r'=4] {'c'}, dimensions={0}, use_global_device_ids=true | all-gather | bytes 786432 | tf_op jit(solution)/shard_map/all_gather | solution.py:286
  65.0 2.3 %all-gather.5 = bf16[256,1024]{1,0:T(8,128)(2,1)} all-gather(bf16[128,1024]{1,0:T(8,128)(2,1)S(1)} %get-tuple-element.38), channel_id=7, replica_groups=mesh['x'=4,'c'=2,'y'=4,'q'=4,'r'=4] {'c'}, dimensions={0}, use_global_device_ids=true | all-gather | bytes 786432 | tf_op jit(solution)/shard_map/all_gather | solution.py:286
  67.3 2.3 %all-gather.6 = bf16[256,1024]{1,0:T(8,128)(2,1)} all-gather(bf16[128,1024]{1,0:T(8,128)(2,1)S(1)} %get-tuple-element.37), channel_id=8, replica_groups=mesh['x'=4,'c'=2,'y'=4,'q'=4,'r'=4] {'c'}, dimensions={0}, use_global_device_ids=true | all-gather | bytes 786432 | tf_op jit(solution)/shard_map/all_gather | solution.py:286
  69.6 2.4 %all-gather.7 = bf16[256,1024]{1,0:T(8,128)(2,1)} all-gather(bf16[128,1024]{1,0:T(8,128)(2,1)S(1)} %get-tuple-element.36), channel_id=9, replica_groups=mesh['x'=4,'c'=2,'y'=4,'q'=4,'r'=4] {'c'}, dimensions={0}, use_global_device_ids=true | all-gather | bytes 786432 | tf_op jit(solution)/shard_map/all_gather | solution.py:286
  72.0 0.2 slice_reduce_fusion
  72.2 2.0 %all-to-all-done.1 = bf16[4,1024,128]{2,1,0:T(8,128)(2,1)S(1)} async-done(((bf16[4,1024,128]{2,1,0:T(8,128)(2,1)}), bf16[4,1024,128]{2,1,0:T(8,128)(2,1)S(1)}, u32[]{:S(2)}, u32[]{:S(2)}) %all-to-all-start.1) | async-done | bytes 1048608 | tf_op jit(solution)/shard_map/all_to_all | solution.py:29
  74.2 3.8 %attend.1 = bf16[2,4,128,128]{3,2,1,0:T(8,128)(2,1)} custom-call(s32[16]{0:T(128)S(1)} %compare_select_fusion.2.group_ref, bf16[4,784,128]{2,1,0:T(8,128)(2,1)S(1)} %bitcast.51, bf16[4096,128]{1,0:T(8,128)(2,1)S(1)} %bitcast.48, f32[4,1,512]{2,1,0:T(1,128)S(1)} %compare_select_fusion.bias_ref), custom_call_target="tpu_custom_call" | custom-call | flops 1000 | bytes 1000 | tf_op jit(solution)/shard_map/attend/pallas_call | solution.py:85
  78.0 6.9 %all-to-all-start.2 = ((bf16[8,128,128]{2,1,0:T(8,128)(2,1)}), bf16[8,128,128]{2,1,0:T(8,128)(2,1)S(1)}, u32[]{:S(2)}, u32[]{:S(2)}) async-start(bf16[8,128,128]{2,1,0:T(8,128)(2,1)} %bitcast.18), calls=%async_computation.2 | async-start | bytes 524288 | tf_op jit(solution)/shard_map/all_to_all | solution.py:305
  85.1 6.3 %all-to-all-done.2 = bf16[8,128,128]{2,1,0:T(8,128)(2,1)S(1)} async-done(((bf16[8,128,128]{2,1,0:T(8,128)(2,1)}), bf16[8,128,128]{2,1,0:T(8,128)(2,1)S(1)}, u32[]{:S(2)}, u32[]{:S(2)}) %all-to-all-start.2) | async-done | bytes 262176 | tf_op jit(solution)/shard_map/all_to_all | solution.py:305
  91.5 10.3 %all_gather.77.context_ref = bf16[8,128,128]{2,1,0:T(8,128)(2,1)S(1)} all-gather(bf16[2,128,128]{2,1,0:T(8,128)(2,1)S(1)} %bitcast_reduce_fusion), channel_id=1, replica_groups=mesh['x'=4,'c'=2,'y'=4,'q'=4,'r'=4] {'x'}, dimensions={0}, use_global_device_ids=true | all-gather | bytes 327680 | tf_op jit(solution)/shard_map/all_gather | solution.py:307
  101.8 4.7 %dense.1 = (bf16[128,1024]{1,0:T(8,128)(2,1)S(1)}, bf16[4,32,1024]{2,1,0:T(8,128)(2,1)}) custom-call(s32[1]{0:T(128)} %bitcast.1.place_ref, bf16[8,128,128]{2,1,0:T(8,128)(2,1)S(1)} %all_gather.77.context_ref, bf16[256,1024]{1,0:T(8,128)(2,1)S(1)} %bitcast.47, f32[1,1024]{1,0:T(1,128)S(1)} %bitcast.55, ...), custom_call_target="tpu_custom_call" | custom-call | flops 1000 | bytes 1000 | tf_op jit(solution)/shard_map/dense/pallas_call | solution.py:212
  106.5 3.4 %all-to-all-start.3 = ((bf16[4,32,1024]{2,1,0:T(8,128)(2,1)}), bf16[4,32,1024]{2,1,0:T(8,128)(2,1)S(1)}, u32[]{:S(2)}, u32[]{:S(2)}) async-start(bf16[4,32,1024]{2,1,0:T(8,128)(2,1)} %get-tuple-element.31), calls=%async_computation.3 | async-start | bytes 524288 | tf_op jit(solution)/shard_map/all_to_all | solution.py:310
  110.1 5.3 %all-to-all-done.3.terms_ref = bf16[4,32,1024]{2,1,0:T(8,128)(2,1)S(1)} async-done(((bf16[4,32,1024]{2,1,0:T(8,128)(2,1)}), bf16[4,32,1024]{2,1,0:T(8,128)(2,1)S(1)}, u32[]{:S(2)}, u32[]{:S(2)}) %all-to-all-start.3) | async-done | bytes 262176 | tf_op jit(solution)/shard_map/all_to_all | solution.py:310
  115.5 1.2 embed.1
  116.6 8.1 %all-to-all-start.4 = ((bf16[32,32,128]{2,1,0:T(8,128)(2,1)}), bf16[32,32,128]{2,1,0:T(8,128)(2,1)S(1)}, u32[]{:S(2)}, u32[]{:S(2)}) async-start(bf16[32,32,128]{2,1,0:T(8,128)(2,1)} %embed.1), calls=%async_computation.4 | async-start | bytes 524288 | tf_op jit(solution)/shard_map/all_to_all | solution.py:315
  124.7 0.1 fusion.3
  124.9 0.8 slice.61
  125.7 0.1 reshape.148
  125.8 1.3 slice.62
  127.2 0.1 copy.58
  127.3 0.1 reduce_window_sum.14.last_ref
  127.4 6.2 %all-to-all-done.4 = bf16[32,32,128]{2,1,0:T(8,128)(2,1)S(1)} async-done(((bf16[32,32,128]{2,1,0:T(8,128)(2,1)}), bf16[32,32,128]{2,1,0:T(8,128)(2,1)S(1)}, u32[]{:S(2)}, u32[]{:S(2)}) %all-to-all-start.4) | async-done | bytes 262176 | tf_op jit(solution)/shard_map/all_to_all | solution.py:315
  133.5 2.9 %match.1 = f32[32,16,128]{2,1,0:T(8,128)} custom-call(s32[64]{0:T(128)S(1)} %convert_element_type.45.need_ref, s32[64]{0:T(128)S(1)} %sub.16.first_ref, s32[64]{0:T(128)S(1)} %reduce_window_sum.14.last_ref, bf16[1024,128]{1,0:T(8,128)(2,1)S(1)} %bitcast.53, bf16[4096,128]{1,0:T(8,128)(2,1)S(1)} %bitcast.49, s32[16,128]{1,0:T(8,128)S(1)} %pad.14.pick_ref), custom_call_target="tpu_custom_call" | custom-call | flops 1000 | bytes 1000 | tf_op jit(solution)/shard_map/match/pallas_call | solution.py:151
  136.4 3.7 %all-to-all-start.5 = ((f32[32,16,128]{2,1,0:T(8,128)}), f32[32,16,128]{2,1,0:T(8,128)S(1)}, u32[]{:S(2)}, u32[]{:S(2)}) async-start(f32[32,16,128]{2,1,0:T(8,128)} %match.1), calls=%async_computation.5 | async-start | bytes 524288 | tf_op jit(solution)/shard_map/all_to_all | solution.py:331
  140.1 0.6 copy.52
  140.7 8.1 %all-to-all-done.5 = f32[32,16,128]{2,1,0:T(8,128)S(1)} async-done(((f32[32,16,128]{2,1,0:T(8,128)}), f32[32,16,128]{2,1,0:T(8,128)S(1)}, u32[]{:S(2)}, u32[]{:S(2)}) %all-to-all-start.5) | async-done | bytes 262176 | tf_op jit(solution)/shard_map/all_to_all | solution.py:331
  148.9 0.7 copy.59
  (64 shorter events, 1.5 us)
Async XLA Ops:
  7.2 18.6 %copy-start = (bf16[1024,128]{1,0:T(8,128)(2,1)S(1)}, bf16[1024,128]{1,0:T(8,128)(2,1)}, u32[]{:S(2)}) copy-start(bf16[1024,128]{1,0:T(8,128)(2,1)} %param.21) | copy-start | bytes 786436
  7.2 20.0 %copy-start.1 = (bf16[4,64,1024]{2,1,0:T(8,128)(2,1)S(1)}, bf16[4,64,1024]{2,1,0:T(8,128)(2,1)}, u32[]{:S(2)}) copy-start(bf16[4,64,1024]{2,1,0:T(8,128)(2,1)} %param.18) | copy-start | bytes 1572868
  7.2 20.0 %copy-start.6 = (bf16[1024,128]{1,0:T(8,128)(2,1)S(1)}, bf16[1024,128]{1,0:T(8,128)(2,1)}, u32[]{:S(2)}) copy-start(bf16[1024,128]{1,0:T(8,128)(2,1)} %param.20) | copy-start | bytes 786436
  7.2 20.3 %copy-start.9 = (s32[4]{0:T(128)S(1)}, s32[4]{0:T(128)}, u32[]{:S(2)}) copy-start(s32[4]{0:T(128)} %param.32) | copy-start | bytes 52
  7.2 20.5 %copy-start.7 = (bf16[1024,128]{1,0:T(8,128)(2,1)S(1)}, bf16[1024,128]{1,0:T(8,128)(2,1)}, u32[]{:S(2)}) copy-start(bf16[1024,128]{1,0:T(8,128)(2,1)} %param.19) | copy-start | bytes 786436
  7.2 94.6 %all-gather.11.cloned.1.call-start = ((), (), s32[]{:S(2)}) async-start(), calls=%async_computation.6 | async-start | bytes 2359296 | tf_op jit(solution)/shard_map/all_gather | solution.py:267
  9.5 31.6 %all-to-all-start = ((bf16[4,256,128]{2,1,0:T(8,128)(2,1)}), bf16[4,256,128]{2,1,0:T(8,128)(2,1)S(1)}, u32[]{:S(2)}, u32[]{:S(2)}) async-start(bf16[4,256,128]{2,1,0:T(8,128)(2,1)} %broadcast_in_dim.48), calls=%async_computation | async-start | bytes 524288 | tf_op jit(solution)/shard_map/all_to_all | solution.py:29
  28.0 20.2 %copy-start.10 = (s32[1,4]{1,0:T(1,128)S(1)}, s32[1,4]{1,0:T(1,128)}, u32[]{:S(2)}) copy-start(s32[1,4]{1,0:T(1,128)} %param.34) | copy-start | bytes 52
  28.0 20.2 %copy-start.8 = (bf16[256,128]{1,0:T(8,128)(2,1)S(1)}, bf16[256,128]{1,0:T(8,128)(2,1)}, u32[]{:S(2)}) copy-start(bf16[256,128]{1,0:T(8,128)(2,1)} %param.33) | copy-start | bytes 196612
  28.0 20.9 %copy-start.11 = (s32[128]{0:T(128)S(1)}, s32[128]{0:T(128)}, u32[]{:S(2)}) copy-start(s32[128]{0:T(128)} %param.30) | copy-start | bytes 1540
  41.1 8.5 %copy-start.12 = (s32[16]{0:T(128)S(1)}, s32[16]{0:T(128)}, u32[]{:S(2)}) copy-start(s32[16]{0:T(128)} %param.31) | copy-start | bytes 196
  42.2 32.0 %all-to-all-start.1 = ((bf16[4,1024,128]{2,1,0:T(8,128)(2,1)}), bf16[4,1024,128]{2,1,0:T(8,128)(2,1)S(1)}, u32[]{:S(2)}, u32[]{:S(2)}) async-start(bf16[4,1024,128]{2,1,0:T(8,128)(2,1)} %broadcast_in_dim.50), calls=%async_computation.1 | async-start | bytes 2097152 | tf_op jit(solution)/shard_map/all_to_all | solution.py:29
  48.2 76.7 %all-gather.13.cloned.1.call-start = ((), (), s32[]{:S(2)}) async-start(), calls=%async_computation.7 | async-start | bytes 1183744 | tf_op jit(solution)/shard_map/all_gather | solution.py:270
  51.0 11.6 %copy-start.5 = (bf16[512,1024]{1,0:T(8,128)(2,1)S(1)}, bf16[512,1024]{1,0:T(8,128)(2,1)}, u32[]{:S(2)}) copy-start(bf16[512,1024]{1,0:T(8,128)(2,1)} %param.25) | copy-start | bytes 3145732
  69.6 32.2 %copy-start.3 = (f32[1024]{0:T(1024)S(1)}, f32[1024]{0:T(1024)}, u32[]{:S(2)}) copy-start(f32[1024]{0:T(1024)} %param.23) | copy-start | bytes 12292
  78.0 13.5 %all-to-all-start.2 = ((bf16[8,128,128]{2,1,0:T(8,128)(2,1)}), bf16[8,128,128]{2,1,0:T(8,128)(2,1)S(1)}, u32[]{:S(2)}, u32[]{:S(2)}) async-start(bf16[8,128,128]{2,1,0:T(8,128)(2,1)} %bitcast.18), calls=%async_computation.2 | async-start | bytes 524288 | tf_op jit(solution)/shard_map/all_to_all | solution.py:305
  101.8 13.7 %copy-start.2 = (bf16[1024,128]{1,0:T(8,128)(2,1)S(1)}, bf16[1024,128]{1,0:T(8,128)(2,1)}, u32[]{:S(2)}) copy-start(bf16[1024,128]{1,0:T(8,128)(2,1)} %w_project_ref.1) | copy-start | bytes 786436
  101.8 13.7 %copy-start.4 = (f32[1024]{0:T(1024)S(1)}, f32[1024]{0:T(1024)}, u32[]{:S(2)}) copy-start(f32[1024]{0:T(1024)} %param.26) | copy-start | bytes 12292
  106.5 8.9 %all-to-all-start.3 = ((bf16[4,32,1024]{2,1,0:T(8,128)(2,1)}), bf16[4,32,1024]{2,1,0:T(8,128)(2,1)S(1)}, u32[]{:S(2)}, u32[]{:S(2)}) async-start(bf16[4,32,1024]{2,1,0:T(8,128)(2,1)} %get-tuple-element.31), calls=%async_computation.3 | async-start | bytes 524288 | tf_op jit(solution)/shard_map/all_to_all | solution.py:310
  116.6 16.9 %all-to-all-start.4 = ((bf16[32,32,128]{2,1,0:T(8,128)(2,1)}), bf16[32,32,128]{2,1,0:T(8,128)(2,1)S(1)}, u32[]{:S(2)}, u32[]{:S(2)}) async-start(bf16[32,32,128]{2,1,0:T(8,128)(2,1)} %embed.1), calls=%async_computation.4 | async-start | bytes 524288 | tf_op jit(solution)/shard_map/all_to_all | solution.py:315
  136.4 12.4 %all-to-all-start.5 = ((f32[32,16,128]{2,1,0:T(8,128)}), f32[32,16,128]{2,1,0:T(8,128)S(1)}, u32[]{:S(2)}, u32[]{:S(2)}) async-start(f32[32,16,128]{2,1,0:T(8,128)} %match.1), calls=%async_computation.5 | async-start | bytes 524288 | tf_op jit(solution)/shard_map/all_to_all | solution.py:331
Sparse Core Ops, SparseCore 0:
  10.2 38.5 all-gather.10
  51.1 63.3 all-gather.12

commit v5 on v3

--- a/solution.py
+++ b/solution.py
@@ -33,52 +33,55 @@
     return lax.dot_general(a, b, (((1,), (1,)), ((), ())), preferred_element_type=F32)
 
 
-def attend_kernel(group_ref, rows_ref, prompt_ref, bias_ref, out_ref):
+def attend_kernel(group_ref, rows_ref, prompt_ref, bias_ref, out_ref, order_ref):
     low_half = lax.broadcasted_iota(jnp.int32, (QL, 128), 1) < 64
-
-    def one_request(i, carry):
+    out_ref[...] = jnp.zeros_like(out_ref)
+    count = jnp.int32(0)
+    for i in range(16):
+        order_ref[count] = jnp.int32(i)
+        count = count + (group_ref[i] >= 0).astype(jnp.int32)
+
+    def one_request(i):
         src = i // RQ
         row = pl.multiple_of((i % RQ) * QL, QL)
-        half = (i % RQ) // 2
-        place = pl.multiple_of((i % 2) * QL, QL)
         group = group_ref[i]
-
-        @pl.when(group >= 0)
-        def _():
-            query = rows_ref[src, pl.ds(row, QL), :]
-            zero = jnp.zeros_like(query)
-            both = jnp.concatenate(
-                [jnp.where(low_half, query, zero), jnp.where(low_half, zero, query)], axis=0
-            )
-            own_key = rows_ref[src, pl.ds(pl.multiple_of(NROW + row, QL), QL), :]
-            own_value = rows_ref[src, pl.ds(pl.multiple_of(2 * NROW + row, QL), QL), :]
-            parts = [nt_dot(both, own_key)]
-            values = [own_value]
-            for piece in range(4):
-                start = pl.multiple_of(piece * 1024 + group * 256, 256)
-                key = prompt_ref[pl.ds(start, 128), :]
-                values.append(prompt_ref[pl.ds(pl.multiple_of(start + 128, 128), 128), :])
-                bias = bias_ref[group, :, piece * 128 : (piece + 1) * 128]
-                parts.append(nt_dot(both, key) + bias)
-            top = jnp.max(parts[0], axis=-1, keepdims=True)
-            for part in parts[1:]:
-                top = jnp.maximum(top, jnp.max(part, axis=-1, keepdims=True))
-            total = jnp.zeros_like(top)
-            mixed = jnp.zeros((2 * QL, 128), F32)
-            for part, value in zip(parts, values):
-                weight = jnp.exp(part - top)
-                total = total + jnp.sum(weight, axis=-1, keepdims=True)
-                mixed = mixed + jnp.dot(weight.astype(BF), value, preferred_element_type=F32)
-            mixed = mixed / total
-            out_ref[half, src, pl.ds(place, QL), :] = jnp.where(low_half, mixed[:QL], mixed[QL:]).astype(BF)
-
-        @pl.when(group < 0)
-        def _():
-            out_ref[half, src, pl.ds(place, QL), :] = jnp.zeros((QL, 128), BF)
-
+        query = rows_ref[src, pl.ds(row, QL), :]
+        zero = jnp.zeros_like(query)
+        both = jnp.concatenate(
+            [jnp.where(low_half, query, zero), jnp.where(low_half, zero, query)], axis=0
+        )
+        own_key = rows_ref[src, pl.ds(pl.multiple_of(NROW + row, QL), QL), :]
+        own_value = rows_ref[src, pl.ds(pl.multiple_of(2 * NROW + row, QL), QL), :]
+        parts = [nt_dot(both, own_key)]
+        values = [own_value]
+        for piece in range(4):
+            start = pl.multiple_of(piece * 1024 + group * 256, 256)
+            key = prompt_ref[pl.ds(start, 128), :]
+            values.append(prompt_ref[pl.ds(pl.multiple_of(start + 128, 128), 128), :])
+            bias = bias_ref[group, :, piece * 128 : (piece + 1) * 128]
+            parts.append(nt_dot(both, key) + bias)
+        top = jnp.max(parts[0], axis=-1, keepdims=True)
+        wide = jnp.maximum(jnp.maximum(parts[1], parts[2]), jnp.maximum(parts[3], parts[4]))
+        top = jnp.maximum(top, jnp.max(wide, axis=-1, keepdims=True))
+        weights = [jnp.exp(part - top) for part in parts]
+        wide = (weights[1] + weights[2]) + (weights[3] + weights[4])
+        total = jnp.sum(weights[0], axis=-1, keepdims=True) + jnp.sum(wide, axis=-1, keepdims=True)
+        mixed = jnp.zeros((2 * QL, 128), F32)
+        for weight, value in zip(weights, values):
+            mixed = mixed + jnp.dot(weight.astype(BF), value, preferred_element_type=F32)
+        mixed = mixed / total
+        return jnp.where(low_half, mixed[:QL], mixed[QL:]).astype(BF)
+
+    def two_requests(step, carry):
+        i = order_ref[2 * step]
+        k = order_ref[jnp.where(2 * step + 1 < count, 2 * step + 1, 2 * step)]
+        results = [one_request(i), one_request(k)]
+        for j, result in zip((i, k), results):
+            place = pl.multiple_of((j % 2) * QL, QL)
+            out_ref[(j % RQ) // 2, j // RQ, pl.ds(place, QL), :] = result
         return carry
 
-    lax.fori_loop(0, 16, one_request, 0)
+    lax.fori_loop(0, (count + 1) // 2, two_requests, 0)
 
 
 def attend(groups, rows, prompt, bias):
@@ -92,6 +95,7 @@
             pl.BlockSpec(memory_space=pltpu.VMEM),
         ],
         out_specs=pl.BlockSpec(memory_space=pltpu.VMEM),
+        scratch_shapes=[pltpu.SMEM((17,), jnp.int32)],
         compiler_params=pltpu.CompilerParams(vmem_limit_bytes=16 << 20),
         cost_estimate=pl.CostEstimate(flops=1000, bytes_accessed=1000, transcendentals=0),
         name="attend",
@@ -174,6 +178,44 @@
         )(*args)
 
     return call
+
+
+def pages_kernel(key_ref, value_ref, out_ref, sems):
+    copies = []
+    for i in range(4):
+        for j, ref in enumerate((key_ref, value_ref)):
+            target = out_ref.at[i, pl.ds(j * 128, 128), :]
+            copies.append(pltpu.make_async_copy(ref, target, sems.at[2 * i + j]))
+    for copy in copies:
+        copy.start()
+    for copy in copies:
+        copy.wait()
+
+
+def repeat_pages(keys, values):
+    return pl.pallas_call(
+        pages_kernel,
+        out_shape=jax.ShapeDtypeStruct((4, 256, 128), BF),
+        in_specs=[pl.BlockSpec(memory_space=pl.ANY)] * 2,
+        out_specs=pl.BlockSpec(memory_space=pl.ANY),
+        scratch_shapes=[pltpu.SemaphoreType.DMA((8,))],
+        compiler_params=pltpu.CompilerParams(vmem_limit_bytes=52 << 20),
+        cost_estimate=pl.CostEstimate(flops=1000, bytes_accessed=1000, transcendentals=0),
+        name="pages",
+    )(keys, values)
+
+
+def total_kernel(place_ref, terms_ref, out_ref):
+    total = terms_ref[0]
+    for i in range(1, 32):
+        total = total + terms_ref[i]
+    lane = lax.broadcasted_iota(jnp.int32, (8, 128), 1)
+    row = lax.broadcasted_iota(jnp.int32, (8, 128), 0)
+    wanted = (lane == place_ref[0] * RQ + row).astype(F32)
+    picked = lax.dot_general(
+        wanted, total, (((1,), (1,)), ((), ())), preferred_element_type=F32, precision=lax.Precision.HIGHEST
+    )
+    out_ref[...] = picked[:RQ]
 
 
 def dense_kernel(place_ref, context_ref, token_ref, gain_ref, *refs):
@@ -217,7 +259,7 @@
         + [pl.BlockSpec(memory_space=pl.ANY)] * 9,
         out_specs=(pl.BlockSpec(memory_space=pltpu.VMEM), pl.BlockSpec(memory_space=pltpu.VMEM)),
         scratch_shapes=[pltpu.VMEM(w.shape, w.dtype) for w in weights] + [pltpu.SemaphoreType.DMA((9,))],
-        compiler_params=pltpu.CompilerParams(vmem_limit_bytes=20 << 20),
+        compiler_params=pltpu.CompilerParams(vmem_limit_bytes=52 << 20),
         cost_estimate=pl.CostEstimate(flops=1000, bytes_accessed=1000, transcendentals=0),
         name="dense",
     )(place, context, tokens, gain, *weights)
@@ -262,17 +304,18 @@
     my_x = lax.axis_index("x").reshape(1)
     token_rows = tokens.reshape(NROW, 1024)
 
-    pages = jnp.concatenate([key_pages.reshape(128, 128), value_pages.reshape(128, 128)], axis=0)
-    pages_q = spread(pages, "q", 4)
-    inner_parts = [
-        lax.all_gather(w_inner[i * 256 : (i + 1) * 256], "c", axis=0, tiled=False) for i in range(4)
-    ]
-    outer_parts = [
-        lax.all_gather(w_outer[i * 128 : (i + 1) * 128], "c", axis=0, tiled=False) for i in range(4)
-    ]
-
-    pages_q, inner_parts, outer_parts = lax.optimization_barrier((pages_q, inner_parts, outer_parts))
+    pages = repeat_pages(key_pages.reshape(128, 128), value_pages.reshape(128, 128))
+    pages_q = lax.all_to_all(pages, "q", 0, 0, tiled=True)
+
+    def both_cores(block, size, parts):
+        return [
+            lax.all_gather(block[i * size : (i + 1) * size], "c", axis=0, tiled=False) for i in parts
+        ]
+
+    inner_parts = both_cores(w_inner, 256, range(4))
+    pages_q, inner_parts, w_outer = lax.optimization_barrier((pages_q, inner_parts, w_outer))
     prompt = spread(pages_q.reshape(1024, 128), "r", 4)
+    outer_parts = both_cores(w_outer, 128, range(2))
 
     w_out_all = lax.all_gather(w_out, HEAD, axis=0, tiled=True)
     doc_rows = jnp.pad(doc_lengths.astype(BF), ((0, DPAD - DT - 1), (0, 124)))
@@ -284,7 +327,9 @@
     own_value = jnp.dot(token_rows, w_value, preferred_element_type=F32).astype(BF)
     ids = jnp.concatenate([candidates // 64, candidates % 64, request_group[:, None]], axis=1)
     ids = jnp.pad(ids.astype(BF), ((0, 12), (0, 128 - 33)))
-    rows = lax.all_gather(jnp.concatenate([query, own_key, own_value, ids], axis=0), "y", axis=0, tiled=True)
+    rows = jnp.concatenate([query, own_key, own_value, ids], axis=0)
+    rows, pages_q = lax.optimization_barrier((rows, pages_q))
+    rows = lax.all_gather(rows, "y", axis=0, tiled=True)
     rows = rows.reshape(4, XROW, 128)
     got = rows[:, 3 * NROW : 3 * NROW + RQ, :33].reshape(16, 33).astype(jnp.int32)
     groups = jnp.where(got[:, 32] // 4 == my_y, got[:, 32] % 4, -1)
@@ -299,7 +344,10 @@
     position = slot[:, :, None] * 64 + jnp.arange(64, dtype=jnp.int32)
     bias = jnp.where(position < lengths[:, None, None], 0.0, -1e30).astype(F32).reshape(4, 1, 512)
 
+    rows, outer_parts = lax.optimization_barrier((rows, outer_parts))
     mixed = attend(groups, rows, prompt, bias)
+    w_outer, mixed = lax.optimization_barrier((w_outer, mixed))
+    outer_parts = outer_parts + both_cores(w_outer, 128, range(2, 4))
     back = lax.all_to_all(mixed.reshape(8, 128, 128), ("c", "y"), 0, 0, tiled=True)
     context = jnp.sum(back.reshape(2, 4, 128, 128).astype(F32), axis=1).astype(BF)
     context = lax.all_gather(context, "x", axis=0, tiled=True)
@@ -327,8 +375,7 @@
         need, doc_first.reshape(64), doc_last.reshape(64), queries.reshape(1024, 128), docs, pick_lanes
     )
     terms = lax.all_to_all(terms, HEAD + ("y",), 0, 0, tiled=True)
-    total = jnp.sum(terms, axis=0)
-    scores = lax.dynamic_slice(total, (0, my_y * RQ), (NC, RQ)).T
+    scores = vmem_call(total_kernel, jax.ShapeDtypeStruct((RQ, NC), F32), "total", 1)(my_y.reshape(1), terms)
     return (embedded, scores)
 
 

time: 168 us -> 159 us (0.946)
  waiting for transfers between devices: 37.9 us -> 23.5 us
  local copies, waits for them, and re-layouts: 17 us -> 10.9 us
  blocking collectives: 42.1 us -> 46.9 us
  starting transfers between devices: 42 us -> 46.1 us
  Pallas kernels: 10.4 us -> 12.4 us
    all_to_all x0 -> x1, starting transfers between devices: none -> 15.6 us  [per_device(): pages_q = lax.all_to_all(pages, 'q', 0, 0, tiled=True)]
    all_to_all x2 -> x1, starting transfers between devices: 19.4 us -> 7.69 us  [spread(): lax.all_to_all(wide, axes, 0, 0, tiled=True)]
    all_to_all x2 -> x1, waiting for transfers between devices: 11.1 us -> 1.84 us  [spread(): lax.all_to_all(wide, axes, 0, 0, tiled=True)]
    unnamed x47 -> x26, local copies, waits for them, and re-layouts: 9.76 us -> 1.69 us
    all_to_all x1, waiting for transfers between devices: 6.35 us -> 1.28 us  [per_device(): lax.all_to_all(mixed.reshape(8, 128, 128), ('c', 'y'), 0, 0, tiled=True)]
    all_gather x9, blocking collectives: 31.5 us -> 36.4 us  [the longest x8 24.7 us: both_cores(): lax.all_gather(block[i * size:(i + 1) * size], 'c', axis=0, tiled=False)]
    slice x2 -> x3, local copies, waits for them, and re-layouts: 1.32 us -> 3.41 us  [both_cores(): block[i * size:(i + 1) * size]]
  transfers between devices with their start and end apart: 8 -> 8, of which waited for: 5 -> 5; matrix products, arithmetic and copies ran while one was open for 6% -> 8% of each run, Pallas kernels for 5% -> 6%
where the time goes in v5:
time: 159 us; the launch traced here: 158 us
  blocking collectives  46.9 us (29%)
  starting transfers between devices  46.1 us (29%)
  waiting for transfers between devices  23.5 us (15%)
  between operations  14.3 us (9%)
  Pallas kernels  12.4 us (8%)
  local copies, waits for them, and re-layouts  10.9 us (7%)
  other arithmetic  2.76 us (2%)
    all_gather x8, blocking collectives, both_cores(): lax.all_gather(block[i * size:(i + 1) * size], 'c', axis=0, tiled=False)  24.7 us
    all_to_all x1, starting transfers between devices, per_device(): pages_q = lax.all_to_all(pages, 'q', 0, 0, tiled=True)  15.6 us
    all_gather x1, blocking collectives, per_device(): rows = lax.all_gather(rows, 'y', axis=0, tiled=True)  11.7 us
    all_gather x1, blocking collectives, per_device(): context = lax.all_gather(context, 'x', axis=0, tiled=True)  10.5 us
    all_to_all x1, waiting for transfers between devices, per_device(): terms = lax.all_to_all(terms, HEAD + ('y',), 0, 0, tiled=True)  8.15 us
    all_to_all x1, starting transfers between devices, per_device(): queries = lax.all_to_all(embed, HEAD + ('y',), 0, 0, tiled=True)  7.86 us
    all_to_all x1, starting transfers between devices, spread(): lax.all_to_all(wide, axes, 0, 0, tiled=True)  7.69 us
    all_to_all x1, waiting for transfers between devices, per_device(): queries = lax.all_to_all(embed, HEAD + ('y',), 0, 0, tiled=True)  6.15 us
  transfers between devices with their start and end apart: 8, of which 5 were waited for; matrix products, arithmetic and copies ran while one was open for 8% of the time, Pallas kernels for 6%

profile of v5, /device:TPU:1, one launch (start us, length us, event | category | flops | bytes accessed | tf_op | source)
XLA Modules:
  0.0 157.8 jit_solution(16549097657502884347)
XLA Ops:
  7.2 0.7 all-gather.11.cloned.1.call-update
  7.9 0.7 copy-done.3
  8.7 0.8 copy-done.4
  9.4 0.8 pages.1
  10.2 15.6 %all-to-all-start = ((bf16[4,256,128]{2,1,0:T(8,128)(2,1)}), bf16[4,256,128]{2,1,0:T(8,128)(2,1)S(1)}, u32[]{:S(2)}, u32[]{:S(2)}) async-start(bf16[4,256,128]{2,1,0:T(8,128)(2,1)} %pages.1), calls=%async_computation | async-start | bytes 524288 | tf_op jit(solution)/shard_map/all_to_all | solution.py:308
  25.8 0.7 convert_element_type.46
  26.5 1.5 fusion.2
  28.0 0.7 dynamic_slice.9
  28.8 0.2 select_reduce_fusion
  29.1 1.3 fusion.18
  30.3 2.8 %all-gather = bf16[512,512]{1,0:T(8,128)(2,1)S(1)} all-gather(bf16[256,512]{1,0:T(8,128)(2,1)S(1)} %get-tuple-element.36), channel_id=2, replica_groups=mesh['x'=4,'c'=2,'y'=4,'q'=4,'r'=4] {'c'}, dimensions={0}, use_global_device_ids=true | all-gather | bytes 786432 | tf_op jit(solution)/shard_map/all_gather | solution.py:312
  33.1 2.3 %all-gather.1 = bf16[512,512]{1,0:T(8,128)(2,1)} all-gather(bf16[256,512]{1,0:T(8,128)(2,1)S(1)} %get-tuple-element.35), channel_id=3, replica_groups=mesh['x'=4,'c'=2,'y'=4,'q'=4,'r'=4] {'c'}, dimensions={0}, use_global_device_ids=true | all-gather | bytes 786432 | tf_op jit(solution)/shard_map/all_gather | solution.py:312
  35.4 2.3 %all-gather.2 = bf16[512,512]{1,0:T(8,128)(2,1)} all-gather(bf16[256,512]{1,0:T(8,128)(2,1)S(1)} %get-tuple-element.37), channel_id=4, replica_groups=mesh['x'=4,'c'=2,'y'=4,'q'=4,'r'=4] {'c'}, dimensions={0}, use_global_device_ids=true | all-gather | bytes 786432 | tf_op jit(solution)/shard_map/all_gather | solution.py:312
  37.7 2.5 %all-gather.3 = bf16[512,512]{1,0:T(8,128)(2,1)} all-gather(bf16[256,512]{1,0:T(8,128)(2,1)S(1)} %get-tuple-element.34), channel_id=5, replica_groups=mesh['x'=4,'c'=2,'y'=4,'q'=4,'r'=4] {'c'}, dimensions={0}, use_global_device_ids=true | all-gather | bytes 786432 | tf_op jit(solution)/shard_map/all_gather | solution.py:312
  40.3 1.1 broadcast_in_dim.45
  41.4 7.7 %all-to-all-start.1 = ((bf16[4,1024,128]{2,1,0:T(8,128)(2,1)}), bf16[4,1024,128]{2,1,0:T(8,128)(2,1)S(1)}, u32[]{:S(2)}, u32[]{:S(2)}) async-start(bf16[4,1024,128]{2,1,0:T(8,128)(2,1)} %broadcast_in_dim.45), calls=%async_computation.1 | async-start | bytes 2097152 | tf_op jit(solution)/shard_map/all_to_all | solution.py:29
  49.3 0.1 copy.50
  49.6 0.3 convolution_convert_fusion
  49.9 0.3 convolution_convert_fusion.1
  50.2 0.3 fusion
  50.6 11.7 %all_gather.68 = bf16[3136,128]{1,0:T(8,128)(2,1)S(1)} all-gather(bf16[784,128]{1,0:T(8,128)(2,1)S(1)} %pad_maximum_fusion), channel_id=1, replica_groups=mesh['x'=4,'c'=2,'y'=4,'q'=4,'r'=4] {'y'}, dimensions={0}, use_global_device_ids=true | all-gather | bytes 1003520 | tf_op jit(solution)/shard_map/all_gather | solution.py:332
  62.3 1.1 fusion.17
  63.4 7.8 %all-gather.4 = bf16[256,1024]{1,0:T(8,128)(2,1)} all-gather(bf16[128,1024]{1,0:T(8,128)(2,1)S(1)} %get-tuple-element.33), channel_id=6, replica_groups=mesh['x'=4,'c'=2,'y'=4,'q'=4,'r'=4] {'c'}, dimensions={0}, use_global_device_ids=true | all-gather | bytes 786432 | tf_op jit(solution)/shard_map/all_gather | solution.py:312
  71.2 2.3 %all-gather.5 = bf16[256,1024]{1,0:T(8,128)(2,1)} all-gather(bf16[128,1024]{1,0:T(8,128)(2,1)S(1)} %get-tuple-element.32), channel_id=7, replica_groups=mesh['x'=4,'c'=2,'y'=4,'q'=4,'r'=4] {'c'}, dimensions={0}, use_global_device_ids=true | all-gather | bytes 786432 | tf_op jit(solution)/shard_map/all_gather | solution.py:312
  73.7 0.2 slice_reduce_fusion
  73.9 1.8 %all-to-all-done.1 = bf16[4,1024,128]{2,1,0:T(8,128)(2,1)S(1)} async-done(((bf16[4,1024,128]{2,1,0:T(8,128)(2,1)}), bf16[4,1024,128]{2,1,0:T(8,128)(2,1)S(1)}, u32[]{:S(2)}, u32[]{:S(2)}) %all-to-all-start.1) | async-done | bytes 1048608 | tf_op jit(solution)/shard_map/all_to_all | solution.py:29
  75.8 3.1 %attend.1 = bf16[2,4,128,128]{3,2,1,0:T(8,128)(2,1)} custom-call(s32[16]{0:T(128)S(1)} %compare_select_fusion.2.group_ref, bf16[4,784,128]{2,1,0:T(8,128)(2,1)S(1)} %bitcast.50, bf16[4096,128]{1,0:T(8,128)(2,1)S(1)} %bitcast.47, f32[4,1,512]{2,1,0:T(1,128)S(1)} %compare_select_fusion.bias_ref), custom_call_target="tpu_custom_call" | custom-call | flops 1000 | bytes 1000 | tf_op jit(solution)/shard_map/attend/pallas_call | solution.py:88
  78.9 6.1 %all-to-all-start.2 = ((bf16[8,128,128]{2,1,0:T(8,128)(2,1)}), bf16[8,128,128]{2,1,0:T(8,128)(2,1)S(1)}, u32[]{:S(2)}, u32[]{:S(2)}) async-start(bf16[8,128,128]{2,1,0:T(8,128)(2,1)} %bitcast.16), calls=%async_computation.2 | async-start | bytes 524288 | tf_op jit(solution)/shard_map/all_to_all | solution.py:351
  85.0 1.1 fusion.16
  86.0 2.3 %all-gather.6 = bf16[256,1024]{1,0:T(8,128)(2,1)} all-gather(bf16[128,1024]{1,0:T(8,128)(2,1)S(1)} %get-tuple-element.31), channel_id=8, replica_groups=mesh['x'=4,'c'=2,'y'=4,'q'=4,'r'=4] {'c'}, dimensions={0}, use_global_device_ids=true | all-gather | bytes 786432 | tf_op jit(solution)/shard_map/all_gather | solution.py:312
  88.4 2.3 %all-gather.7 = bf16[256,1024]{1,0:T(8,128)(2,1)} all-gather(bf16[128,1024]{1,0:T(8,128)(2,1)S(1)} %get-tuple-element.30), channel_id=9, replica_groups=mesh['x'=4,'c'=2,'y'=4,'q'=4,'r'=4] {'c'}, dimensions={0}, use_global_device_ids=true | all-gather | bytes 786432 | tf_op jit(solution)/shard_map/all_gather | solution.py:312
  90.7 1.3 all-to-all-done.2
  92.0 10.5 %all_gather.73.context_ref = bf16[8,128,128]{2,1,0:T(8,128)(2,1)S(1)} all-gather(bf16[2,128,128]{2,1,0:T(8,128)(2,1)S(1)} %bitcast_reduce_fusion), channel_id=1, replica_groups=mesh['x'=4,'c'=2,'y'=4,'q'=4,'r'=4] {'x'}, dimensions={0}, use_global_device_ids=true | all-gather | bytes 327680 | tf_op jit(solution)/shard_map/all_gather | solution.py:353
  102.5 4.7 %dense.1 = (bf16[128,1024]{1,0:T(8,128)(2,1)S(1)}, bf16[4,32,1024]{2,1,0:T(8,128)(2,1)}) custom-call(s32[1]{0:T(128)} %bitcast.1.place_ref, bf16[8,128,128]{2,1,0:T(8,128)(2,1)S(1)} %all_gather.73.context_ref, bf16[256,1024]{1,0:T(8,128)(2,1)S(1)} %bitcast.46, f32[1,1024]{1,0:T(1,128)S(1)} %bitcast.56, ...), custom_call_target="tpu_custom_call" | custom-call | flops 1000 | bytes 1000 | tf_op jit(solution)/shard_map/dense/pallas_call | solution.py:254
  107.2 3.5 %all-to-all-start.3 = ((bf16[4,32,1024]{2,1,0:T(8,128)(2,1)}), bf16[4,32,1024]{2,1,0:T(8,128)(2,1)S(1)}, u32[]{:S(2)}, u32[]{:S(2)}) async-start(bf16[4,32,1024]{2,1,0:T(8,128)(2,1)} %get-tuple-element.29), calls=%async_computation.3 | async-start | bytes 524288 | tf_op jit(solution)/shard_map/all_to_all | solution.py:356
  110.9 5.4 %all-to-all-done.3.terms_ref = bf16[4,32,1024]{2,1,0:T(8,128)(2,1)S(1)} async-done(((bf16[4,32,1024]{2,1,0:T(8,128)(2,1)}), bf16[4,32,1024]{2,1,0:T(8,128)(2,1)S(1)}, u32[]{:S(2)}, u32[]{:S(2)}) %all-to-all-start.3) | async-done | bytes 262176 | tf_op jit(solution)/shard_map/all_to_all | solution.py:356
  116.3 1.1 embed.1
  117.4 7.9 %all-to-all-start.4 = ((bf16[32,32,128]{2,1,0:T(8,128)(2,1)}), bf16[32,32,128]{2,1,0:T(8,128)(2,1)S(1)}, u32[]{:S(2)}, u32[]{:S(2)}) async-start(bf16[32,32,128]{2,1,0:T(8,128)(2,1)} %embed.1), calls=%async_computation.4 | async-start | bytes 524288 | tf_op jit(solution)/shard_map/all_to_all | solution.py:361
  125.3 0.1 fusion.3
  125.4 0.8 slice.61
  126.4 1.3 slice.62
  127.8 0.1 reduce_window_sum.14.last_ref
  127.9 6.2 %all-to-all-done.4 = bf16[32,32,128]{2,1,0:T(8,128)(2,1)S(1)} async-done(((bf16[32,32,128]{2,1,0:T(8,128)(2,1)}), bf16[32,32,128]{2,1,0:T(8,128)(2,1)S(1)}, u32[]{:S(2)}, u32[]{:S(2)}) %all-to-all-start.4) | async-done | bytes 262176 | tf_op jit(solution)/shard_map/all_to_all | solution.py:361
  134.1 2.0 %match.1 = f32[32,16,128]{2,1,0:T(8,128)} custom-call(s32[64]{0:T(128)S(1)} %convert_element_type.45.need_ref, s32[64]{0:T(128)S(1)} %sub.16.first_ref, s32[64]{0:T(128)S(1)} %reduce_window_sum.14.last_ref, bf16[1024,128]{1,0:T(8,128)(2,1)S(1)} %bitcast.52, bf16[4096,128]{1,0:T(8,128)(2,1)S(1)} %bitcast.48, s32[16,128]{1,0:T(8,128)S(1)} %pad.14.pick_ref), custom_call_target="tpu_custom_call" | custom-call | flops 1000 | bytes 1000 | tf_op jit(solution)/shard_map/match/pallas_call | solution.py:155
  136.1 5.3 %all-to-all-start.5 = ((f32[32,16,128]{2,1,0:T(8,128)}), f32[32,16,128]{2,1,0:T(8,128)S(1)}, u32[]{:S(2)}, u32[]{:S(2)}) async-start(f32[32,16,128]{2,1,0:T(8,128)} %match.1), calls=%async_computation.5 | async-start | bytes 524288 | tf_op jit(solution)/shard_map/all_to_all | solution.py:377
  141.4 0.6 copy.51
  142.1 8.1 %all-to-all-done.5.terms_ref = f32[32,16,128]{2,1,0:T(8,128)S(1)} async-done(((f32[32,16,128]{2,1,0:T(8,128)}), f32[32,16,128]{2,1,0:T(8,128)S(1)}, u32[]{:S(2)}, u32[]{:S(2)}) %all-to-all-start.5) | async-done | bytes 262176 | tf_op jit(solution)/shard_map/all_to_all | solution.py:377
  150.2 0.7 total.1
  (60 shorter events, 1.5 us)
Async XLA Ops:
  7.2 42.4 %copy-start = (bf16[1024,128]{1,0:T(8,128)(2,1)S(1)}, bf16[1024,128]{1,0:T(8,128)(2,1)}, u32[]{:S(2)}) copy-start(bf16[1024,128]{1,0:T(8,128)(2,1)} %param.21) | copy-start | bytes 786436
  7.2 95.3 %all-gather.11.cloned.1.call-start = ((), (), s32[]{:S(2)}) async-start(), calls=%async_computation.6 | async-start | bytes 2359296 | tf_op jit(solution)/shard_map/all_gather | solution.py:320
  7.9 0.8 copy-start.3
  8.7 0.8 copy-start.4
  10.2 30.1 %all-to-all-start = ((bf16[4,256,128]{2,1,0:T(8,128)(2,1)}), bf16[4,256,128]{2,1,0:T(8,128)(2,1)S(1)}, u32[]{:S(2)}, u32[]{:S(2)}) async-start(bf16[4,256,128]{2,1,0:T(8,128)(2,1)} %pages.1), calls=%async_computation | async-start | bytes 524288 | tf_op jit(solution)/shard_map/all_to_all | solution.py:308
  25.8 99.6 %all-gather.13.cloned.1.call-start = ((), (), s32[]{:S(2)}) async-start(), calls=%async_computation.7 | async-start | bytes 1183744 | tf_op jit(solution)/shard_map/all_gather | solution.py:323
  37.7 11.6 %copy-start.10 = (s32[4]{0:T(128)S(1)}, s32[4]{0:T(128)}, u32[]{:S(2)}) copy-start(s32[4]{0:T(128)} %param.32) | copy-start | bytes 52
  37.7 11.7 %copy-start.11 = (s32[16]{0:T(128)S(1)}, s32[16]{0:T(128)}, u32[]{:S(2)}) copy-start(s32[16]{0:T(128)} %param.31) | copy-start | bytes 196
  37.7 11.8 %copy-start.9 = (s32[4,16]{1,0:T(4,128)S(1)}, s32[4,16]{1,0:T(4,128)}, u32[]{:S(2)}) copy-start(s32[4,16]{1,0:T(4,128)} %param.35) | copy-start | bytes 772
  37.7 11.9 %copy-start.1 = (bf16[4,64,1024]{2,1,0:T(8,128)(2,1)S(1)}, bf16[4,64,1024]{2,1,0:T(8,128)(2,1)}, u32[]{:S(2)}) copy-start(bf16[4,64,1024]{2,1,0:T(8,128)(2,1)} %param.18) | copy-start | bytes 1572868
  40.3 9.6 %copy-start.7 = (bf16[1024,128]{1,0:T(8,128)(2,1)S(1)}, bf16[1024,128]{1,0:T(8,128)(2,1)}, u32[]{:S(2)}) copy-start(bf16[1024,128]{1,0:T(8,128)(2,1)} %param.20) | copy-start | bytes 786436
  41.4 8.8 %copy-start.8 = (bf16[1024,128]{1,0:T(8,128)(2,1)S(1)}, bf16[1024,128]{1,0:T(8,128)(2,1)}, u32[]{:S(2)}) copy-start(bf16[1024,128]{1,0:T(8,128)(2,1)} %param.19) | copy-start | bytes 786436
  41.4 34.4 %all-to-all-start.1 = ((bf16[4,1024,128]{2,1,0:T(8,128)(2,1)}), bf16[4,1024,128]{2,1,0:T(8,128)(2,1)S(1)}, u32[]{:S(2)}, u32[]{:S(2)}) async-start(bf16[4,1024,128]{2,1,0:T(8,128)(2,1)} %broadcast_in_dim.45), calls=%async_computation.1 | async-start | bytes 2097152 | tf_op jit(solution)/shard_map/all_to_all | solution.py:29
  78.9 23.6 %copy-start.5 = (f32[1024]{0:T(1024)S(1)}, f32[1024]{0:T(1024)}, u32[]{:S(2)}) copy-start(f32[1024]{0:T(1024)} %param.23) | copy-start | bytes 12292
  78.9 13.1 %all-to-all-start.2 = ((bf16[8,128,128]{2,1,0:T(8,128)(2,1)}), bf16[8,128,128]{2,1,0:T(8,128)(2,1)S(1)}, u32[]{:S(2)}, u32[]{:S(2)}) async-start(bf16[8,128,128]{2,1,0:T(8,128)(2,1)} %bitcast.16), calls=%async_computation.2 | async-start | bytes 524288 | tf_op jit(solution)/shard_map/all_to_all | solution.py:351
  102.5 13.8 %copy-start.2 = (bf16[1024,128]{1,0:T(8,128)(2,1)S(1)}, bf16[1024,128]{1,0:T(8,128)(2,1)}, u32[]{:S(2)}) copy-start(bf16[1024,128]{1,0:T(8,128)(2,1)} %w_project_ref.1) | copy-start | bytes 786436
  102.5 13.8 %copy-start.6 = (f32[1024]{0:T(1024)S(1)}, f32[1024]{0:T(1024)}, u32[]{:S(2)}) copy-start(f32[1024]{0:T(1024)} %param.26) | copy-start | bytes 12292
  107.2 9.0 %all-to-all-start.3 = ((bf16[4,32,1024]{2,1,0:T(8,128)(2,1)}), bf16[4,32,1024]{2,1,0:T(8,128)(2,1)S(1)}, u32[]{:S(2)}, u32[]{:S(2)}) async-start(bf16[4,32,1024]{2,1,0:T(8,128)(2,1)} %get-tuple-element.29), calls=%async_computation.3 | async-start | bytes 524288 | tf_op jit(solution)/shard_map/all_to_all | solution.py:356
  117.4 16.7 %all-to-all-start.4 = ((bf16[32,32,128]{2,1,0:T(8,128)(2,1)}), bf16[32,32,128]{2,1,0:T(8,128)(2,1)S(1)}, u32[]{:S(2)}, u32[]{:S(2)}) async-start(bf16[32,32,128]{2,1,0:T(8,128)(2,1)} %embed.1), calls=%async_computation.4 | async-start | bytes 524288 | tf_op jit(solution)/shard_map/all_to_all | solution.py:361
  136.1 14.1 %all-to-all-start.5 = ((f32[32,16,128]{2,1,0:T(8,128)}), f32[32,16,128]{2,1,0:T(8,128)S(1)}, u32[]{:S(2)}, u32[]{:S(2)}) async-start(f32[32,16,128]{2,1,0:T(8,128)} %match.1), calls=%async_computation.5 | async-start | bytes 524288 | tf_op jit(solution)/shard_map/all_to_all | solution.py:377
Sparse Core Ops, SparseCore 0:
  10.2 38.5 all-gather.10
  50.8 62.9 all-gather.12

commit v6 on v5

--- a/solution.py
+++ b/solution.py
@@ -180,31 +180,6 @@
     return call
 
 
-def pages_kernel(key_ref, value_ref, out_ref, sems):
-    copies = []
-    for i in range(4):
-        for j, ref in enumerate((key_ref, value_ref)):
-            target = out_ref.at[i, pl.ds(j * 128, 128), :]
-            copies.append(pltpu.make_async_copy(ref, target, sems.at[2 * i + j]))
-    for copy in copies:
-        copy.start()
-    for copy in copies:
-        copy.wait()
-
-
-def repeat_pages(keys, values):
-    return pl.pallas_call(
-        pages_kernel,
-        out_shape=jax.ShapeDtypeStruct((4, 256, 128), BF),
-        in_specs=[pl.BlockSpec(memory_space=pl.ANY)] * 2,
-        out_specs=pl.BlockSpec(memory_space=pl.ANY),
-        scratch_shapes=[pltpu.SemaphoreType.DMA((8,))],
-        compiler_params=pltpu.CompilerParams(vmem_limit_bytes=52 << 20),
-        cost_estimate=pl.CostEstimate(flops=1000, bytes_accessed=1000, transcendentals=0),
-        name="pages",
-    )(keys, values)
-
-
 def total_kernel(place_ref, terms_ref, out_ref):
     total = terms_ref[0]
     for i in range(1, 32):
@@ -304,18 +279,8 @@
     my_x = lax.axis_index("x").reshape(1)
     token_rows = tokens.reshape(NROW, 1024)
 
-    pages = repeat_pages(key_pages.reshape(128, 128), value_pages.reshape(128, 128))
-    pages_q = lax.all_to_all(pages, "q", 0, 0, tiled=True)
-
-    def both_cores(block, size, parts):
-        return [
-            lax.all_gather(block[i * size : (i + 1) * size], "c", axis=0, tiled=False) for i in parts
-        ]
-
-    inner_parts = both_cores(w_inner, 256, range(4))
-    pages_q, inner_parts, w_outer = lax.optimization_barrier((pages_q, inner_parts, w_outer))
-    prompt = spread(pages_q.reshape(1024, 128), "r", 4)
-    outer_parts = both_cores(w_outer, 128, range(2))
+    pages = jnp.concatenate([key_pages.reshape(128, 128), value_pages.reshape(128, 128)], axis=0)
+    pages_q = spread(pages, "q", 4)
 
     w_out_all = lax.all_gather(w_out, HEAD, axis=0, tiled=True)
     doc_rows = jnp.pad(doc_lengths.astype(BF), ((0, DPAD - DT - 1), (0, 124)))
@@ -328,8 +293,18 @@
     ids = jnp.concatenate([candidates // 64, candidates % 64, request_group[:, None]], axis=1)
     ids = jnp.pad(ids.astype(BF), ((0, 12), (0, 128 - 33)))
     rows = jnp.concatenate([query, own_key, own_value, ids], axis=0)
-    rows, pages_q = lax.optimization_barrier((rows, pages_q))
     rows = lax.all_gather(rows, "y", axis=0, tiled=True)
+    pages_q, rows = lax.optimization_barrier((pages_q, rows))
+    prompt = spread(pages_q.reshape(1024, 128), "r", 4)
+
+    w_inner, w_outer, pages_q = lax.optimization_barrier((w_inner, w_outer, pages_q))
+    inner_parts = [
+        lax.all_gather(w_inner[i * 256 : (i + 1) * 256], "c", axis=0, tiled=False) for i in range(4)
+    ]
+    outer_parts = [
+        lax.all_gather(w_outer[i * 128 : (i + 1) * 128], "c", axis=0, tiled=False) for i in range(4)
+    ]
+
     rows = rows.reshape(4, XROW, 128)
     got = rows[:, 3 * NROW : 3 * NROW + RQ, :33].reshape(16, 33).astype(jnp.int32)
     groups = jnp.where(got[:, 32] // 4 == my_y, got[:, 32] % 4, -1)
@@ -344,10 +319,8 @@
     position = slot[:, :, None] * 64 + jnp.arange(64, dtype=jnp.int32)
     bias = jnp.where(position < lengths[:, None, None], 0.0, -1e30).astype(F32).reshape(4, 1, 512)
 
-    rows, outer_parts = lax.optimization_barrier((rows, outer_parts))
+    rows, inner_parts, outer_parts = lax.optimization_barrier((rows, inner_parts, outer_parts))
     mixed = attend(groups, rows, prompt, bias)
-    w_outer, mixed = lax.optimization_barrier((w_outer, mixed))
-    outer_parts = outer_parts + both_cores(w_outer, 128, range(2, 4))
     back = lax.all_to_all(mixed.reshape(8, 128, 128), ("c", "y"), 0, 0, tiled=True)
     context = jnp.sum(back.reshape(2, 4, 128, 128).astype(F32), axis=1).astype(BF)
     context = lax.all_gather(context, "x", axis=0, tiled=True)

time: 159 us -> 157 us (0.987)
  waiting for transfers between devices: 23.5 us -> 28.8 us
  local copies, waits for them, and re-layouts: 10.9 us -> 7.43 us
  blocking collectives: 46.9 us -> 44.5 us
  starting transfers between devices: 46.1 us -> 44.3 us
    all_to_all x1 -> x0, starting transfers between devices: 15.6 us -> none  [per_device(): pages_q = lax.all_to_all(pages, 'q', 0, 0, tiled=True)]
    all_to_all x1 -> x2, starting transfers between devices: 7.69 us -> 21.6 us  [spread(): lax.all_to_all(wide, axes, 0, 0, tiled=True)]
    all_to_all x1, waiting for transfers between devices: 1.28 us -> 6.34 us  [per_device(): lax.all_to_all(mixed.reshape(8, 128, 128), ('c', 'y'), 0, 0, tiled=True)]
    all_gather x8, blocking collectives: 24.7 us -> 20.9 us  [the longest x4 11.5 us: per_device(): lax.all_gather(w_inner[i * 256:(i + 1) * 256], 'c', axis=0, tiled=False)]
    slice x3 -> x2, local copies, waits for them, and re-layouts: 3.41 us -> 1.33 us  [the longest x1 1.26 us: per_device(): w_inner[i * 256:(i + 1) * 256]]
where the time goes in v6:
time: 157 us; the launch traced here: 156 us
  blocking collectives  44.5 us (28%)
  starting transfers between devices  44.3 us (28%)
  waiting for transfers between devices  28.8 us (18%)
  between operations  14.3 us (9%)
  Pallas kernels  12.5 us (8%)
  local copies, waits for them, and re-layouts  7.43 us (5%)
  other arithmetic  2.76 us (2%)
  matrix products  1.9 us (1%)
    all_to_all x2, starting transfers between devices, spread(): lax.all_to_all(wide, axes, 0, 0, tiled=True)  21.6 us
    all_gather x1, blocking collectives, per_device(): rows = lax.all_gather(rows, 'y', axis=0, tiled=True)  13.1 us
    all_gather x4, blocking collectives, per_device(): lax.all_gather(w_inner[i * 256:(i + 1) * 256], 'c', axis=0, tiled=False)  11.5 us
    all_gather x1, blocking collectives, per_device(): context = lax.all_gather(context, 'x', axis=0, tiled=True)  10.6 us
    all_gather x4, blocking collectives, per_device(): lax.all_gather(w_outer[i * 128:(i + 1) * 128], 'c', axis=0, tiled=False)  9.35 us
    all_to_all x1, waiting for transfers between devices, per_device(): terms = lax.all_to_all(terms, HEAD + ('y',), 0, 0, tiled=True)  8.15 us
    all_to_all x1, starting transfers between devices, per_device(): queries = lax.all_to_all(embed, HEAD + ('y',), 0, 0, tiled=True)  7.93 us
    all_to_all x1, starting transfers between devices, per_device(): lax.all_to_all(mixed.reshape(8, 128, 128), ('c', 'y'), 0, 0, tiled=True)  6.48 us
  transfers between devices with their start and end apart: 8, of which 5 were waited for; matrix products, arithmetic and copies ran while one was open for 8% of the time, Pallas kernels for 6%

profile of v6, /device:TPU:1, one launch (start us, length us, event | category | flops | bytes accessed | tf_op | source)
XLA Modules:
  0.0 156.5 jit_solution(8785786991797786985)
XLA Ops:
  7.3 0.7 all-gather.11.cloned.1.call-update
  8.0 0.8 pad_maximum_fusion.1
  8.7 0.7 broadcast_in_dim.48
  9.5 15.6 %all-to-all-start = ((bf16[4,256,128]{2,1,0:T(8,128)(2,1)}), bf16[4,256,128]{2,1,0:T(8,128)(2,1)S(1)}, u32[]{:S(2)}, u32[]{:S(2)}) async-start(bf16[4,256,128]{2,1,0:T(8,128)(2,1)} %broadcast_in_dim.48), calls=%async_computation | async-start | bytes 524288 | tf_op jit(solution)/shard_map/all_to_all | solution.py:29
  25.1 0.7 fusion.13
  25.8 1.3 convolution_convert_fusion
  27.2 0.3 convolution_convert_fusion.1
  27.5 0.1 copy.50
  27.7 0.3 fusion
  28.0 13.1 %all_gather.60 = bf16[3136,128]{1,0:T(8,128)(2,1)S(1)} all-gather(bf16[784,128]{1,0:T(8,128)(2,1)S(1)} %pad_maximum_fusion), channel_id=1, replica_groups=mesh['x'=4,'c'=2,'y'=4,'q'=4,'r'=4] {'y'}, dimensions={0}, use_global_device_ids=true | all-gather | bytes 1003520 | tf_op jit(solution)/shard_map/all_gather | solution.py:296
  41.1 1.1 broadcast_in_dim.50
  42.2 6.0 %all-to-all-start.1 = ((bf16[4,1024,128]{2,1,0:T(8,128)(2,1)}), bf16[4,1024,128]{2,1,0:T(8,128)(2,1)S(1)}, u32[]{:S(2)}, u32[]{:S(2)}) async-start(bf16[4,1024,128]{2,1,0:T(8,128)(2,1)} %broadcast_in_dim.50), calls=%async_computation.1 | async-start | bytes 2097152 | tf_op jit(solution)/shard_map/all_to_all | solution.py:29
  48.2 0.6 fusion.2
  49.0 0.1 eq.48
  49.1 0.2 select_reduce_fusion
  49.7 1.3 fusion.17
  51.0 4.6 %all-gather = bf16[512,512]{1,0:T(8,128)(2,1)S(1)} all-gather(bf16[256,512]{1,0:T(8,128)(2,1)S(1)} %get-tuple-element.39), channel_id=2, replica_groups=mesh['x'=4,'c'=2,'y'=4,'q'=4,'r'=4] {'c'}, dimensions={0}, use_global_device_ids=true | all-gather | bytes 786432 | tf_op jit(solution)/shard_map/all_gather | solution.py:302
  55.6 2.3 %all-gather.1 = bf16[512,512]{1,0:T(8,128)(2,1)} all-gather(bf16[256,512]{1,0:T(8,128)(2,1)S(1)} %get-tuple-element.38), channel_id=3, replica_groups=mesh['x'=4,'c'=2,'y'=4,'q'=4,'r'=4] {'c'}, dimensions={0}, use_global_device_ids=true | all-gather | bytes 786432 | tf_op jit(solution)/shard_map/all_gather | solution.py:302
  57.9 2.3 %all-gather.2 = bf16[512,512]{1,0:T(8,128)(2,1)} all-gather(bf16[256,512]{1,0:T(8,128)(2,1)S(1)} %get-tuple-element.37), channel_id=4, replica_groups=mesh['x'=4,'c'=2,'y'=4,'q'=4,'r'=4] {'c'}, dimensions={0}, use_global_device_ids=true | all-gather | bytes 786432 | tf_op jit(solution)/shard_map/all_gather | solution.py:302
  60.2 2.3 %all-gather.3 = bf16[512,512]{1,0:T(8,128)(2,1)} all-gather(bf16[256,512]{1,0:T(8,128)(2,1)S(1)} %get-tuple-element.36), channel_id=5, replica_groups=mesh['x'=4,'c'=2,'y'=4,'q'=4,'r'=4] {'c'}, dimensions={0}, use_global_device_ids=true | all-gather | bytes 786432 | tf_op jit(solution)/shard_map/all_gather | solution.py:302
  62.6 2.3 %all-gather.4 = bf16[256,1024]{1,0:T(8,128)(2,1)} all-gather(bf16[128,1024]{1,0:T(8,128)(2,1)S(1)} %get-tuple-element.35), channel_id=6, replica_groups=mesh['x'=4,'c'=2,'y'=4,'q'=4,'r'=4] {'c'}, dimensions={0}, use_global_device_ids=true | all-gather | bytes 786432 | tf_op jit(solution)/shard_map/all_gather | solution.py:305
  64.9 2.3 %all-gather.5 = bf16[256,1024]{1,0:T(8,128)(2,1)} all-gather(bf16[128,1024]{1,0:T(8,128)(2,1)S(1)} %get-tuple-element.34), channel_id=7, replica_groups=mesh['x'=4,'c'=2,'y'=4,'q'=4,'r'=4] {'c'}, dimensions={0}, use_global_device_ids=true | all-gather | bytes 786432 | tf_op jit(solution)/shard_map/all_gather | solution.py:305
  67.2 2.3 %all-gather.6 = bf16[256,1024]{1,0:T(8,128)(2,1)} all-gather(bf16[128,1024]{1,0:T(8,128)(2,1)S(1)} %get-tuple-element.33), channel_id=8, replica_groups=mesh['x'=4,'c'=2,'y'=4,'q'=4,'r'=4] {'c'}, dimensions={0}, use_global_device_ids=true | all-gather | bytes 786432 | tf_op jit(solution)/shard_map/all_gather | solution.py:305
  69.5 2.4 %all-gather.7 = bf16[256,1024]{1,0:T(8,128)(2,1)} all-gather(bf16[128,1024]{1,0:T(8,128)(2,1)S(1)} %get-tuple-element.32), channel_id=9, replica_groups=mesh['x'=4,'c'=2,'y'=4,'q'=4,'r'=4] {'c'}, dimensions={0}, use_global_device_ids=true | all-gather | bytes 786432 | tf_op jit(solution)/shard_map/all_gather | solution.py:305
  72.0 0.2 slice_reduce_fusion
  72.2 2.0 %all-to-all-done.1 = bf16[4,1024,128]{2,1,0:T(8,128)(2,1)S(1)} async-done(((bf16[4,1024,128]{2,1,0:T(8,128)(2,1)}), bf16[4,1024,128]{2,1,0:T(8,128)(2,1)S(1)}, u32[]{:S(2)}, u32[]{:S(2)}) %all-to-all-start.1) | async-done | bytes 1048608 | tf_op jit(solution)/shard_map/all_to_all | solution.py:29
  74.2 3.1 %attend.1 = bf16[2,4,128,128]{3,2,1,0:T(8,128)(2,1)} custom-call(s32[16]{0:T(128)S(1)} %compare_select_fusion.2.group_ref, bf16[4,784,128]{2,1,0:T(8,128)(2,1)S(1)} %bitcast.50, bf16[4096,128]{1,0:T(8,128)(2,1)S(1)} %bitcast.47, f32[4,1,512]{2,1,0:T(1,128)S(1)} %compare_select_fusion.bias_ref), custom_call_target="tpu_custom_call" | custom-call | flops 1000 | bytes 1000 | tf_op jit(solution)/shard_map/attend/pallas_call | solution.py:88
  77.2 6.5 %all-to-all-start.2 = ((bf16[8,128,128]{2,1,0:T(8,128)(2,1)}), bf16[8,128,128]{2,1,0:T(8,128)(2,1)S(1)}, u32[]{:S(2)}, u32[]{:S(2)}) async-start(bf16[8,128,128]{2,1,0:T(8,128)(2,1)} %bitcast.18), calls=%async_computation.2 | async-start | bytes 524288 | tf_op jit(solution)/shard_map/all_to_all | solution.py:324
  83.9 6.3 %all-to-all-done.2 = bf16[8,128,128]{2,1,0:T(8,128)(2,1)S(1)} async-done(((bf16[8,128,128]{2,1,0:T(8,128)(2,1)}), bf16[8,128,128]{2,1,0:T(8,128)(2,1)S(1)}, u32[]{:S(2)}, u32[]{:S(2)}) %all-to-all-start.2) | async-done | bytes 262176 | tf_op jit(solution)/shard_map/all_to_all | solution.py:324
  90.3 10.6 %all_gather.77.context_ref = bf16[8,128,128]{2,1,0:T(8,128)(2,1)S(1)} all-gather(bf16[2,128,128]{2,1,0:T(8,128)(2,1)S(1)} %bitcast_reduce_fusion), channel_id=1, replica_groups=mesh['x'=4,'c'=2,'y'=4,'q'=4,'r'=4] {'x'}, dimensions={0}, use_global_device_ids=true | all-gather | bytes 327680 | tf_op jit(solution)/shard_map/all_gather | solution.py:326
  100.9 4.7 %dense.1 = (bf16[128,1024]{1,0:T(8,128)(2,1)S(1)}, bf16[4,32,1024]{2,1,0:T(8,128)(2,1)}) custom-call(s32[1]{0:T(128)} %bitcast.1.place_ref, bf16[8,128,128]{2,1,0:T(8,128)(2,1)S(1)} %all_gather.77.context_ref, bf16[256,1024]{1,0:T(8,128)(2,1)S(1)} %bitcast.46, f32[1,1024]{1,0:T(1,128)S(1)} %bitcast.54, ...), custom_call_target="tpu_custom_call" | custom-call | flops 1000 | bytes 1000 | tf_op jit(solution)/shard_map/dense/pallas_call | solution.py:229
  105.6 3.4 %all-to-all-start.3 = ((bf16[4,32,1024]{2,1,0:T(8,128)(2,1)}), bf16[4,32,1024]{2,1,0:T(8,128)(2,1)S(1)}, u32[]{:S(2)}, u32[]{:S(2)}) async-start(bf16[4,32,1024]{2,1,0:T(8,128)(2,1)} %get-tuple-element.31), calls=%async_computation.3 | async-start | bytes 524288 | tf_op jit(solution)/shard_map/all_to_all | solution.py:329
  109.2 5.4 %all-to-all-done.3.terms_ref = bf16[4,32,1024]{2,1,0:T(8,128)(2,1)S(1)} async-done(((bf16[4,32,1024]{2,1,0:T(8,128)(2,1)}), bf16[4,32,1024]{2,1,0:T(8,128)(2,1)S(1)}, u32[]{:S(2)}, u32[]{:S(2)}) %all-to-all-start.3) | async-done | bytes 262176 | tf_op jit(solution)/shard_map/all_to_all | solution.py:329
  114.5 1.1 embed.1
  115.7 7.9 %all-to-all-start.4 = ((bf16[32,32,128]{2,1,0:T(8,128)(2,1)}), bf16[32,32,128]{2,1,0:T(8,128)(2,1)S(1)}, u32[]{:S(2)}, u32[]{:S(2)}) async-start(bf16[32,32,128]{2,1,0:T(8,128)(2,1)} %embed.1), calls=%async_computation.4 | async-start | bytes 524288 | tf_op jit(solution)/shard_map/all_to_all | solution.py:334
  123.6 0.1 fusion.3
  123.8 0.8 slice.61
  124.6 0.1 copy.56
  124.6 0.1 reshape.152
  124.7 1.3 slice.62
  126.1 0.1 copy.57
  126.2 0.1 reduce_window_sum.14.last_ref
  126.3 6.2 %all-to-all-done.4 = bf16[32,32,128]{2,1,0:T(8,128)(2,1)S(1)} async-done(((bf16[32,32,128]{2,1,0:T(8,128)(2,1)}), bf16[32,32,128]{2,1,0:T(8,128)(2,1)S(1)}, u32[]{:S(2)}, u32[]{:S(2)}) %all-to-all-start.4) | async-done | bytes 262176 | tf_op jit(solution)/shard_map/all_to_all | solution.py:334
  132.4 2.9 %match.1 = f32[32,16,128]{2,1,0:T(8,128)} custom-call(s32[64]{0:T(128)S(1)} %convert_element_type.45.need_ref, s32[64]{0:T(128)S(1)} %sub.16.first_ref, s32[64]{0:T(128)S(1)} %reduce_window_sum.14.last_ref, bf16[1024,128]{1,0:T(8,128)(2,1)S(1)} %bitcast.52, bf16[4096,128]{1,0:T(8,128)(2,1)S(1)} %bitcast.48, s32[16,128]{1,0:T(8,128)S(1)} %pad.14.pick_ref), custom_call_target="tpu_custom_call" | custom-call | flops 1000 | bytes 1000 | tf_op jit(solution)/shard_map/match/pallas_call | solution.py:155
  135.3 4.8 %all-to-all-start.5 = ((f32[32,16,128]{2,1,0:T(8,128)}), f32[32,16,128]{2,1,0:T(8,128)S(1)}, u32[]{:S(2)}, u32[]{:S(2)}) async-start(f32[32,16,128]{2,1,0:T(8,128)} %match.1), calls=%async_computation.5 | async-start | bytes 524288 | tf_op jit(solution)/shard_map/all_to_all | solution.py:350
  140.1 0.6 copy.51
  140.8 8.1 %all-to-all-done.5.terms_ref = f32[32,16,128]{2,1,0:T(8,128)S(1)} async-done(((f32[32,16,128]{2,1,0:T(8,128)}), f32[32,16,128]{2,1,0:T(8,128)S(1)}, u32[]{:S(2)}, u32[]{:S(2)}) %all-to-all-start.5) | async-done | bytes 262176 | tf_op jit(solution)/shard_map/all_to_all | solution.py:350
  148.9 0.7 total.1
  (62 shorter events, 1.4 us)
Async XLA Ops:
  7.2 18.6 %copy-start = (bf16[1024,128]{1,0:T(8,128)(2,1)S(1)}, bf16[1024,128]{1,0:T(8,128)(2,1)}, u32[]{:S(2)}) copy-start(bf16[1024,128]{1,0:T(8,128)(2,1)} %param.21) | copy-start | bytes 786436
  7.2 20.0 %copy-start.1 = (bf16[4,64,1024]{2,1,0:T(8,128)(2,1)S(1)}, bf16[4,64,1024]{2,1,0:T(8,128)(2,1)}, u32[]{:S(2)}) copy-start(bf16[4,64,1024]{2,1,0:T(8,128)(2,1)} %param.18) | copy-start | bytes 1572868
  7.2 20.0 %copy-start.6 = (bf16[1024,128]{1,0:T(8,128)(2,1)S(1)}, bf16[1024,128]{1,0:T(8,128)(2,1)}, u32[]{:S(2)}) copy-start(bf16[1024,128]{1,0:T(8,128)(2,1)} %param.20) | copy-start | bytes 786436
  7.2 20.2 %copy-start.9 = (s32[4]{0:T(128)S(1)}, s32[4]{0:T(128)}, u32[]{:S(2)}) copy-start(s32[4]{0:T(128)} %param.32) | copy-start | bytes 52
  7.2 20.4 %copy-start.7 = (bf16[1024,128]{1,0:T(8,128)(2,1)S(1)}, bf16[1024,128]{1,0:T(8,128)(2,1)}, u32[]{:S(2)}) copy-start(bf16[1024,128]{1,0:T(8,128)(2,1)} %param.19) | copy-start | bytes 786436
  7.2 93.6 %all-gather.11.cloned.1.call-start = ((), (), s32[]{:S(2)}) async-start(), calls=%async_computation.6 | async-start | bytes 2359296 | tf_op jit(solution)/shard_map/all_gather | solution.py:285
  9.5 31.6 %all-to-all-start = ((bf16[4,256,128]{2,1,0:T(8,128)(2,1)}), bf16[4,256,128]{2,1,0:T(8,128)(2,1)S(1)}, u32[]{:S(2)}, u32[]{:S(2)}) async-start(bf16[4,256,128]{2,1,0:T(8,128)(2,1)} %broadcast_in_dim.48), calls=%async_computation | async-start | bytes 524288 | tf_op jit(solution)/shard_map/all_to_all | solution.py:29
  28.0 20.2 %copy-start.10 = (s32[1,4]{1,0:T(1,128)S(1)}, s32[1,4]{1,0:T(1,128)}, u32[]{:S(2)}) copy-start(s32[1,4]{1,0:T(1,128)} %param.34) | copy-start | bytes 52
  28.0 20.2 %copy-start.8 = (bf16[256,128]{1,0:T(8,128)(2,1)S(1)}, bf16[256,128]{1,0:T(8,128)(2,1)}, u32[]{:S(2)}) copy-start(bf16[256,128]{1,0:T(8,128)(2,1)} %param.33) | copy-start | bytes 196612
  28.0 20.9 %copy-start.11 = (s32[128]{0:T(128)S(1)}, s32[128]{0:T(128)}, u32[]{:S(2)}) copy-start(s32[128]{0:T(128)} %param.30) | copy-start | bytes 1540
  41.1 8.5 %copy-start.12 = (s32[16]{0:T(128)S(1)}, s32[16]{0:T(128)}, u32[]{:S(2)}) copy-start(s32[16]{0:T(128)} %param.31) | copy-start | bytes 196
  42.2 32.0 %all-to-all-start.1 = ((bf16[4,1024,128]{2,1,0:T(8,128)(2,1)}), bf16[4,1024,128]{2,1,0:T(8,128)(2,1)S(1)}, u32[]{:S(2)}, u32[]{:S(2)}) async-start(bf16[4,1024,128]{2,1,0:T(8,128)(2,1)} %broadcast_in_dim.50), calls=%async_computation.1 | async-start | bytes 2097152 | tf_op jit(solution)/shard_map/all_to_all | solution.py:29
  48.2 75.6 %all-gather.13.cloned.1.call-start = ((), (), s32[]{:S(2)}) async-start(), calls=%async_computation.7 | async-start | bytes 1183744 | tf_op jit(solution)/shard_map/all_gather | solution.py:288
  51.0 11.6 %copy-start.5 = (bf16[512,1024]{1,0:T(8,128)(2,1)S(1)}, bf16[512,1024]{1,0:T(8,128)(2,1)}, u32[]{:S(2)}) copy-start(bf16[512,1024]{1,0:T(8,128)(2,1)} %param.25) | copy-start | bytes 3145732
  69.5 31.3 %copy-start.3 = (f32[1024]{0:T(1024)S(1)}, f32[1024]{0:T(1024)}, u32[]{:S(2)}) copy-start(f32[1024]{0:T(1024)} %param.23) | copy-start | bytes 12292
  77.2 13.0 %all-to-all-start.2 = ((bf16[8,128,128]{2,1,0:T(8,128)(2,1)}), bf16[8,128,128]{2,1,0:T(8,128)(2,1)S(1)}, u32[]{:S(2)}, u32[]{:S(2)}) async-start(bf16[8,128,128]{2,1,0:T(8,128)(2,1)} %bitcast.18), calls=%async_computation.2 | async-start | bytes 524288 | tf_op jit(solution)/shard_map/all_to_all | solution.py:324
  100.9 13.7 %copy-start.2 = (bf16[1024,128]{1,0:T(8,128)(2,1)S(1)}, bf16[1024,128]{1,0:T(8,128)(2,1)}, u32[]{:S(2)}) copy-start(bf16[1024,128]{1,0:T(8,128)(2,1)} %w_project_ref.1) | copy-start | bytes 786436
  100.9 13.7 %copy-start.4 = (f32[1024]{0:T(1024)S(1)}, f32[1024]{0:T(1024)}, u32[]{:S(2)}) copy-start(f32[1024]{0:T(1024)} %param.26) | copy-start | bytes 12292
  105.6 9.0 %all-to-all-start.3 = ((bf16[4,32,1024]{2,1,0:T(8,128)(2,1)}), bf16[4,32,1024]{2,1,0:T(8,128)(2,1)S(1)}, u32[]{:S(2)}, u32[]{:S(2)}) async-start(bf16[4,32,1024]{2,1,0:T(8,128)(2,1)} %get-tuple-element.31), calls=%async_computation.3 | async-start | bytes 524288 | tf_op jit(solution)/shard_map/all_to_all | solution.py:329
  115.7 16.7 %all-to-all-start.4 = ((bf16[32,32,128]{2,1,0:T(8,128)(2,1)}), bf16[32,32,128]{2,1,0:T(8,128)(2,1)S(1)}, u32[]{:S(2)}, u32[]{:S(2)}) async-start(bf16[32,32,128]{2,1,0:T(8,128)(2,1)} %embed.1), calls=%async_computation.4 | async-start | bytes 524288 | tf_op jit(solution)/shard_map/all_to_all | solution.py:334
  135.3 13.6 %all-to-all-start.5 = ((f32[32,16,128]{2,1,0:T(8,128)}), f32[32,16,128]{2,1,0:T(8,128)S(1)}, u32[]{:S(2)}, u32[]{:S(2)}) async-start(f32[32,16,128]{2,1,0:T(8,128)} %match.1), calls=%async_computation.5 | async-start | bytes 524288 | tf_op jit(solution)/shard_map/all_to_all | solution.py:350
Sparse Core Ops, SparseCore 0:
  10.2 38.5 all-gather.10
  51.1 63.4 all-gather.12

commit v7 on v6

--- a/solution.py
+++ b/solution.py
@@ -29,11 +29,16 @@
     return lax.all_to_all(wide, axes, 0, 0, tiled=True).reshape((-1,) + block.shape[1:])
 
 
+def from_ahead(block, step):
+    return lax.ppermute(block, ("q", "r"), [((i + step) % 16, i) for i in range(16)])
+
+
 def nt_dot(a, b):
     return lax.dot_general(a, b, (((1,), (1,)), ((), ())), preferred_element_type=F32)
 
 
-def attend_kernel(group_ref, rows_ref, prompt_ref, bias_ref, out_ref, order_ref):
+def attend_kernel(group_ref, rows_ref, bias_ref, *refs):
+    prompt_refs, out_ref, order_ref = refs[:4], refs[4], refs[5]
     low_half = lax.broadcasted_iota(jnp.int32, (QL, 128), 1) < 64
     out_ref[...] = jnp.zeros_like(out_ref)
     count = jnp.int32(0)
@@ -55,9 +60,9 @@
         parts = [nt_dot(both, own_key)]
         values = [own_value]
         for piece in range(4):
-            start = pl.multiple_of(piece * 1024 + group * 256, 256)
-            key = prompt_ref[pl.ds(start, 128), :]
-            values.append(prompt_ref[pl.ds(pl.multiple_of(start + 128, 128), 128), :])
+            start = pl.multiple_of(group * 256, 256)
+            key = prompt_refs[piece][pl.ds(start, 128), :]
+            values.append(prompt_refs[piece][pl.ds(pl.multiple_of(start + 128, 128), 128), :])
             bias = bias_ref[group, :, piece * 128 : (piece + 1) * 128]
             parts.append(nt_dot(both, key) + bias)
         top = jnp.max(parts[0], axis=-1, keepdims=True)
@@ -77,8 +82,7 @@
         k = order_ref[jnp.where(2 * step + 1 < count, 2 * step + 1, 2 * step)]
         results = [one_request(i), one_request(k)]
         for j, result in zip((i, k), results):
-            place = pl.multiple_of((j % 2) * QL, QL)
-            out_ref[(j % RQ) // 2, j // RQ, pl.ds(place, QL), :] = result
+            out_ref[j // RQ, pl.ds(pl.multiple_of((j % RQ) * QL, QL), QL), :] = result
         return carry
 
     lax.fori_loop(0, (count + 1) // 2, two_requests, 0)
@@ -87,19 +91,17 @@
 def attend(groups, rows, prompt, bias):
     return pl.pallas_call(
         attend_kernel,
-        out_shape=jax.ShapeDtypeStruct((2, 4, 2 * QL, 128), BF),
+        out_shape=jax.ShapeDtypeStruct((4, NROW, 128), BF),
         in_specs=[
             pl.BlockSpec(memory_space=pltpu.SMEM),
-            pl.BlockSpec(memory_space=pltpu.VMEM),
-            pl.BlockSpec(memory_space=pltpu.VMEM),
-            pl.BlockSpec(memory_space=pltpu.VMEM),
-        ],
+        ]
+        + [pl.BlockSpec(memory_space=pltpu.VMEM)] * 6,
         out_specs=pl.BlockSpec(memory_space=pltpu.VMEM),
         scratch_shapes=[pltpu.SMEM((17,), jnp.int32)],
         compiler_params=pltpu.CompilerParams(vmem_limit_bytes=16 << 20),
         cost_estimate=pl.CostEstimate(flops=1000, bytes_accessed=1000, transcendentals=0),
         name="attend",
-    )(groups, rows, prompt, bias)
+    )(groups, rows, bias, *prompt)
 
 
 def match_kernel(need_ref, first_ref, last_ref, query_ref, docs_ref, pick_ref, out_ref, sims_ref, best_ref, term_ref):
@@ -142,7 +144,7 @@
     ).reshape(64, 8, 128)
     head = lax.broadcasted_iota(jnp.int32, (64, 8, 128), 1)
     request = lax.broadcasted_iota(jnp.int32, (64, 8, 128), 2)
-    per_doc = jnp.sum(jnp.where((head % 2) * 2 + head // 4 == request % RQ, sums, 0.0), axis=1)
+    per_doc = jnp.sum(jnp.where(head // 2 == request % RQ, sums, 0.0), axis=1)
     doc_row = lax.broadcasted_iota(jnp.int32, (64, 128), 0)
     for c in range(NC):
         hit = doc_row == pick_ref[c : c + 1, :]
@@ -193,14 +195,13 @@
     out_ref[...] = picked[:RQ]
 
 
-def dense_kernel(place_ref, context_ref, token_ref, gain_ref, *refs):
-    held, first_ref, terms_ref, scratch, sems = refs[:9], refs[9], refs[10], refs[11:20], refs[20]
-    copies = [pltpu.make_async_copy(held[i], scratch[i], sems.at[i]) for i in range(9)]
+def dense_kernel(context_ref, token_ref, gain_ref, *refs):
+    held, first_ref, terms_ref, scratch, sems = refs[:3], refs[3], refs[4], refs[5:8], refs[8]
+    copies = [pltpu.make_async_copy(held[i], scratch[i], sems.at[i]) for i in range(3)]
     for copy in copies:
         copy.start()
-    w_out_ref, inner_refs, outer_refs = scratch[0], scratch[1:5], scratch[5:9]
-    start = pl.multiple_of(place_ref[0] * 128, 128)
-    attn = token_ref[pl.ds(start, 128), :].astype(F32)
+    w_out_ref, inner_ref, outer_ref = scratch
+    attn = token_ref[...].astype(F32)
     copies[0].wait()
     for h in range(8):
         attn = attn + jnp.dot(
@@ -208,43 +209,32 @@
         )
     first = layer_norm(attn, gain_ref[...]).astype(BF)
     first_ref[...] = first
-    for copy in copies[1:]:
-        copy.wait()
-    total = jnp.zeros((128, 1024), F32)
-    for core in range(2):
-        inner = jnp.zeros((128, 512), F32)
-        for part in range(4):
-            inner = inner + jnp.dot(
-                first[:, part * 256 : (part + 1) * 256], inner_refs[part][core], preferred_element_type=F32
-            )
-        active = (0.5 * inner * (1.0 + lax.erf(inner * (0.5**0.5)))).astype(BF)
-        for part in range(4):
-            total = total + jnp.dot(
-                active[:, part * 128 : (part + 1) * 128], outer_refs[part][core], preferred_element_type=F32
-            )
-    terms_ref[...] = total.astype(BF).reshape(4, 32, 1024)
-
-
-def dense(place, context, tokens, gain, weights):
+    copies[1].wait()
+    inner = jnp.dot(first, inner_ref[...], preferred_element_type=F32)
+    active = (0.5 * inner * (1.0 + lax.erf(inner * (0.5**0.5)))).astype(BF)
+    copies[2].wait()
+    total = jnp.dot(active, outer_ref[...], preferred_element_type=F32)
+    terms_ref[...] = total.astype(BF).reshape(8, 32, 1024)
+
+
+def dense(context, tokens, gain, weights):
     return pl.pallas_call(
         dense_kernel,
-        out_shape=(jax.ShapeDtypeStruct((128, 1024), BF), jax.ShapeDtypeStruct((4, 32, 1024), BF)),
-        in_specs=[pl.BlockSpec(memory_space=pltpu.SMEM)]
-        + [pl.BlockSpec(memory_space=pltpu.VMEM)] * 3
-        + [pl.BlockSpec(memory_space=pl.ANY)] * 9,
+        out_shape=(jax.ShapeDtypeStruct((NROW, 1024), BF), jax.ShapeDtypeStruct((8, 32, 1024), BF)),
+        in_specs=[pl.BlockSpec(memory_space=pltpu.VMEM)] * 3 + [pl.BlockSpec(memory_space=pl.ANY)] * 3,
         out_specs=(pl.BlockSpec(memory_space=pltpu.VMEM), pl.BlockSpec(memory_space=pltpu.VMEM)),
-        scratch_shapes=[pltpu.VMEM(w.shape, w.dtype) for w in weights] + [pltpu.SemaphoreType.DMA((9,))],
+        scratch_shapes=[pltpu.VMEM(w.shape, w.dtype) for w in weights] + [pltpu.SemaphoreType.DMA((3,))],
         compiler_params=pltpu.CompilerParams(vmem_limit_bytes=52 << 20),
         cost_estimate=pl.CostEstimate(flops=1000, bytes_accessed=1000, transcendentals=0),
         name="dense",
-    )(place, context, tokens, gain, *weights)
+    )(context, tokens, gain, *weights)
 
 
 def embed_kernel(place_ref, first_ref, terms_ref, gain_ref, w_project_ref, out_ref):
     start = pl.multiple_of(place_ref[0] * 32, 32)
     total = first_ref[pl.ds(start, 32), :].astype(F32)
-    for x in range(4):
-        total = total + terms_ref[x].astype(F32)
+    for h in range(8):
+        total = total + terms_ref[h].astype(F32)
     second = layer_norm(total, gain_ref[...]).astype(BF)
     projected = jnp.dot(second, w_project_ref[...], preferred_element_type=F32)
     scale = lax.rsqrt(jnp.sum(projected * projected, axis=-1, keepdims=True) + 1e-06)
@@ -275,8 +265,6 @@
 ):
     my_y = lax.axis_index("y")
     my_head = lax.axis_index(HEAD)
-    my_core = lax.axis_index("c").reshape(1)
-    my_x = lax.axis_index("x").reshape(1)
     token_rows = tokens.reshape(NROW, 1024)
 
     pages = jnp.concatenate([key_pages.reshape(128, 128), value_pages.reshape(128, 128)], axis=0)
@@ -295,15 +283,9 @@
     rows = jnp.concatenate([query, own_key, own_value, ids], axis=0)
     rows = lax.all_gather(rows, "y", axis=0, tiled=True)
     pages_q, rows = lax.optimization_barrier((pages_q, rows))
-    prompt = spread(pages_q.reshape(1024, 128), "r", 4)
-
-    w_inner, w_outer, pages_q = lax.optimization_barrier((w_inner, w_outer, pages_q))
-    inner_parts = [
-        lax.all_gather(w_inner[i * 256 : (i + 1) * 256], "c", axis=0, tiled=False) for i in range(4)
-    ]
-    outer_parts = [
-        lax.all_gather(w_outer[i * 128 : (i + 1) * 128], "c", axis=0, tiled=False) for i in range(4)
-    ]
+    pages_q = pages_q.reshape(1024, 128)
+    ahead_two = jnp.concatenate([from_ahead(pages_q[:512], 2), from_ahead(pages_q[512:], -2)], axis=0)
+    prompt = [pages_q, from_ahead(pages_q, 1), ahead_two, from_ahead(pages_q, -1)]
 
     rows = rows.reshape(4, XROW, 128)
     got = rows[:, 3 * NROW : 3 * NROW + RQ, :33].reshape(16, 33).astype(jnp.int32)
@@ -317,25 +299,26 @@
         jnp.where(table[:, None, :] == page_ids[:, :, None], jnp.arange(8, dtype=jnp.int32), 0), axis=-1
     )
     position = slot[:, :, None] * 64 + jnp.arange(64, dtype=jnp.int32)
-    bias = jnp.where(position < lengths[:, None, None], 0.0, -1e30).astype(F32).reshape(4, 1, 512)
-
-    rows, inner_parts, outer_parts = lax.optimization_barrier((rows, inner_parts, outer_parts))
+    bias = jnp.where(position < lengths[:, None, None], 0.0, -1e30).astype(F32).reshape(4, 4, 128)
+    ahead = (lax.axis_index("r") + jnp.arange(4, dtype=jnp.int32)) % 4
+    turn = ahead[:, None] == jnp.arange(4, dtype=jnp.int32)
+    bias = jnp.sum(jnp.where(turn[None, :, :, None], bias[:, None], 0.0), axis=2).reshape(4, 1, 512)
+
     mixed = attend(groups, rows, prompt, bias)
-    back = lax.all_to_all(mixed.reshape(8, 128, 128), ("c", "y"), 0, 0, tiled=True)
-    context = jnp.sum(back.reshape(2, 4, 128, 128).astype(F32), axis=1).astype(BF)
-    context = lax.all_gather(context, "x", axis=0, tiled=True)
-    weights = [w_out_all] + inner_parts + outer_parts
-    first, terms = dense(my_core, context, token_rows, norm1_gain[None], weights)
-    terms = lax.all_to_all(terms, "x", 0, 0, tiled=True)
+    back = lax.all_to_all(mixed, "y", 0, 0, tiled=True)
+    context = jnp.sum(back.astype(F32), axis=0).astype(BF)
+    context = lax.all_gather(context, HEAD, axis=0, tiled=False)
+    first, terms = dense(context, token_rows, norm1_gain[None], [w_out_all, w_inner, w_outer])
+    terms = lax.all_to_all(terms, HEAD, 0, 0, tiled=True)
     embed = vmem_call(embed_kernel, jax.ShapeDtypeStruct((32, 32, 128), BF), "embed", 1)(
-        my_x, first, terms, norm2_gain[None], w_project
+        my_head.reshape(1), first, terms, norm2_gain[None], w_project
     )
 
     queries = lax.all_to_all(embed, HEAD + ("y",), 0, 0, tiled=True)
-    own = lax.dynamic_slice(queries.reshape(4, 2, 4, 32, 128), (0, 0, my_y, 0, 0), (4, 2, 1, 32, 128))
-    embedded = jnp.transpose(own, (1, 0, 2, 3, 4)).reshape(RQ, QL, 128)
-
-    docs = docs.reshape(16, DPAD, 128)
+    own = lax.dynamic_slice(queries.reshape(8, 4, 32, 128), (0, my_y, 0, 0), (8, 1, 32, 128))
+    embedded = own.reshape(RQ, QL, 128)
+
+    docs = lax.optimization_barrier((docs, embed))[0].reshape(16, DPAD, 128)
     doc_len = docs[:, DT, :4].astype(jnp.int32)
     docs = docs[:, :DT].reshape(16 * DT, 128)
     doc_last = jnp.cumsum(doc_len, axis=1)

time: 157 us -> 154 us (0.981)
  blocking collectives: 44.5 us -> 41.6 us
  starting transfers between devices: 44.3 us -> 42.3 us
  local copies, waits for them, and re-layouts: 7.43 us -> 5.67 us
    ppermute x0 -> x4, starting transfers between devices: none -> 13.9 us  [from_ahead(): lax.ppermute(block, ('q', 'r'), [((i + step) % 16, i) for i in range(16)])]
    all_gather x9 -> x1, blocking collectives: 31.4 us -> 20.6 us  [per_device(): context = lax.all_gather(context, HEAD, axis=0, tiled=False)]
    all_to_all x0 -> x1, blocking collectives: none -> 7.97 us  [per_device(): back = lax.all_to_all(mixed, 'y', 0, 0, tiled=True)]
    all_to_all x2 -> x1, starting transfers between devices: 9.89 us -> 3.85 us  [per_device(): terms = lax.all_to_all(terms, HEAD, 0, 0, tiled=True)]
    all_to_all x2 -> x1, starting transfers between devices: 21.6 us -> 15.6 us  [spread(): lax.all_to_all(wide, axes, 0, 0, tiled=True)]
    ppermute x0 -> x4, waiting for transfers between devices: none -> 5.49 us  [from_ahead(): lax.ppermute(block, ('q', 'r'), [((i + step) % 16, i) for i in range(16)])]
    all_to_all x1, starting transfers between devices: 7.93 us -> 4.41 us  [per_device(): queries = lax.all_to_all(embed, HEAD + ('y',), 0, 0, tiled=True)]
    all_to_all x2 -> x1, waiting for transfers between devices: 11.7 us -> 9.1 us  [per_device(): terms = lax.all_to_all(terms, HEAD, 0, 0, tiled=True)]
  transfers between devices with their start and end apart: 8 -> 10, of which waited for: 5 -> 5; matrix products, arithmetic and copies ran while one was open for 8% -> 7% of each run, Pallas kernels for 6% -> 7%
where the time goes in v7:
time: 154 us; the launch traced here: 153 us
  starting transfers between devices  42.3 us (27%)
  blocking collectives  41.6 us (27%)
  waiting for transfers between devices  29.7 us (19%)
  between operations  14.4 us (9%)
  Pallas kernels  13.6 us (9%)
  local copies, waits for them, and re-layouts  5.67 us (4%)
  other arithmetic  3.76 us (2%)
  matrix products  1.91 us (1%)
    all_gather x1, blocking collectives, per_device(): context = lax.all_gather(context, HEAD, axis=0, tiled=False)  20.6 us
    all_to_all x1, starting transfers between devices, spread(): lax.all_to_all(wide, axes, 0, 0, tiled=True)  15.6 us
    ppermute x4, starting transfers between devices, from_ahead(): lax.ppermute(block, ('q', 'r'), [((i + step) % 16, i) for i in range(16)])  13.9 us
    all_gather x1, blocking collectives, per_device(): rows = lax.all_gather(rows, 'y', axis=0, tiled=True)  13.1 us
    all_to_all x1, waiting for transfers between devices, per_device(): terms = lax.all_to_all(terms, HEAD, 0, 0, tiled=True)  9.1 us
    all_to_all x1, waiting for transfers between devices, per_device(): terms = lax.all_to_all(terms, HEAD + ('y',), 0, 0, tiled=True)  8.16 us
    all_to_all x1, blocking collectives, per_device(): back = lax.all_to_all(mixed, 'y', 0, 0, tiled=True)  7.97 us
    all_to_all x1, waiting for transfers between devices, per_device(): queries = lax.all_to_all(embed, HEAD + ('y',), 0, 0, tiled=True)  6.25 us
  transfers between devices with their start and end apart: 10, of which 5 were waited for; matrix products, arithmetic and copies ran while one was open for 7% of the time, Pallas kernels for 7%

profile of v7, /device:TPU:1, one launch (start us, length us, event | category | flops | bytes accessed | tf_op | source)
XLA Modules:
  0.0 153.0 jit_solution(6095700294406188199)
XLA Ops:
  7.3 0.7 all-gather.4.cloned.1.call-update
  8.0 0.8 pad_maximum_fusion.2
  8.8 0.8 broadcast_in_dim.65
  9.5 15.6 %all-to-all-start = ((bf16[4,256,128]{2,1,0:T(8,128)(2,1)}), bf16[4,256,128]{2,1,0:T(8,128)(2,1)S(1)}, u32[]{:S(2)}, u32[]{:S(2)}) async-start(bf16[4,256,128]{2,1,0:T(8,128)(2,1)} %broadcast_in_dim.65), calls=%async_computation | async-start | bytes 524288 | tf_op jit(solution)/shard_map/all_to_all | solution.py:29
  25.1 0.7 convert_element_type.46
  25.8 1.5 fusion.2
  27.3 0.7 dynamic_slice.9
  28.0 0.1 eq.70
  28.1 0.2 select_reduce_fusion.1
  28.5 1.3 convolution_convert_fusion
  29.8 0.3 convolution_convert_fusion.1
  30.1 0.3 fusion
  30.5 0.1 copy.39
  30.6 0.1 fusion.13
  30.7 0.1 add.102
  30.8 0.1 add.104
  30.9 0.1 dynamic_slice.10
  31.1 0.1 select_reduce_fusion
  31.2 13.1 %all_gather.15 = bf16[3136,128]{1,0:T(8,128)(2,1)S(1)} all-gather(bf16[784,128]{1,0:T(8,128)(2,1)S(1)} %pad_maximum_fusion.1), channel_id=1, replica_groups=mesh['x'=4,'c'=2,'y'=4,'q'=4,'r'=4] {'y'}, dimensions={0}, use_global_device_ids=true | all-gather | bytes 1003520 | tf_op jit(solution)/shard_map/all_gather | solution.py:284
  44.2 5.8 %collective-permute-start = (bf16[1024,128]{1,0:T(8,128)(2,1)S(1)}, bf16[1024,128]{1,0:T(8,128)(2,1)S(1)}, u32[]{:S(2)}, u32[]{:S(2)}) collective-permute-start(bf16[1024,128]{1,0:T(8,128)(2,1)S(1)} %bitcast.33), channel_id=1, source_target_pairs={{1,0},{2,1},{3,2},{4,3},{5,4},{6,5},{7,6},{8,7},{9,8},{10,9},{11,1... | collective-permute-start | bytes 786440 | tf_op jit(solution)/shard_map/ppermute | solution.py:33
  50.1 1.9 %collective-permute-start.3 = (bf16[1024,128]{1,0:T(8,128)(2,1)S(1)}, bf16[1024,128]{1,0:T(8,128)(2,1)S(1)}, u32[]{:S(2)}, u32[]{:S(2)}) collective-permute-start(bf16[1024,128]{1,0:T(8,128)(2,1)S(1)} %bitcast.34), channel_id=1, source_target_pairs={{15,0},{0,1},{1,2},{2,3},{3,4},{4,5},{5,6},{6,7},{7,8},{8,9},{9,10... | collective-permute-start | bytes 786440 | tf_op jit(solution)/shard_map/ppermute | solution.py:33
  52.0 3.9 %collective-permute-start.1 = (bf16[512,128]{1,0:T(8,128)(2,1)S(1)}, bf16[512,128]{1,0:T(8,128)(2,1)S(1)}, u32[]{:S(2)}, u32[]{:S(2)}) collective-permute-start(bf16[512,128]{1,0:T(8,128)(2,1)S(1)} %get-tuple-element.12), channel_id=1, source_target_pairs={{2,0},{3,1},{4,2},{5,3},{6,4},{7,5},{8,6},{9,7},{10,8},{11,9},{12,... | collective-permute-start | bytes 393224 | tf_op jit(solution)/shard_map/ppermute | solution.py:33
  56.0 2.2 %collective-permute-start.2 = (bf16[512,128]{1,0:T(8,128)(2,1)S(1)}, bf16[512,128]{1,0:T(8,128)(2,1)S(1)}, u32[]{:S(2)}, u32[]{:S(2)}) collective-permute-start(bf16[512,128]{1,0:T(8,128)(2,1)S(1)} %get-tuple-element.13), channel_id=1, source_target_pairs={{14,0},{15,1},{0,2},{1,3},{2,4},{3,5},{4,6},{5,7},{6,8},{7,9},{8,1... | collective-permute-start | bytes 393224 | tf_op jit(solution)/shard_map/ppermute | solution.py:33
  58.3 0.2 slice_reduce_fusion
  58.4 1.3 collective-permute-done.1
  59.7 4.2 %collective-permute-done.2 = bf16[512,128]{1,0:T(8,128)(2,1)S(1)} collective-permute-done((bf16[512,128]{1,0:T(8,128)(2,1)S(1)}, bf16[512,128]{1,0:T(8,128)(2,1)S(1)}, u32[]{:S(2)}, u32[]{:S(2)}) %collective-permute-start.2) | collective-permute-done | bytes 131104 | tf_op jit(solution)/shard_map/ppermute | solution.py:33
  64.0 3.3 %attend.1 = bf16[4,256,128]{2,1,0:T(8,128)(2,1)S(1)} custom-call(s32[16]{0:T(128)S(1)} %compare_select_fusion.3.group_ref, bf16[4,784,128]{2,1,0:T(8,128)(2,1)S(1)} %bitcast.32, f32[4,1,512]{2,1,0:T(1,128)S(1)} %bitcast.40, bf16[1024,128]{1,0:T(8,128)(2,1)S(1)} %bitcast.36, bf16[1024,128]{1,0:T(8,128)(2,1)S(1)} %collective-permute-done.refs_1_, ...), custom_call_target="tpu_custom_call" | custom-call | flops 1000 | bytes 1000 | tf_op jit(solution)/shard_map/attend/pallas_call | solution.py:92
  67.3 8.0 %all_to_all.25 = bf16[4,256,128]{2,1,0:T(8,128)(2,1)S(1)} all-to-all(bf16[4,256,128]{2,1,0:T(8,128)(2,1)S(1)} %attend.1), channel_id=1, replica_groups=mesh['x'=4,'c'=2,'y'=4,'q'=4,'r'=4] {'y'}, dimensions={0} | all-to-all | bytes 524288 | tf_op jit(solution)/shard_map/all_to_all | solution.py:308
  75.3 20.6 %all-gather = bf16[2048,128]{1,0:T(8,128)(2,1)S(1)} all-gather(bf16[256,128]{1,0:T(8,128)(2,1)S(1)} %reduce_sum.32), channel_id=2, replica_groups=mesh['x'=4,'c'=2,'y'=4,'q'=4,'r'=4] {'x','c'}, dimensions={0}, use_global_device_ids=true | all-gather | bytes 589824 | tf_op jit(solution)/shard_map/all_gather | solution.py:310
  95.9 5.9 %dense.1 = (bf16[256,1024]{1,0:T(8,128)(2,1)S(1)}, bf16[8,32,1024]{2,1,0:T(8,128)(2,1)}) custom-call(bf16[8,256,128]{2,1,0:T(8,128)(2,1)S(1)} %bitcast.37, bf16[256,1024]{1,0:T(8,128)(2,1)} %bitcast.44, f32[1,1024]{1,0:T(1,128)S(1)} %bitcast.42, bf16[1024,1024]{1,0:T(8,128)(2,1)} %all-gather.4.cloned.1.call-done.refs_0_, bf16[1024,512]{1,0:T(8,128)(2,1)} %refs_1_.1, ...), custom_call_target="tpu_custom_call" | custom-call | flops 1000 | bytes 1000 | tf_op jit(solution)/shard_map/dense/pallas_call | solution.py:221
  101.8 3.8 %all-to-all-start.2 = ((bf16[8,32,1024]{2,1,0:T(8,128)(2,1)}), bf16[8,32,1024]{2,1,0:T(8,128)(2,1)S(1)}, u32[]{:S(2)}, u32[]{:S(2)}) async-start(bf16[8,32,1024]{2,1,0:T(8,128)(2,1)} %get-tuple-element.10), calls=%async_computation.2 | async-start | bytes 1048576 | tf_op jit(solution)/shard_map/all_to_all | solution.py:312
  106.0 0.1 eq.76
  106.0 9.1 %all-to-all-done.2.terms_ref = bf16[8,32,1024]{2,1,0:T(8,128)(2,1)S(1)} async-done(((bf16[8,32,1024]{2,1,0:T(8,128)(2,1)}), bf16[8,32,1024]{2,1,0:T(8,128)(2,1)S(1)}, u32[]{:S(2)}, u32[]{:S(2)}) %all-to-all-start.2) | async-done | bytes 524320 | tf_op jit(solution)/shard_map/all_to_all | solution.py:312
  115.1 1.2 embed.1
  116.3 4.4 %all-to-all-start.3 = ((bf16[32,32,128]{2,1,0:T(8,128)(2,1)}), bf16[32,32,128]{2,1,0:T(8,128)(2,1)S(1)}, u32[]{:S(2)}, u32[]{:S(2)}) async-start(bf16[32,32,128]{2,1,0:T(8,128)(2,1)} %embed.1), calls=%async_computation.3 | async-start | bytes 524288 | tf_op jit(solution)/shard_map/all_to_all | solution.py:317
  120.7 0.1 fusion.3
  120.9 1.3 slice.38
  122.2 0.8 slice.37
  123.0 0.1 copy.44
  123.1 0.1 reshape.134
  123.2 0.1 copy.45
  123.3 0.1 reduce_window_sum.14.last_ref
  123.4 6.3 %all-to-all-done.3 = bf16[32,32,128]{2,1,0:T(8,128)(2,1)S(1)} async-done(((bf16[32,32,128]{2,1,0:T(8,128)(2,1)}), bf16[32,32,128]{2,1,0:T(8,128)(2,1)S(1)}, u32[]{:S(2)}, u32[]{:S(2)}) %all-to-all-start.3) | async-done | bytes 262176 | tf_op jit(solution)/shard_map/all_to_all | solution.py:317
  129.6 2.5 %match.1 = f32[32,16,128]{2,1,0:T(8,128)} custom-call(s32[64]{0:T(128)S(1)} %convert_element_type.45.need_ref, s32[64]{0:T(128)S(1)} %sub.16.first_ref, s32[64]{0:T(128)S(1)} %reduce_window_sum.14.last_ref, bf16[1024,128]{1,0:T(8,128)(2,1)S(1)} %bitcast.38, bf16[4096,128]{1,0:T(8,128)(2,1)S(1)} %bitcast.30, s32[16,128]{1,0:T(8,128)S(1)} %pad.14.pick_ref), custom_call_target="tpu_custom_call" | custom-call | flops 1000 | bytes 1000 | tf_op jit(solution)/shard_map/match/pallas_call | solution.py:157
  132.1 4.5 %all-to-all-start.4 = ((f32[32,16,128]{2,1,0:T(8,128)}), f32[32,16,128]{2,1,0:T(8,128)S(1)}, u32[]{:S(2)}, u32[]{:S(2)}) async-start(f32[32,16,128]{2,1,0:T(8,128)} %match.1), calls=%async_computation.4 | async-start | bytes 524288 | tf_op jit(solution)/shard_map/all_to_all | solution.py:333
  136.6 0.6 constant_dynamic-slice_fusion
  137.3 8.2 %all-to-all-done.4.terms_ref = f32[32,16,128]{2,1,0:T(8,128)S(1)} async-done(((f32[32,16,128]{2,1,0:T(8,128)}), f32[32,16,128]{2,1,0:T(8,128)S(1)}, u32[]{:S(2)}, u32[]{:S(2)}) %all-to-all-start.4) | async-done | bytes 262176 | tf_op jit(solution)/shard_map/all_to_all | solution.py:333
  145.4 0.7 total.1
  (54 shorter events, 0.9 us)
Async XLA Ops:
  7.2 21.3 %copy-start = (bf16[1024,128]{1,0:T(8,128)(2,1)S(1)}, bf16[1024,128]{1,0:T(8,128)(2,1)}, u32[]{:S(2)}) copy-start(bf16[1024,128]{1,0:T(8,128)(2,1)} %param.21) | copy-start | bytes 786436
  7.2 22.6 %copy-start.4 = (bf16[4,64,1024]{2,1,0:T(8,128)(2,1)S(1)}, bf16[4,64,1024]{2,1,0:T(8,128)(2,1)}, u32[]{:S(2)}) copy-start(bf16[4,64,1024]{2,1,0:T(8,128)(2,1)} %param.18) | copy-start | bytes 1572868
  7.2 22.6 %copy-start.5 = (bf16[1024,128]{1,0:T(8,128)(2,1)S(1)}, bf16[1024,128]{1,0:T(8,128)(2,1)}, u32[]{:S(2)}) copy-start(bf16[1024,128]{1,0:T(8,128)(2,1)} %param.20) | copy-start | bytes 786436
  7.2 22.9 %copy-start.6 = (bf16[1024,128]{1,0:T(8,128)(2,1)S(1)}, bf16[1024,128]{1,0:T(8,128)(2,1)}, u32[]{:S(2)}) copy-start(bf16[1024,128]{1,0:T(8,128)(2,1)} %param.19) | copy-start | bytes 786436
  7.2 23.2 %copy-start.7 = (s32[4,16]{1,0:T(4,128)S(1)}, s32[4,16]{1,0:T(4,128)}, u32[]{:S(2)}) copy-start(s32[4,16]{1,0:T(4,128)} %param.35) | copy-start | bytes 772
  7.2 23.2 %copy-start.8 = (s32[4]{0:T(128)S(1)}, s32[4]{0:T(128)}, u32[]{:S(2)}) copy-start(s32[4]{0:T(128)} %param.32) | copy-start | bytes 52
  7.2 23.7 %copy-start.9 = (s32[16]{0:T(128)S(1)}, s32[16]{0:T(128)}, u32[]{:S(2)}) copy-start(s32[16]{0:T(128)} %param.31) | copy-start | bytes 196
  7.2 88.6 %all-gather.4.cloned.1.call-start = ((), (), s32[]{:S(2)}) async-start(), calls=%async_computation.5 | async-start | bytes 2359296 | tf_op jit(solution)/shard_map/all_gather | solution.py:273
  9.5 34.7 %all-to-all-start = ((bf16[4,256,128]{2,1,0:T(8,128)(2,1)}), bf16[4,256,128]{2,1,0:T(8,128)(2,1)S(1)}, u32[]{:S(2)}, u32[]{:S(2)}) async-start(bf16[4,256,128]{2,1,0:T(8,128)(2,1)} %broadcast_in_dim.65), calls=%async_computation | async-start | bytes 524288 | tf_op jit(solution)/shard_map/all_to_all | solution.py:29
  25.1 95.8 %all-gather.6.cloned.1.call-start = ((), (), s32[]{:S(2)}) async-start(), calls=%async_computation.6 | async-start | bytes 1183744 | tf_op jit(solution)/shard_map/all_gather | solution.py:276
  44.2 19.7 %collective-permute-start = (bf16[1024,128]{1,0:T(8,128)(2,1)S(1)}, bf16[1024,128]{1,0:T(8,128)(2,1)S(1)}, u32[]{:S(2)}, u32[]{:S(2)}) collective-permute-start(bf16[1024,128]{1,0:T(8,128)(2,1)S(1)} %bitcast.33), channel_id=1, source_target_pairs={{1,0},{2,1},{3,2},{4,3},{5,4},{6,5},{7,6},{8,7},{9,8},{10,9},{11,1... | collective-permute-start | bytes 786440 | tf_op jit(solution)/shard_map/ppermute | solution.py:33
  50.1 13.9 %collective-permute-start.3 = (bf16[1024,128]{1,0:T(8,128)(2,1)S(1)}, bf16[1024,128]{1,0:T(8,128)(2,1)S(1)}, u32[]{:S(2)}, u32[]{:S(2)}) collective-permute-start(bf16[1024,128]{1,0:T(8,128)(2,1)S(1)} %bitcast.34), channel_id=1, source_target_pairs={{15,0},{0,1},{1,2},{2,3},{3,4},{4,5},{5,6},{6,7},{7,8},{8,9},{9,10... | collective-permute-start | bytes 786440 | tf_op jit(solution)/shard_map/ppermute | solution.py:33
  52.0 43.8 %copy-start.3 = (f32[1024]{0:T(1024)S(1)}, f32[1024]{0:T(1024)}, u32[]{:S(2)}) copy-start(f32[1024]{0:T(1024)} %param.23) | copy-start | bytes 12292
  52.0 7.7 %collective-permute-start.1 = (bf16[512,128]{1,0:T(8,128)(2,1)S(1)}, bf16[512,128]{1,0:T(8,128)(2,1)S(1)}, u32[]{:S(2)}, u32[]{:S(2)}) collective-permute-start(bf16[512,128]{1,0:T(8,128)(2,1)S(1)} %get-tuple-element.12), channel_id=1, source_target_pairs={{2,0},{3,1},{4,2},{5,3},{6,4},{7,5},{8,6},{9,7},{10,8},{11,9},{12,... | collective-permute-start | bytes 393224 | tf_op jit(solution)/shard_map/ppermute | solution.py:33
  56.0 8.0 %collective-permute-start.2 = (bf16[512,128]{1,0:T(8,128)(2,1)S(1)}, bf16[512,128]{1,0:T(8,128)(2,1)S(1)}, u32[]{:S(2)}, u32[]{:S(2)}) collective-permute-start(bf16[512,128]{1,0:T(8,128)(2,1)S(1)} %get-tuple-element.13), channel_id=1, source_target_pairs={{14,0},{15,1},{0,2},{1,3},{2,4},{3,5},{4,6},{5,7},{6,8},{7,9},{8,1... | collective-permute-start | bytes 393224 | tf_op jit(solution)/shard_map/ppermute | solution.py:33
  95.9 19.3 %copy-start.1 = (bf16[1024,128]{1,0:T(8,128)(2,1)S(1)}, bf16[1024,128]{1,0:T(8,128)(2,1)}, u32[]{:S(2)}) copy-start(bf16[1024,128]{1,0:T(8,128)(2,1)} %w_project_ref.1) | copy-start | bytes 786436
  95.9 19.3 %copy-start.2 = (f32[1024]{0:T(1024)S(1)}, f32[1024]{0:T(1024)}, u32[]{:S(2)}) copy-start(f32[1024]{0:T(1024)} %param.26) | copy-start | bytes 12292
  101.8 13.3 %all-to-all-start.2 = ((bf16[8,32,1024]{2,1,0:T(8,128)(2,1)}), bf16[8,32,1024]{2,1,0:T(8,128)(2,1)S(1)}, u32[]{:S(2)}, u32[]{:S(2)}) async-start(bf16[8,32,1024]{2,1,0:T(8,128)(2,1)} %get-tuple-element.10), calls=%async_computation.2 | async-start | bytes 1048576 | tf_op jit(solution)/shard_map/all_to_all | solution.py:312
  116.3 13.3 %all-to-all-start.3 = ((bf16[32,32,128]{2,1,0:T(8,128)(2,1)}), bf16[32,32,128]{2,1,0:T(8,128)(2,1)S(1)}, u32[]{:S(2)}, u32[]{:S(2)}) async-start(bf16[32,32,128]{2,1,0:T(8,128)(2,1)} %embed.1), calls=%async_computation.3 | async-start | bytes 524288 | tf_op jit(solution)/shard_map/all_to_all | solution.py:317
  132.1 13.3 %all-to-all-start.4 = ((f32[32,16,128]{2,1,0:T(8,128)}), f32[32,16,128]{2,1,0:T(8,128)S(1)}, u32[]{:S(2)}, u32[]{:S(2)}) async-start(f32[32,16,128]{2,1,0:T(8,128)} %match.1), calls=%async_computation.4 | async-start | bytes 524288 | tf_op jit(solution)/shard_map/all_to_all | solution.py:333
Sparse Core Ops, SparseCore 0:
  10.2 38.5 all-gather.3
  50.9 61.9 all-gather.5

commit v8 on v7

--- a/solution.py
+++ b/solution.py
@@ -201,12 +201,9 @@
     for copy in copies:
         copy.start()
     w_out_ref, inner_ref, outer_ref = scratch
-    attn = token_ref[...].astype(F32)
+    context = jnp.concatenate([context_ref[h] for h in range(8)], axis=1)
     copies[0].wait()
-    for h in range(8):
-        attn = attn + jnp.dot(
-            context_ref[h], w_out_ref[h * 128 : (h + 1) * 128, :], preferred_element_type=F32
-        )
+    attn = token_ref[...].astype(F32) + jnp.dot(context, w_out_ref[...], preferred_element_type=F32)
     first = layer_norm(attn, gain_ref[...]).astype(BF)
     first_ref[...] = first
     copies[1].wait()

time: 154 us -> 154 us (level)
  transfers between devices with their start and end apart: 10 -> 10, of which waited for: 5 -> 5; matrix products, arithmetic and copies ran while one was open for 7% -> 7% of each run, Pallas kernels for 7% -> 6%
where the time goes in v8:
time: 154 us; the launch traced here: 152 us
  starting transfers between devices  42.5 us (28%)
  blocking collectives  41.6 us (27%)
  waiting for transfers between devices  29.8 us (19%)
  between operations  14.4 us (9%)
  Pallas kernels  12.6 us (8%)
  local copies, waits for them, and re-layouts  5.67 us (4%)
  other arithmetic  3.76 us (2%)
  matrix products  1.91 us (1%)
    all_gather x1, blocking collectives, per_device(): context = lax.all_gather(context, HEAD, axis=0, tiled=False)  20.6 us
    all_to_all x1, starting transfers between devices, spread(): lax.all_to_all(wide, axes, 0, 0, tiled=True)  15.6 us
    ppermute x4, starting transfers between devices, from_ahead(): lax.ppermute(block, ('q', 'r'), [((i + step) % 16, i) for i in range(16)])  13.9 us
    all_gather x1, blocking collectives, per_device(): rows = lax.all_gather(rows, 'y', axis=0, tiled=True)  13.1 us
    all_to_all x1, waiting for transfers between devices, per_device(): terms = lax.all_to_all(terms, HEAD, 0, 0, tiled=True)  9.11 us
    all_to_all x1, waiting for transfers between devices, per_device(): terms = lax.all_to_all(terms, HEAD + ('y',), 0, 0, tiled=True)  8.19 us
    all_to_all x1, blocking collectives, per_device(): back = lax.all_to_all(mixed, 'y', 0, 0, tiled=True)  7.97 us
    all_to_all x1, waiting for transfers between devices, per_device(): queries = lax.all_to_all(embed, HEAD + ('y',), 0, 0, tiled=True)  6.25 us
  transfers between devices with their start and end apart: 10, of which 5 were waited for; matrix products, arithmetic and copies ran while one was open for 7% of the time, Pallas kernels for 6%

profile of v8, /device:TPU:1, one launch (start us, length us, event | category | flops | bytes accessed | tf_op | source)
XLA Modules:
  0.0 152.2 jit_solution(2127816134495793375)
XLA Ops:
  7.3 0.7 all-gather.4.cloned.1.call-update
  8.0 0.8 pad_maximum_fusion.2
  8.8 0.8 broadcast_in_dim.65
  9.5 15.6 %all-to-all-start = ((bf16[4,256,128]{2,1,0:T(8,128)(2,1)}), bf16[4,256,128]{2,1,0:T(8,128)(2,1)S(1)}, u32[]{:S(2)}, u32[]{:S(2)}) async-start(bf16[4,256,128]{2,1,0:T(8,128)(2,1)} %broadcast_in_dim.65), calls=%async_computation | async-start | bytes 524288 | tf_op jit(solution)/shard_map/all_to_all | solution.py:29
  25.1 0.7 convert_element_type.46
  25.8 1.5 fusion.2
  27.3 0.7 dynamic_slice.9
  28.0 0.1 eq.70
  28.1 0.2 select_reduce_fusion.1
  28.5 1.3 convolution_convert_fusion
  29.8 0.3 convolution_convert_fusion.1
  30.1 0.3 fusion
  30.5 0.1 copy.39
  30.6 0.1 fusion.13
  30.7 0.1 add.102
  30.8 0.1 add.104
  30.9 0.1 dynamic_slice.10
  31.1 0.1 select_reduce_fusion
  31.2 13.1 %all_gather.15 = bf16[3136,128]{1,0:T(8,128)(2,1)S(1)} all-gather(bf16[784,128]{1,0:T(8,128)(2,1)S(1)} %pad_maximum_fusion.1), channel_id=1, replica_groups=mesh['x'=4,'c'=2,'y'=4,'q'=4,'r'=4] {'y'}, dimensions={0}, use_global_device_ids=true | all-gather | bytes 1003520 | tf_op jit(solution)/shard_map/all_gather | solution.py:281
  44.2 5.8 %collective-permute-start = (bf16[1024,128]{1,0:T(8,128)(2,1)S(1)}, bf16[1024,128]{1,0:T(8,128)(2,1)S(1)}, u32[]{:S(2)}, u32[]{:S(2)}) collective-permute-start(bf16[1024,128]{1,0:T(8,128)(2,1)S(1)} %bitcast.33), channel_id=1, source_target_pairs={{1,0},{2,1},{3,2},{4,3},{5,4},{6,5},{7,6},{8,7},{9,8},{10,9},{11,1... | collective-permute-start | bytes 786440 | tf_op jit(solution)/shard_map/ppermute | solution.py:33
  50.1 1.9 %collective-permute-start.3 = (bf16[1024,128]{1,0:T(8,128)(2,1)S(1)}, bf16[1024,128]{1,0:T(8,128)(2,1)S(1)}, u32[]{:S(2)}, u32[]{:S(2)}) collective-permute-start(bf16[1024,128]{1,0:T(8,128)(2,1)S(1)} %bitcast.34), channel_id=1, source_target_pairs={{15,0},{0,1},{1,2},{2,3},{3,4},{4,5},{5,6},{6,7},{7,8},{8,9},{9,10... | collective-permute-start | bytes 786440 | tf_op jit(solution)/shard_map/ppermute | solution.py:33
  52.0 3.9 %collective-permute-start.1 = (bf16[512,128]{1,0:T(8,128)(2,1)S(1)}, bf16[512,128]{1,0:T(8,128)(2,1)S(1)}, u32[]{:S(2)}, u32[]{:S(2)}) collective-permute-start(bf16[512,128]{1,0:T(8,128)(2,1)S(1)} %get-tuple-element.12), channel_id=1, source_target_pairs={{2,0},{3,1},{4,2},{5,3},{6,4},{7,5},{8,6},{9,7},{10,8},{11,9},{12,... | collective-permute-start | bytes 393224 | tf_op jit(solution)/shard_map/ppermute | solution.py:33
  56.0 2.2 %collective-permute-start.2 = (bf16[512,128]{1,0:T(8,128)(2,1)S(1)}, bf16[512,128]{1,0:T(8,128)(2,1)S(1)}, u32[]{:S(2)}, u32[]{:S(2)}) collective-permute-start(bf16[512,128]{1,0:T(8,128)(2,1)S(1)} %get-tuple-element.13), channel_id=1, source_target_pairs={{14,0},{15,1},{0,2},{1,3},{2,4},{3,5},{4,6},{5,7},{6,8},{7,9},{8,1... | collective-permute-start | bytes 393224 | tf_op jit(solution)/shard_map/ppermute | solution.py:33
  58.3 0.2 slice_reduce_fusion
  58.4 1.3 collective-permute-done.1
  59.7 4.2 %collective-permute-done.2 = bf16[512,128]{1,0:T(8,128)(2,1)S(1)} collective-permute-done((bf16[512,128]{1,0:T(8,128)(2,1)S(1)}, bf16[512,128]{1,0:T(8,128)(2,1)S(1)}, u32[]{:S(2)}, u32[]{:S(2)}) %collective-permute-start.2) | collective-permute-done | bytes 131104 | tf_op jit(solution)/shard_map/ppermute | solution.py:33
  64.0 3.3 %attend.1 = bf16[4,256,128]{2,1,0:T(8,128)(2,1)S(1)} custom-call(s32[16]{0:T(128)S(1)} %compare_select_fusion.3.group_ref, bf16[4,784,128]{2,1,0:T(8,128)(2,1)S(1)} %bitcast.32, f32[4,1,512]{2,1,0:T(1,128)S(1)} %bitcast.40, bf16[1024,128]{1,0:T(8,128)(2,1)S(1)} %bitcast.36, bf16[1024,128]{1,0:T(8,128)(2,1)S(1)} %collective-permute-done.refs_1_, ...), custom_call_target="tpu_custom_call" | custom-call | flops 1000 | bytes 1000 | tf_op jit(solution)/shard_map/attend/pallas_call | solution.py:92
  67.3 8.0 %all_to_all.25 = bf16[4,256,128]{2,1,0:T(8,128)(2,1)S(1)} all-to-all(bf16[4,256,128]{2,1,0:T(8,128)(2,1)S(1)} %attend.1), channel_id=1, replica_groups=mesh['x'=4,'c'=2,'y'=4,'q'=4,'r'=4] {'y'}, dimensions={0} | all-to-all | bytes 524288 | tf_op jit(solution)/shard_map/all_to_all | solution.py:305
  75.3 20.6 %all-gather = bf16[2048,128]{1,0:T(8,128)(2,1)S(1)} all-gather(bf16[256,128]{1,0:T(8,128)(2,1)S(1)} %reduce_sum.32), channel_id=2, replica_groups=mesh['x'=4,'c'=2,'y'=4,'q'=4,'r'=4] {'x','c'}, dimensions={0}, use_global_device_ids=true | all-gather | bytes 589824 | tf_op jit(solution)/shard_map/all_gather | solution.py:307
  95.9 5.4 %dense.1 = (bf16[256,1024]{1,0:T(8,128)(2,1)S(1)}, bf16[8,32,1024]{2,1,0:T(8,128)(2,1)}) custom-call(bf16[8,256,128]{2,1,0:T(8,128)(2,1)S(1)} %bitcast.37, bf16[256,1024]{1,0:T(8,128)(2,1)} %bitcast.44, f32[1,1024]{1,0:T(1,128)S(1)} %bitcast.42, bf16[1024,1024]{1,0:T(8,128)(2,1)} %all-gather.4.cloned.1.call-done.refs_0_, bf16[1024,512]{1,0:T(8,128)(2,1)} %refs_1_.1, ...), custom_call_target="tpu_custom_call" | custom-call | flops 1000 | bytes 1000 | tf_op jit(solution)/shard_map/dense/pallas_call | solution.py:218
  101.3 3.9 %all-to-all-start.2 = ((bf16[8,32,1024]{2,1,0:T(8,128)(2,1)}), bf16[8,32,1024]{2,1,0:T(8,128)(2,1)S(1)}, u32[]{:S(2)}, u32[]{:S(2)}) async-start(bf16[8,32,1024]{2,1,0:T(8,128)(2,1)} %get-tuple-element.10), calls=%async_computation.2 | async-start | bytes 1048576 | tf_op jit(solution)/shard_map/all_to_all | solution.py:309
  105.4 0.1 eq.76
  105.5 9.1 %all-to-all-done.2.terms_ref = bf16[8,32,1024]{2,1,0:T(8,128)(2,1)S(1)} async-done(((bf16[8,32,1024]{2,1,0:T(8,128)(2,1)}), bf16[8,32,1024]{2,1,0:T(8,128)(2,1)S(1)}, u32[]{:S(2)}, u32[]{:S(2)}) %all-to-all-start.2) | async-done | bytes 524320 | tf_op jit(solution)/shard_map/all_to_all | solution.py:309
  114.6 1.2 embed.1
  115.8 4.4 %all-to-all-start.3 = ((bf16[32,32,128]{2,1,0:T(8,128)(2,1)}), bf16[32,32,128]{2,1,0:T(8,128)(2,1)S(1)}, u32[]{:S(2)}, u32[]{:S(2)}) async-start(bf16[32,32,128]{2,1,0:T(8,128)(2,1)} %embed.1), calls=%async_computation.3 | async-start | bytes 524288 | tf_op jit(solution)/shard_map/all_to_all | solution.py:314
  120.2 0.1 fusion.3
  120.4 1.3 slice.38
  121.7 0.8 slice.37
  122.5 0.1 copy.44
  122.6 0.1 reshape.134
  122.7 0.1 copy.45
  122.8 0.1 reduce_window_sum.14.last_ref
  122.9 6.3 %all-to-all-done.3 = bf16[32,32,128]{2,1,0:T(8,128)(2,1)S(1)} async-done(((bf16[32,32,128]{2,1,0:T(8,128)(2,1)}), bf16[32,32,128]{2,1,0:T(8,128)(2,1)S(1)}, u32[]{:S(2)}, u32[]{:S(2)}) %all-to-all-start.3) | async-done | bytes 262176 | tf_op jit(solution)/shard_map/all_to_all | solution.py:314
  129.1 2.0 %match.1 = f32[32,16,128]{2,1,0:T(8,128)} custom-call(s32[64]{0:T(128)S(1)} %convert_element_type.45.need_ref, s32[64]{0:T(128)S(1)} %sub.16.first_ref, s32[64]{0:T(128)S(1)} %reduce_window_sum.14.last_ref, bf16[1024,128]{1,0:T(8,128)(2,1)S(1)} %bitcast.38, bf16[4096,128]{1,0:T(8,128)(2,1)S(1)} %bitcast.30, s32[16,128]{1,0:T(8,128)S(1)} %pad.14.pick_ref), custom_call_target="tpu_custom_call" | custom-call | flops 1000 | bytes 1000 | tf_op jit(solution)/shard_map/match/pallas_call | solution.py:157
  131.1 4.6 %all-to-all-start.4 = ((f32[32,16,128]{2,1,0:T(8,128)}), f32[32,16,128]{2,1,0:T(8,128)S(1)}, u32[]{:S(2)}, u32[]{:S(2)}) async-start(f32[32,16,128]{2,1,0:T(8,128)} %match.1), calls=%async_computation.4 | async-start | bytes 524288 | tf_op jit(solution)/shard_map/all_to_all | solution.py:330
  135.8 0.6 constant_dynamic-slice_fusion
  136.4 8.2 %all-to-all-done.4.terms_ref = f32[32,16,128]{2,1,0:T(8,128)S(1)} async-done(((f32[32,16,128]{2,1,0:T(8,128)}), f32[32,16,128]{2,1,0:T(8,128)S(1)}, u32[]{:S(2)}, u32[]{:S(2)}) %all-to-all-start.4) | async-done | bytes 262176 | tf_op jit(solution)/shard_map/all_to_all | solution.py:330
  144.6 0.7 total.1
  (54 shorter events, 0.9 us)
Async XLA Ops:
  7.2 21.3 %copy-start = (bf16[1024,128]{1,0:T(8,128)(2,1)S(1)}, bf16[1024,128]{1,0:T(8,128)(2,1)}, u32[]{:S(2)}) copy-start(bf16[1024,128]{1,0:T(8,128)(2,1)} %param.21) | copy-start | bytes 786436
  7.2 22.6 %copy-start.4 = (bf16[4,64,1024]{2,1,0:T(8,128)(2,1)S(1)}, bf16[4,64,1024]{2,1,0:T(8,128)(2,1)}, u32[]{:S(2)}) copy-start(bf16[4,64,1024]{2,1,0:T(8,128)(2,1)} %param.18) | copy-start | bytes 1572868
  7.2 22.6 %copy-start.5 = (bf16[1024,128]{1,0:T(8,128)(2,1)S(1)}, bf16[1024,128]{1,0:T(8,128)(2,1)}, u32[]{:S(2)}) copy-start(bf16[1024,128]{1,0:T(8,128)(2,1)} %param.20) | copy-start | bytes 786436
  7.2 22.9 %copy-start.6 = (bf16[1024,128]{1,0:T(8,128)(2,1)S(1)}, bf16[1024,128]{1,0:T(8,128)(2,1)}, u32[]{:S(2)}) copy-start(bf16[1024,128]{1,0:T(8,128)(2,1)} %param.19) | copy-start | bytes 786436
  7.2 23.2 %copy-start.7 = (s32[4,16]{1,0:T(4,128)S(1)}, s32[4,16]{1,0:T(4,128)}, u32[]{:S(2)}) copy-start(s32[4,16]{1,0:T(4,128)} %param.35) | copy-start | bytes 772
  7.2 23.2 %copy-start.8 = (s32[4]{0:T(128)S(1)}, s32[4]{0:T(128)}, u32[]{:S(2)}) copy-start(s32[4]{0:T(128)} %param.32) | copy-start | bytes 52
  7.2 23.7 %copy-start.9 = (s32[16]{0:T(128)S(1)}, s32[16]{0:T(128)}, u32[]{:S(2)}) copy-start(s32[16]{0:T(128)} %param.31) | copy-start | bytes 196
  7.2 88.6 %all-gather.4.cloned.1.call-start = ((), (), s32[]{:S(2)}) async-start(), calls=%async_computation.5 | async-start | bytes 2359296 | tf_op jit(solution)/shard_map/all_gather | solution.py:270
  9.5 34.7 %all-to-all-start = ((bf16[4,256,128]{2,1,0:T(8,128)(2,1)}), bf16[4,256,128]{2,1,0:T(8,128)(2,1)S(1)}, u32[]{:S(2)}, u32[]{:S(2)}) async-start(bf16[4,256,128]{2,1,0:T(8,128)(2,1)} %broadcast_in_dim.65), calls=%async_computation | async-start | bytes 524288 | tf_op jit(solution)/shard_map/all_to_all | solution.py:29
  25.1 95.2 %all-gather.6.cloned.1.call-start = ((), (), s32[]{:S(2)}) async-start(), calls=%async_computation.6 | async-start | bytes 1183744 | tf_op jit(solution)/shard_map/all_gather | solution.py:273
  44.2 19.7 %collective-permute-start = (bf16[1024,128]{1,0:T(8,128)(2,1)S(1)}, bf16[1024,128]{1,0:T(8,128)(2,1)S(1)}, u32[]{:S(2)}, u32[]{:S(2)}) collective-permute-start(bf16[1024,128]{1,0:T(8,128)(2,1)S(1)} %bitcast.33), channel_id=1, source_target_pairs={{1,0},{2,1},{3,2},{4,3},{5,4},{6,5},{7,6},{8,7},{9,8},{10,9},{11,1... | collective-permute-start | bytes 786440 | tf_op jit(solution)/shard_map/ppermute | solution.py:33
  50.1 13.9 %collective-permute-start.3 = (bf16[1024,128]{1,0:T(8,128)(2,1)S(1)}, bf16[1024,128]{1,0:T(8,128)(2,1)S(1)}, u32[]{:S(2)}, u32[]{:S(2)}) collective-permute-start(bf16[1024,128]{1,0:T(8,128)(2,1)S(1)} %bitcast.34), channel_id=1, source_target_pairs={{15,0},{0,1},{1,2},{2,3},{3,4},{4,5},{5,6},{6,7},{7,8},{8,9},{9,10... | collective-permute-start | bytes 786440 | tf_op jit(solution)/shard_map/ppermute | solution.py:33
  52.0 43.8 %copy-start.3 = (f32[1024]{0:T(1024)S(1)}, f32[1024]{0:T(1024)}, u32[]{:S(2)}) copy-start(f32[1024]{0:T(1024)} %param.23) | copy-start | bytes 12292
  52.0 7.7 %collective-permute-start.1 = (bf16[512,128]{1,0:T(8,128)(2,1)S(1)}, bf16[512,128]{1,0:T(8,128)(2,1)S(1)}, u32[]{:S(2)}, u32[]{:S(2)}) collective-permute-start(bf16[512,128]{1,0:T(8,128)(2,1)S(1)} %get-tuple-element.12), channel_id=1, source_target_pairs={{2,0},{3,1},{4,2},{5,3},{6,4},{7,5},{8,6},{9,7},{10,8},{11,9},{12,... | collective-permute-start | bytes 393224 | tf_op jit(solution)/shard_map/ppermute | solution.py:33
  56.0 8.0 %collective-permute-start.2 = (bf16[512,128]{1,0:T(8,128)(2,1)S(1)}, bf16[512,128]{1,0:T(8,128)(2,1)S(1)}, u32[]{:S(2)}, u32[]{:S(2)}) collective-permute-start(bf16[512,128]{1,0:T(8,128)(2,1)S(1)} %get-tuple-element.13), channel_id=1, source_target_pairs={{14,0},{15,1},{0,2},{1,3},{2,4},{3,5},{4,6},{5,7},{6,8},{7,9},{8,1... | collective-permute-start | bytes 393224 | tf_op jit(solution)/shard_map/ppermute | solution.py:33
  95.9 18.8 %copy-start.1 = (bf16[1024,128]{1,0:T(8,128)(2,1)S(1)}, bf16[1024,128]{1,0:T(8,128)(2,1)}, u32[]{:S(2)}) copy-start(bf16[1024,128]{1,0:T(8,128)(2,1)} %w_project_ref.1) | copy-start | bytes 786436
  95.9 18.8 %copy-start.2 = (f32[1024]{0:T(1024)S(1)}, f32[1024]{0:T(1024)}, u32[]{:S(2)}) copy-start(f32[1024]{0:T(1024)} %param.26) | copy-start | bytes 12292
  101.3 13.3 %all-to-all-start.2 = ((bf16[8,32,1024]{2,1,0:T(8,128)(2,1)}), bf16[8,32,1024]{2,1,0:T(8,128)(2,1)S(1)}, u32[]{:S(2)}, u32[]{:S(2)}) async-start(bf16[8,32,1024]{2,1,0:T(8,128)(2,1)} %get-tuple-element.10), calls=%async_computation.2 | async-start | bytes 1048576 | tf_op jit(solution)/shard_map/all_to_all | solution.py:309
  115.8 13.3 %all-to-all-start.3 = ((bf16[32,32,128]{2,1,0:T(8,128)(2,1)}), bf16[32,32,128]{2,1,0:T(8,128)(2,1)S(1)}, u32[]{:S(2)}, u32[]{:S(2)}) async-start(bf16[32,32,128]{2,1,0:T(8,128)(2,1)} %embed.1), calls=%async_computation.3 | async-start | bytes 524288 | tf_op jit(solution)/shard_map/all_to_all | solution.py:314
  131.1 13.5 %all-to-all-start.4 = ((f32[32,16,128]{2,1,0:T(8,128)}), f32[32,16,128]{2,1,0:T(8,128)S(1)}, u32[]{:S(2)}, u32[]{:S(2)}) async-start(f32[32,16,128]{2,1,0:T(8,128)} %match.1), calls=%async_computation.4 | async-start | bytes 524288 | tf_op jit(solution)/shard_map/all_to_all | solution.py:330
Sparse Core Ops, SparseCore 0:
  10.2 38.5 all-gather.3
  50.9 62.3 all-gather.5

commit v9 on v8

--- a/solution.py
+++ b/solution.py
@@ -268,9 +268,6 @@
     pages_q = spread(pages, "q", 4)
 
     w_out_all = lax.all_gather(w_out, HEAD, axis=0, tiled=True)
-    doc_rows = jnp.pad(doc_lengths.astype(BF), ((0, DPAD - DT - 1), (0, 124)))
-    doc_block = jnp.concatenate([doc_vectors, doc_rows], axis=0)
-    docs = lax.all_gather(doc_block, ("q", "r"), axis=0, tiled=True)
 
     query = jnp.dot(token_rows, w_query, preferred_element_type=F32).astype(BF) * BF(0.125)
     own_key = jnp.dot(token_rows, w_key, preferred_element_type=F32).astype(BF)
@@ -281,8 +278,13 @@
     rows = lax.all_gather(rows, "y", axis=0, tiled=True)
     pages_q, rows = lax.optimization_barrier((pages_q, rows))
     pages_q = pages_q.reshape(1024, 128)
-    ahead_two = jnp.concatenate([from_ahead(pages_q[:512], 2), from_ahead(pages_q[512:], -2)], axis=0)
+    ahead_two = from_ahead(pages_q, 2)
     prompt = [pages_q, from_ahead(pages_q, 1), ahead_two, from_ahead(pages_q, -1)]
+
+    doc_vectors, page_table, pages_q = lax.optimization_barrier((doc_vectors, page_table, pages_q))
+    doc_rows = jnp.pad(doc_lengths.astype(BF), ((0, DPAD - DT - 1), (0, 124)))
+    doc_block = jnp.concatenate([doc_vectors, doc_rows], axis=0)
+    docs = lax.all_gather(doc_block, ("q", "r"), axis=0, tiled=True)
 
     rows = rows.reshape(4, XROW, 128)
     got = rows[:, 3 * NROW : 3 * NROW + RQ, :33].reshape(16, 33).astype(jnp.int32)

time: 154 us -> 153 us (level)
  starting transfers between devices: 42.5 us -> 39.3 us
  waiting for transfers between devices: 29.8 us -> 32.6 us
  Pallas kernels: 12.6 us -> 14.5 us
    ppermute x4 -> x3, waiting for transfers between devices: 5.49 us -> 8.41 us  [from_ahead(): lax.ppermute(block, ('q', 'r'), [((i + step) % 16, i) for i in range(16)])]
    ppermute x4 -> x3, starting transfers between devices: 13.9 us -> 11.7 us  [from_ahead(): lax.ppermute(block, ('q', 'r'), [((i + step) % 16, i) for i in range(16)])]
    pallas_call x1, Pallas kernels: 2.03 us -> 3.95 us  [match(): pl.pallas_call(match_kernel, out_shape=jax.ShapeDtypeStruct((32, NC, 128)...]
  transfers between devices with their start and end apart: 10 -> 9, of which waited for: 5 -> 4; matrix products, arithmetic and copies ran while one was open for 7% -> 7% of each run, Pallas kernels for 6% -> 6%
where the time goes in v9:
time: 153 us; the launch traced here: 152 us
  blocking collectives  41 us (27%)
  starting transfers between devices  39.3 us (26%)
  waiting for transfers between devices  32.6 us (21%)
  Pallas kernels  14.5 us (9%)
  between operations  14.3 us (9%)
  local copies, waits for them, and re-layouts  4.98 us (3%)
  other arithmetic  3.61 us (2%)
  matrix products  1.92 us (1%)
    all_gather x1, blocking collectives, per_device(): context = lax.all_gather(context, HEAD, axis=0, tiled=False)  20.1 us
    all_to_all x1, starting transfers between devices, spread(): lax.all_to_all(wide, axes, 0, 0, tiled=True)  15.6 us
    all_gather x1, blocking collectives, per_device(): rows = lax.all_gather(rows, 'y', axis=0, tiled=True)  12.9 us
    ppermute x3, starting transfers between devices, from_ahead(): lax.ppermute(block, ('q', 'r'), [((i + step) % 16, i) for i in range(16)])  11.7 us
    all_to_all x1, waiting for transfers between devices, per_device(): terms = lax.all_to_all(terms, HEAD, 0, 0, tiled=True)  9.11 us
    ppermute x3, waiting for transfers between devices, from_ahead(): lax.ppermute(block, ('q', 'r'), [((i + step) % 16, i) for i in range(16)])  8.41 us
    all_to_all x1, waiting for transfers between devices, per_device(): terms = lax.all_to_all(terms, HEAD + ('y',), 0, 0, tiled=True)  8.06 us
    all_to_all x1, blocking collectives, per_device(): back = lax.all_to_all(mixed, 'y', 0, 0, tiled=True)  7.92 us
  transfers between devices with their start and end apart: 9, of which 4 were waited for; matrix products, arithmetic and copies ran while one was open for 7% of the time, Pallas kernels for 6%

profile of v9, /device:TPU:1, one launch (start us, length us, event | category | flops | bytes accessed | tf_op | source)
XLA Modules:
  0.0 152.2 jit_solution(10082945499334036907)
XLA Ops:
  7.3 0.7 all-gather.4.cloned.1.call-update
  8.0 0.8 pad_maximum_fusion.1
  8.7 0.7 broadcast_in_dim.65
  9.5 15.6 %all-to-all-start = ((bf16[4,256,128]{2,1,0:T(8,128)(2,1)}), bf16[4,256,128]{2,1,0:T(8,128)(2,1)S(1)}, u32[]{:S(2)}, u32[]{:S(2)}) async-start(bf16[4,256,128]{2,1,0:T(8,128)(2,1)} %broadcast_in_dim.65), calls=%async_computation | async-start | bytes 524288 | tf_op jit(solution)/shard_map/all_to_all | solution.py:29
  25.1 0.7 convert_bitcast_fusion
  25.8 0.7 fusion.14
  26.5 1.3 convolution_convert_fusion
  27.9 0.3 convolution_convert_fusion.1
  28.2 0.3 fusion
  28.5 0.1 copy.39
  28.6 0.1 add.104
  28.7 0.1 dynamic_slice.10
  28.8 0.1 fusion.13
  28.9 0.1 iota_compare_fusion.4
  29.0 12.9 %all_gather.15 = bf16[3136,128]{1,0:T(8,128)(2,1)S(1)} all-gather(bf16[784,128]{1,0:T(8,128)(2,1)S(1)} %pad_maximum_fusion), channel_id=1, replica_groups=mesh['x'=4,'c'=2,'y'=4,'q'=4,'r'=4] {'y'}, dimensions={0}, use_global_device_ids=true | all-gather | bytes 1003520 | tf_op jit(solution)/shard_map/all_gather | solution.py:278
  41.9 0.6 fusion.2
  42.6 6.3 %collective-permute-start = (bf16[1024,128]{1,0:T(8,128)(2,1)S(1)}, bf16[1024,128]{1,0:T(8,128)(2,1)S(1)}, u32[]{:S(2)}, u32[]{:S(2)}) collective-permute-start(bf16[1024,128]{1,0:T(8,128)(2,1)S(1)} %bitcast.36), channel_id=1, source_target_pairs={{1,0},{2,1},{3,2},{4,3},{5,4},{6,5},{7,6},{8,7},{9,8},{10,9},{11,1... | collective-permute-start | bytes 786440 | tf_op jit(solution)/shard_map/ppermute | solution.py:33
  48.9 2.7 %collective-permute-start.1 = (bf16[1024,128]{1,0:T(8,128)(2,1)S(1)}, bf16[1024,128]{1,0:T(8,128)(2,1)S(1)}, u32[]{:S(2)}, u32[]{:S(2)}) collective-permute-start(bf16[1024,128]{1,0:T(8,128)(2,1)S(1)} %bitcast.37), channel_id=1, source_target_pairs={{2,0},{3,1},{4,2},{5,3},{6,4},{7,5},{8,6},{9,7},{10,8},{11,9},{12,... | collective-permute-start | bytes 786440 | tf_op jit(solution)/shard_map/ppermute | solution.py:33
  51.6 2.7 %collective-permute-start.2 = (bf16[1024,128]{1,0:T(8,128)(2,1)S(1)}, bf16[1024,128]{1,0:T(8,128)(2,1)S(1)}, u32[]{:S(2)}, u32[]{:S(2)}) collective-permute-start(bf16[1024,128]{1,0:T(8,128)(2,1)S(1)} %bitcast.38), channel_id=1, source_target_pairs={{15,0},{0,1},{1,2},{2,3},{3,4},{4,5},{5,6},{6,7},{7,8},{8,9},{9,10... | collective-permute-start | bytes 786440 | tf_op jit(solution)/shard_map/ppermute | solution.py:33
  54.3 0.1 dynamic_slice.9
  54.4 0.1 eq.70
  54.5 0.2 select_reduce_fusion.1
  54.8 0.1 add.102
  54.9 0.1 select_reduce_fusion
  55.1 0.2 slice_reduce_fusion
  55.3 8.4 %collective-permute-done.1.refs_2_ = bf16[1024,128]{1,0:T(8,128)(2,1)S(1)} collective-permute-done((bf16[1024,128]{1,0:T(8,128)(2,1)S(1)}, bf16[1024,128]{1,0:T(8,128)(2,1)S(1)}, u32[]{:S(2)}, u32[]{:S(2)}) %collective-permute-start.1) | collective-permute-done | bytes 262176 | tf_op jit(solution)/shard_map/ppermute | solution.py:33
  63.7 3.3 %attend.1 = bf16[4,256,128]{2,1,0:T(8,128)(2,1)S(1)} custom-call(s32[16]{0:T(128)S(1)} %compare_select_fusion.3.group_ref, bf16[4,784,128]{2,1,0:T(8,128)(2,1)S(1)} %bitcast.32, f32[4,1,512]{2,1,0:T(1,128)S(1)} %bitcast.40, bf16[1024,128]{1,0:T(8,128)(2,1)S(1)} %bitcast.39, bf16[1024,128]{1,0:T(8,128)(2,1)S(1)} %collective-permute-done.refs_1_, ...), custom_call_target="tpu_custom_call" | custom-call | flops 1000 | bytes 1000 | tf_op jit(solution)/shard_map/attend/pallas_call | solution.py:92
  66.9 7.9 %all_to_all.25 = bf16[4,256,128]{2,1,0:T(8,128)(2,1)S(1)} all-to-all(bf16[4,256,128]{2,1,0:T(8,128)(2,1)S(1)} %attend.1), channel_id=1, replica_groups=mesh['x'=4,'c'=2,'y'=4,'q'=4,'r'=4] {'y'}, dimensions={0} | all-to-all | bytes 524288 | tf_op jit(solution)/shard_map/all_to_all | solution.py:307
  74.9 20.1 %all-gather = bf16[2048,128]{1,0:T(8,128)(2,1)S(1)} all-gather(bf16[256,128]{1,0:T(8,128)(2,1)S(1)} %reduce_sum.32), channel_id=2, replica_groups=mesh['x'=4,'c'=2,'y'=4,'q'=4,'r'=4] {'x','c'}, dimensions={0}, use_global_device_ids=true | all-gather | bytes 589824 | tf_op jit(solution)/shard_map/all_gather | solution.py:309
  95.0 5.4 %dense.1 = (bf16[256,1024]{1,0:T(8,128)(2,1)S(1)}, bf16[8,32,1024]{2,1,0:T(8,128)(2,1)}) custom-call(bf16[8,256,128]{2,1,0:T(8,128)(2,1)S(1)} %bitcast.33, bf16[256,1024]{1,0:T(8,128)(2,1)} %bitcast.44, f32[1,1024]{1,0:T(1,128)S(1)} %bitcast.42, bf16[1024,1024]{1,0:T(8,128)(2,1)} %all-gather.4.cloned.1.call-done.refs_0_, bf16[1024,512]{1,0:T(8,128)(2,1)} %refs_1_.1, ...), custom_call_target="tpu_custom_call" | custom-call | flops 1000 | bytes 1000 | tf_op jit(solution)/shard_map/dense/pallas_call | solution.py:218
  100.4 3.9 %all-to-all-start.2 = ((bf16[8,32,1024]{2,1,0:T(8,128)(2,1)}), bf16[8,32,1024]{2,1,0:T(8,128)(2,1)S(1)}, u32[]{:S(2)}, u32[]{:S(2)}) async-start(bf16[8,32,1024]{2,1,0:T(8,128)(2,1)} %get-tuple-element.13), calls=%async_computation.2 | async-start | bytes 1048576 | tf_op jit(solution)/shard_map/all_to_all | solution.py:311
  104.6 0.1 eq.76
  104.7 9.1 %all-to-all-done.2.terms_ref = bf16[8,32,1024]{2,1,0:T(8,128)(2,1)S(1)} async-done(((bf16[8,32,1024]{2,1,0:T(8,128)(2,1)}), bf16[8,32,1024]{2,1,0:T(8,128)(2,1)S(1)}, u32[]{:S(2)}, u32[]{:S(2)}) %all-to-all-start.2) | async-done | bytes 524320 | tf_op jit(solution)/shard_map/all_to_all | solution.py:311
  113.8 1.2 embed.1
  115.0 4.4 %all-to-all-start.3 = ((bf16[32,32,128]{2,1,0:T(8,128)(2,1)}), bf16[32,32,128]{2,1,0:T(8,128)(2,1)S(1)}, u32[]{:S(2)}, u32[]{:S(2)}) async-start(bf16[32,32,128]{2,1,0:T(8,128)(2,1)} %embed.1), calls=%async_computation.3 | async-start | bytes 524288 | tf_op jit(solution)/shard_map/all_to_all | solution.py:316
  119.4 0.1 fusion.3
  119.5 1.3 slice.30
  120.8 0.8 slice.29
  121.6 0.1 copy.44
  121.7 0.1 reshape.134
  121.8 0.1 copy.45
  121.9 0.1 reduce_window_sum.14.last_ref
  122.0 6.3 %all-to-all-done.3 = bf16[32,32,128]{2,1,0:T(8,128)(2,1)S(1)} async-done(((bf16[32,32,128]{2,1,0:T(8,128)(2,1)}), bf16[32,32,128]{2,1,0:T(8,128)(2,1)S(1)}, u32[]{:S(2)}, u32[]{:S(2)}) %all-to-all-start.3) | async-done | bytes 262176 | tf_op jit(solution)/shard_map/all_to_all | solution.py:316
  128.3 4.0 %match.1 = f32[32,16,128]{2,1,0:T(8,128)} custom-call(s32[64]{0:T(128)S(1)} %convert_element_type.45.need_ref, s32[64]{0:T(128)S(1)} %sub.16.first_ref, s32[64]{0:T(128)S(1)} %reduce_window_sum.14.last_ref, bf16[1024,128]{1,0:T(8,128)(2,1)S(1)} %bitcast.34, bf16[4096,128]{1,0:T(8,128)(2,1)S(1)} %bitcast.30, s32[16,128]{1,0:T(8,128)S(1)} %pad.14.pick_ref), custom_call_target="tpu_custom_call" | custom-call | flops 1000 | bytes 1000 | tf_op jit(solution)/shard_map/match/pallas_call | solution.py:157
  132.2 3.7 %all-to-all-start.4 = ((f32[32,16,128]{2,1,0:T(8,128)}), f32[32,16,128]{2,1,0:T(8,128)S(1)}, u32[]{:S(2)}, u32[]{:S(2)}) async-start(f32[32,16,128]{2,1,0:T(8,128)} %match.1), calls=%async_computation.4 | async-start | bytes 524288 | tf_op jit(solution)/shard_map/all_to_all | solution.py:332
  135.9 0.6 constant_dynamic-slice_fusion
  136.5 8.1 %all-to-all-done.4.terms_ref = f32[32,16,128]{2,1,0:T(8,128)S(1)} async-done(((f32[32,16,128]{2,1,0:T(8,128)}), f32[32,16,128]{2,1,0:T(8,128)S(1)}, u32[]{:S(2)}, u32[]{:S(2)}) %all-to-all-start.4) | async-done | bytes 262176 | tf_op jit(solution)/shard_map/all_to_all | solution.py:332
  144.6 0.7 total.1
  (52 shorter events, 0.8 us)
Async XLA Ops:
  7.2 19.3 %copy-start = (bf16[1024,128]{1,0:T(8,128)(2,1)S(1)}, bf16[1024,128]{1,0:T(8,128)(2,1)}, u32[]{:S(2)}) copy-start(bf16[1024,128]{1,0:T(8,128)(2,1)} %param.21) | copy-start | bytes 786436
  7.2 20.7 %copy-start.4 = (bf16[4,64,1024]{2,1,0:T(8,128)(2,1)S(1)}, bf16[4,64,1024]{2,1,0:T(8,128)(2,1)}, u32[]{:S(2)}) copy-start(bf16[4,64,1024]{2,1,0:T(8,128)(2,1)} %param.18) | copy-start | bytes 1572868
  7.2 20.7 %copy-start.5 = (bf16[1024,128]{1,0:T(8,128)(2,1)S(1)}, bf16[1024,128]{1,0:T(8,128)(2,1)}, u32[]{:S(2)}) copy-start(bf16[1024,128]{1,0:T(8,128)(2,1)} %param.20) | copy-start | bytes 786436
  7.2 21.0 %copy-start.6 = (bf16[1024,128]{1,0:T(8,128)(2,1)S(1)}, bf16[1024,128]{1,0:T(8,128)(2,1)}, u32[]{:S(2)}) copy-start(bf16[1024,128]{1,0:T(8,128)(2,1)} %param.19) | copy-start | bytes 786436
  7.2 21.5 %copy-start.8 = (s32[1,4]{1,0:T(1,128)S(1)}, s32[1,4]{1,0:T(1,128)}, u32[]{:S(2)}) copy-start(s32[1,4]{1,0:T(1,128)} %param.34) | copy-start | bytes 52
  7.2 21.5 %copy-start.9 = (s32[16]{0:T(128)S(1)}, s32[16]{0:T(128)}, u32[]{:S(2)}) copy-start(s32[16]{0:T(128)} %param.31) | copy-start | bytes 196
  7.2 87.8 %all-gather.4.cloned.1.call-start = ((), (), s32[]{:S(2)}) async-start(), calls=%async_computation.5 | async-start | bytes 2359296 | tf_op jit(solution)/shard_map/all_gather | solution.py:270
  9.5 32.4 %all-to-all-start = ((bf16[4,256,128]{2,1,0:T(8,128)(2,1)}), bf16[4,256,128]{2,1,0:T(8,128)(2,1)S(1)}, u32[]{:S(2)}, u32[]{:S(2)}) async-start(bf16[4,256,128]{2,1,0:T(8,128)(2,1)} %broadcast_in_dim.65), calls=%async_computation | async-start | bytes 524288 | tf_op jit(solution)/shard_map/all_to_all | solution.py:29
  25.1 16.8 %copy-start.7 = (bf16[256,128]{1,0:T(8,128)(2,1)S(1)}, bf16[256,128]{1,0:T(8,128)(2,1)}, u32[]{:S(2)}) copy-start(bf16[256,128]{1,0:T(8,128)(2,1)} %param.33) | copy-start | bytes 196612
  25.1 94.4 %all-gather.6.cloned.1.call-start = ((), (), s32[]{:S(2)}) async-start(), calls=%async_computation.6 | async-start | bytes 1183744 | tf_op jit(solution)/shard_map/all_gather | solution.py:287
  26.5 27.8 %copy-start.10 = (s32[128]{0:T(128)S(1)}, s32[128]{0:T(128)}, u32[]{:S(2)}) copy-start(s32[128]{0:T(128)} %param.30) | copy-start | bytes 1540
  41.9 53.1 %copy-start.3 = (f32[1024]{0:T(1024)S(1)}, f32[1024]{0:T(1024)}, u32[]{:S(2)}) copy-start(f32[1024]{0:T(1024)} %param.23) | copy-start | bytes 12292
  42.6 12.7 %collective-permute-start = (bf16[1024,128]{1,0:T(8,128)(2,1)S(1)}, bf16[1024,128]{1,0:T(8,128)(2,1)S(1)}, u32[]{:S(2)}, u32[]{:S(2)}) collective-permute-start(bf16[1024,128]{1,0:T(8,128)(2,1)S(1)} %bitcast.36), channel_id=1, source_target_pairs={{1,0},{2,1},{3,2},{4,3},{5,4},{6,5},{7,6},{8,7},{9,8},{10,9},{11,1... | collective-permute-start | bytes 786440 | tf_op jit(solution)/shard_map/ppermute | solution.py:33
  48.9 14.8 %collective-permute-start.1 = (bf16[1024,128]{1,0:T(8,128)(2,1)S(1)}, bf16[1024,128]{1,0:T(8,128)(2,1)S(1)}, u32[]{:S(2)}, u32[]{:S(2)}) collective-permute-start(bf16[1024,128]{1,0:T(8,128)(2,1)S(1)} %bitcast.37), channel_id=1, source_target_pairs={{2,0},{3,1},{4,2},{5,3},{6,4},{7,5},{8,6},{9,7},{10,8},{11,9},{12,... | collective-permute-start | bytes 786440 | tf_op jit(solution)/shard_map/ppermute | solution.py:33
  51.6 12.1 %collective-permute-start.2 = (bf16[1024,128]{1,0:T(8,128)(2,1)S(1)}, bf16[1024,128]{1,0:T(8,128)(2,1)S(1)}, u32[]{:S(2)}, u32[]{:S(2)}) collective-permute-start(bf16[1024,128]{1,0:T(8,128)(2,1)S(1)} %bitcast.38), channel_id=1, source_target_pairs={{15,0},{0,1},{1,2},{2,3},{3,4},{4,5},{5,6},{6,7},{7,8},{8,9},{9,10... | collective-permute-start | bytes 786440 | tf_op jit(solution)/shard_map/ppermute | solution.py:33
  95.0 18.8 %copy-start.1 = (bf16[1024,128]{1,0:T(8,128)(2,1)S(1)}, bf16[1024,128]{1,0:T(8,128)(2,1)}, u32[]{:S(2)}) copy-start(bf16[1024,128]{1,0:T(8,128)(2,1)} %w_project_ref.1) | copy-start | bytes 786436
  95.0 18.8 %copy-start.2 = (f32[1024]{0:T(1024)S(1)}, f32[1024]{0:T(1024)}, u32[]{:S(2)}) copy-start(f32[1024]{0:T(1024)} %param.26) | copy-start | bytes 12292
  100.4 13.3 %all-to-all-start.2 = ((bf16[8,32,1024]{2,1,0:T(8,128)(2,1)}), bf16[8,32,1024]{2,1,0:T(8,128)(2,1)S(1)}, u32[]{:S(2)}, u32[]{:S(2)}) async-start(bf16[8,32,1024]{2,1,0:T(8,128)(2,1)} %get-tuple-element.13), calls=%async_computation.2 | async-start | bytes 1048576 | tf_op jit(solution)/shard_map/all_to_all | solution.py:311
  115.0 13.3 %all-to-all-start.3 = ((bf16[32,32,128]{2,1,0:T(8,128)(2,1)}), bf16[32,32,128]{2,1,0:T(8,128)(2,1)S(1)}, u32[]{:S(2)}, u32[]{:S(2)}) async-start(bf16[32,32,128]{2,1,0:T(8,128)(2,1)} %embed.1), calls=%async_computation.3 | async-start | bytes 524288 | tf_op jit(solution)/shard_map/all_to_all | solution.py:316
  132.2 12.4 %all-to-all-start.4 = ((f32[32,16,128]{2,1,0:T(8,128)}), f32[32,16,128]{2,1,0:T(8,128)S(1)}, u32[]{:S(2)}, u32[]{:S(2)}) async-start(f32[32,16,128]{2,1,0:T(8,128)} %match.1), calls=%async_computation.4 | async-start | bytes 524288 | tf_op jit(solution)/shard_map/all_to_all | solution.py:332
Sparse Core Ops, SparseCore 0:
  10.2 38.5 all-gather.3
  50.9 61.8 all-gather.5

commit v10 on v9

--- a/solution.py
+++ b/solution.py
@@ -278,7 +278,8 @@
     rows = lax.all_gather(rows, "y", axis=0, tiled=True)
     pages_q, rows = lax.optimization_barrier((pages_q, rows))
     pages_q = pages_q.reshape(1024, 128)
-    ahead_two = from_ahead(pages_q, 2)
+    pairs = [((i + 2 if i % 2 == 0 else i - 2) % 16, i) for i in range(16)]
+    ahead_two = lax.ppermute(pages_q, ("q", "r"), pairs)
     prompt = [pages_q, from_ahead(pages_q, 1), ahead_two, from_ahead(pages_q, -1)]
 
     doc_vectors, page_table, pages_q = lax.optimization_barrier((doc_vectors, page_table, pages_q))

time: 153 us -> 152 us (level)
  starting transfers between devices: 39.3 us -> 42.9 us
  Pallas kernels: 14.5 us -> 12.2 us
  blocking collectives: 41 us -> 39.1 us
    ppermute x0 -> x1, waiting for transfers between devices: none -> 5.38 us  [per_device(): ahead_two = lax.ppermute(pages_q, ('q', 'r'), pairs)]
    ppermute x3 -> x2, waiting for transfers between devices: 8.41 us -> 3.04 us  [from_ahead(): lax.ppermute(block, ('q', 'r'), [((i + step) % 16, i) for i in range(16)])]
    all_to_all x1, starting transfers between devices: 3.66 us -> 7.91 us  [per_device(): terms = lax.all_to_all(terms, HEAD + ('y',), 0, 0, tiled=True)]
    ppermute x3 -> x2, starting transfers between devices: 11.7 us -> 8.42 us  [from_ahead(): lax.ppermute(block, ('q', 'r'), [((i + step) % 16, i) for i in range(16)])]
    all_gather x1, blocking collectives: 20.1 us -> 17.2 us  [per_device(): context = lax.all_gather(context, HEAD, axis=0, tiled=False)]
    ppermute x0 -> x1, starting transfers between devices: none -> 2.69 us  [per_device(): ahead_two = lax.ppermute(pages_q, ('q', 'r'), pairs)]
  transfers between devices with their start and end apart: 9 -> 9, of which waited for: 4 -> 5; matrix products, arithmetic and copies ran while one was open for 7% -> 7% of each run, Pallas kernels for 6% -> 6%
where the time goes in v10:
time: 152 us
  starting transfers between devices  42.9 us (28%)
  blocking collectives  39.1 us (26%)
  waiting for transfers between devices  32.7 us (22%)
  between operations  14.3 us (9%)
  Pallas kernels  12.2 us (8%)
  local copies, waits for them, and re-layouts  4.98 us (3%)
  other arithmetic  3.61 us (2%)
  matrix products  1.92 us (1%)
    all_gather x1, blocking collectives, per_device(): context = lax.all_gather(context, HEAD, axis=0, tiled=False)  17.2 us
    all_to_all x1, starting transfers between devices, spread(): lax.all_to_all(wide, axes, 0, 0, tiled=True)  15.6 us
    all_gather x1, blocking collectives, per_device(): rows = lax.all_gather(rows, 'y', axis=0, tiled=True)  12.9 us
    all_to_all x1, waiting for transfers between devices, per_device(): terms = lax.all_to_all(terms, HEAD, 0, 0, tiled=True)  9.11 us
    all_to_all x1, blocking collectives, per_device(): back = lax.all_to_all(mixed, 'y', 0, 0, tiled=True)  8.92 us
    ppermute x2, starting transfers between devices, from_ahead(): lax.ppermute(block, ('q', 'r'), [((i + step) % 16, i) for i in range(16)])  8.42 us
    all_to_all x1, waiting for transfers between devices, per_device(): terms = lax.all_to_all(terms, HEAD + ('y',), 0, 0, tiled=True)  8.16 us
    all_to_all x1, starting transfers between devices, per_device(): terms = lax.all_to_all(terms, HEAD + ('y',), 0, 0, tiled=True)  7.91 us
  transfers between devices with their start and end apart: 9, of which 5 were waited for; matrix products, arithmetic and copies ran while one was open for 7% of the time, Pallas kernels for 6%

profile of v10, /device:TPU:1, one launch (start us, length us, event | category | flops | bytes accessed | tf_op | source)
XLA Modules:
  0.0 151.7 jit_solution(4983628950411333144)
XLA Ops:
  7.3 0.7 all-gather.4.cloned.1.call-update
  8.0 0.8 pad_maximum_fusion.1
  8.7 0.7 broadcast_in_dim.65
  9.5 15.6 %all-to-all-start = ((bf16[4,256,128]{2,1,0:T(8,128)(2,1)}), bf16[4,256,128]{2,1,0:T(8,128)(2,1)S(1)}, u32[]{:S(2)}, u32[]{:S(2)}) async-start(bf16[4,256,128]{2,1,0:T(8,128)(2,1)} %broadcast_in_dim.65), calls=%async_computation | async-start | bytes 524288 | tf_op jit(solution)/shard_map/all_to_all | solution.py:29
  25.1 0.7 convert_bitcast_fusion
  25.8 0.7 fusion.14
  26.5 1.3 convolution_convert_fusion
  27.9 0.3 convolution_convert_fusion.1
  28.2 0.3 fusion
  28.5 0.1 copy.39
  28.6 0.1 add.104
  28.7 0.1 dynamic_slice.10
  28.8 0.1 fusion.13
  29.0 12.9 %all_gather.15 = bf16[3136,128]{1,0:T(8,128)(2,1)S(1)} all-gather(bf16[784,128]{1,0:T(8,128)(2,1)S(1)} %pad_maximum_fusion), channel_id=1, replica_groups=mesh['x'=4,'c'=2,'y'=4,'q'=4,'r'=4] {'y'}, dimensions={0}, use_global_device_ids=true | all-gather | bytes 1003520 | tf_op jit(solution)/shard_map/all_gather | solution.py:278
  41.9 0.6 fusion.2
  42.6 6.3 %collective-permute-start = (bf16[1024,128]{1,0:T(8,128)(2,1)S(1)}, bf16[1024,128]{1,0:T(8,128)(2,1)S(1)}, u32[]{:S(2)}, u32[]{:S(2)}) collective-permute-start(bf16[1024,128]{1,0:T(8,128)(2,1)S(1)} %bitcast.36), channel_id=1, source_target_pairs={{1,0},{2,1},{3,2},{4,3},{5,4},{6,5},{7,6},{8,7},{9,8},{10,9},{11,1... | collective-permute-start | bytes 786440 | tf_op jit(solution)/shard_map/ppermute | solution.py:33
  48.9 2.7 %collective-permute-start.1 = (bf16[1024,128]{1,0:T(8,128)(2,1)S(1)}, bf16[1024,128]{1,0:T(8,128)(2,1)S(1)}, u32[]{:S(2)}, u32[]{:S(2)}) collective-permute-start(bf16[1024,128]{1,0:T(8,128)(2,1)S(1)} %bitcast.37), channel_id=1, source_target_pairs={{2,0},{15,1},{4,2},{1,3},{6,4},{3,5},{8,6},{5,7},{10,8},{7,9},{12,... | collective-permute-start | bytes 786440 | tf_op jit(solution)/shard_map/ppermute | solution.py:282
  51.6 2.1 %collective-permute-start.2 = (bf16[1024,128]{1,0:T(8,128)(2,1)S(1)}, bf16[1024,128]{1,0:T(8,128)(2,1)S(1)}, u32[]{:S(2)}, u32[]{:S(2)}) collective-permute-start(bf16[1024,128]{1,0:T(8,128)(2,1)S(1)} %bitcast.38), channel_id=1, source_target_pairs={{15,0},{0,1},{1,2},{2,3},{3,4},{4,5},{5,6},{6,7},{7,8},{8,9},{9,10... | collective-permute-start | bytes 786440 | tf_op jit(solution)/shard_map/ppermute | solution.py:33
  53.7 0.1 dynamic_slice.9
  53.8 0.1 eq.70
  53.9 0.2 select_reduce_fusion.1
  54.2 0.1 add.102
  54.3 0.1 select_reduce_fusion
  54.5 0.2 slice_reduce_fusion
  54.7 5.4 %collective-permute-done.1.refs_2_ = bf16[1024,128]{1,0:T(8,128)(2,1)S(1)} collective-permute-done((bf16[1024,128]{1,0:T(8,128)(2,1)S(1)}, bf16[1024,128]{1,0:T(8,128)(2,1)S(1)}, u32[]{:S(2)}, u32[]{:S(2)}) %collective-permute-start.1) | collective-permute-done | bytes 262176 | tf_op jit(solution)/shard_map/ppermute | solution.py:282
  60.0 3.0 %collective-permute-done.2.refs_3_ = bf16[1024,128]{1,0:T(8,128)(2,1)S(1)} collective-permute-done((bf16[1024,128]{1,0:T(8,128)(2,1)S(1)}, bf16[1024,128]{1,0:T(8,128)(2,1)S(1)}, u32[]{:S(2)}, u32[]{:S(2)}) %collective-permute-start.2) | collective-permute-done | bytes 262176 | tf_op jit(solution)/shard_map/ppermute | solution.py:33
  63.1 2.4 %attend.1 = bf16[4,256,128]{2,1,0:T(8,128)(2,1)S(1)} custom-call(s32[16]{0:T(128)S(1)} %compare_select_fusion.3.group_ref, bf16[4,784,128]{2,1,0:T(8,128)(2,1)S(1)} %bitcast.32, f32[4,1,512]{2,1,0:T(1,128)S(1)} %bitcast.40, bf16[1024,128]{1,0:T(8,128)(2,1)S(1)} %bitcast.39, bf16[1024,128]{1,0:T(8,128)(2,1)S(1)} %collective-permute-done.refs_1_, ...), custom_call_target="tpu_custom_call" | custom-call | flops 1000 | bytes 1000 | tf_op jit(solution)/shard_map/attend/pallas_call | solution.py:92
  65.5 8.9 %all_to_all.25 = bf16[4,256,128]{2,1,0:T(8,128)(2,1)S(1)} all-to-all(bf16[4,256,128]{2,1,0:T(8,128)(2,1)S(1)} %attend.1), channel_id=1, replica_groups=mesh['x'=4,'c'=2,'y'=4,'q'=4,'r'=4] {'y'}, dimensions={0} | all-to-all | bytes 524288 | tf_op jit(solution)/shard_map/all_to_all | solution.py:308
  74.4 17.2 %all-gather = bf16[2048,128]{1,0:T(8,128)(2,1)S(1)} all-gather(bf16[256,128]{1,0:T(8,128)(2,1)S(1)} %reduce_sum.32), channel_id=2, replica_groups=mesh['x'=4,'c'=2,'y'=4,'q'=4,'r'=4] {'x','c'}, dimensions={0}, use_global_device_ids=true | all-gather | bytes 589824 | tf_op jit(solution)/shard_map/all_gather | solution.py:310
  91.7 5.4 %dense.1 = (bf16[256,1024]{1,0:T(8,128)(2,1)S(1)}, bf16[8,32,1024]{2,1,0:T(8,128)(2,1)}) custom-call(bf16[8,256,128]{2,1,0:T(8,128)(2,1)S(1)} %bitcast.33, bf16[256,1024]{1,0:T(8,128)(2,1)} %bitcast.44, f32[1,1024]{1,0:T(1,128)S(1)} %bitcast.42, bf16[1024,1024]{1,0:T(8,128)(2,1)} %all-gather.4.cloned.1.call-done.refs_0_, bf16[1024,512]{1,0:T(8,128)(2,1)} %refs_1_.1, ...), custom_call_target="tpu_custom_call" | custom-call | flops 1000 | bytes 1000 | tf_op jit(solution)/shard_map/dense/pallas_call | solution.py:218
  97.1 3.8 %all-to-all-start.2 = ((bf16[8,32,1024]{2,1,0:T(8,128)(2,1)}), bf16[8,32,1024]{2,1,0:T(8,128)(2,1)S(1)}, u32[]{:S(2)}, u32[]{:S(2)}) async-start(bf16[8,32,1024]{2,1,0:T(8,128)(2,1)} %get-tuple-element.13), calls=%async_computation.2 | async-start | bytes 1048576 | tf_op jit(solution)/shard_map/all_to_all | solution.py:312
  101.2 0.1 eq.76
  101.3 9.1 %all-to-all-done.2.terms_ref = bf16[8,32,1024]{2,1,0:T(8,128)(2,1)S(1)} async-done(((bf16[8,32,1024]{2,1,0:T(8,128)(2,1)}), bf16[8,32,1024]{2,1,0:T(8,128)(2,1)S(1)}, u32[]{:S(2)}, u32[]{:S(2)}) %all-to-all-start.2) | async-done | bytes 524320 | tf_op jit(solution)/shard_map/all_to_all | solution.py:312
  110.4 1.2 embed.1
  111.6 4.4 %all-to-all-start.3 = ((bf16[32,32,128]{2,1,0:T(8,128)(2,1)}), bf16[32,32,128]{2,1,0:T(8,128)(2,1)S(1)}, u32[]{:S(2)}, u32[]{:S(2)}) async-start(bf16[32,32,128]{2,1,0:T(8,128)(2,1)} %embed.1), calls=%async_computation.3 | async-start | bytes 524288 | tf_op jit(solution)/shard_map/all_to_all | solution.py:317
  116.0 0.1 fusion.3
  116.2 1.3 slice.30
  117.5 0.8 slice.29
  118.2 0.1 copy.44
  118.3 0.1 reshape.134
  118.5 0.1 copy.45
  118.5 0.1 reduce_window_sum.14.last_ref
  118.6 6.3 %all-to-all-done.3 = bf16[32,32,128]{2,1,0:T(8,128)(2,1)S(1)} async-done(((bf16[32,32,128]{2,1,0:T(8,128)(2,1)}), bf16[32,32,128]{2,1,0:T(8,128)(2,1)S(1)}, u32[]{:S(2)}, u32[]{:S(2)}) %all-to-all-start.3) | async-done | bytes 262176 | tf_op jit(solution)/shard_map/all_to_all | solution.py:317
  124.9 2.5 %match.1 = f32[32,16,128]{2,1,0:T(8,128)} custom-call(s32[64]{0:T(128)S(1)} %convert_element_type.45.need_ref, s32[64]{0:T(128)S(1)} %sub.16.first_ref, s32[64]{0:T(128)S(1)} %reduce_window_sum.14.last_ref, bf16[1024,128]{1,0:T(8,128)(2,1)S(1)} %bitcast.34, bf16[4096,128]{1,0:T(8,128)(2,1)S(1)} %bitcast.30, s32[16,128]{1,0:T(8,128)S(1)} %pad.14.pick_ref), custom_call_target="tpu_custom_call" | custom-call | flops 1000 | bytes 1000 | tf_op jit(solution)/shard_map/match/pallas_call | solution.py:157
  127.4 7.9 %all-to-all-start.4 = ((f32[32,16,128]{2,1,0:T(8,128)}), f32[32,16,128]{2,1,0:T(8,128)S(1)}, u32[]{:S(2)}, u32[]{:S(2)}) async-start(f32[32,16,128]{2,1,0:T(8,128)} %match.1), calls=%async_computation.4 | async-start | bytes 524288 | tf_op jit(solution)/shard_map/all_to_all | solution.py:333
  135.3 0.6 constant_dynamic-slice_fusion
  135.9 8.2 %all-to-all-done.4.terms_ref = f32[32,16,128]{2,1,0:T(8,128)S(1)} async-done(((f32[32,16,128]{2,1,0:T(8,128)}), f32[32,16,128]{2,1,0:T(8,128)S(1)}, u32[]{:S(2)}, u32[]{:S(2)}) %all-to-all-start.4) | async-done | bytes 262176 | tf_op jit(solution)/shard_map/all_to_all | solution.py:333
  144.1 0.7 total.1
  (52 shorter events, 0.8 us)
Async XLA Ops:
  7.2 19.3 %copy-start = (bf16[1024,128]{1,0:T(8,128)(2,1)S(1)}, bf16[1024,128]{1,0:T(8,128)(2,1)}, u32[]{:S(2)}) copy-start(bf16[1024,128]{1,0:T(8,128)(2,1)} %param.21) | copy-start | bytes 786436
  7.2 20.7 %copy-start.4 = (bf16[4,64,1024]{2,1,0:T(8,128)(2,1)S(1)}, bf16[4,64,1024]{2,1,0:T(8,128)(2,1)}, u32[]{:S(2)}) copy-start(bf16[4,64,1024]{2,1,0:T(8,128)(2,1)} %param.18) | copy-start | bytes 1572868
  7.2 20.7 %copy-start.5 = (bf16[1024,128]{1,0:T(8,128)(2,1)S(1)}, bf16[1024,128]{1,0:T(8,128)(2,1)}, u32[]{:S(2)}) copy-start(bf16[1024,128]{1,0:T(8,128)(2,1)} %param.20) | copy-start | bytes 786436
  7.2 21.0 %copy-start.6 = (bf16[1024,128]{1,0:T(8,128)(2,1)S(1)}, bf16[1024,128]{1,0:T(8,128)(2,1)}, u32[]{:S(2)}) copy-start(bf16[1024,128]{1,0:T(8,128)(2,1)} %param.19) | copy-start | bytes 786436
  7.2 21.5 %copy-start.8 = (s32[1,4]{1,0:T(1,128)S(1)}, s32[1,4]{1,0:T(1,128)}, u32[]{:S(2)}) copy-start(s32[1,4]{1,0:T(1,128)} %param.34) | copy-start | bytes 52
  7.2 21.5 %copy-start.9 = (s32[16]{0:T(128)S(1)}, s32[16]{0:T(128)}, u32[]{:S(2)}) copy-start(s32[16]{0:T(128)} %param.31) | copy-start | bytes 196
  7.2 84.4 %all-gather.4.cloned.1.call-start = ((), (), s32[]{:S(2)}) async-start(), calls=%async_computation.5 | async-start | bytes 2359296 | tf_op jit(solution)/shard_map/all_gather | solution.py:270
  9.5 32.4 %all-to-all-start = ((bf16[4,256,128]{2,1,0:T(8,128)(2,1)}), bf16[4,256,128]{2,1,0:T(8,128)(2,1)S(1)}, u32[]{:S(2)}, u32[]{:S(2)}) async-start(bf16[4,256,128]{2,1,0:T(8,128)(2,1)} %broadcast_in_dim.65), calls=%async_computation | async-start | bytes 524288 | tf_op jit(solution)/shard_map/all_to_all | solution.py:29
  25.1 16.8 %copy-start.7 = (bf16[256,128]{1,0:T(8,128)(2,1)S(1)}, bf16[256,128]{1,0:T(8,128)(2,1)}, u32[]{:S(2)}) copy-start(bf16[256,128]{1,0:T(8,128)(2,1)} %param.33) | copy-start | bytes 196612
  25.1 91.0 %all-gather.6.cloned.1.call-start = ((), (), s32[]{:S(2)}) async-start(), calls=%async_computation.6 | async-start | bytes 1183744 | tf_op jit(solution)/shard_map/all_gather | solution.py:288
  26.5 27.2 %copy-start.10 = (s32[128]{0:T(128)S(1)}, s32[128]{0:T(128)}, u32[]{:S(2)}) copy-start(s32[128]{0:T(128)} %param.30) | copy-start | bytes 1540
  41.9 49.7 %copy-start.3 = (f32[1024]{0:T(1024)S(1)}, f32[1024]{0:T(1024)}, u32[]{:S(2)}) copy-start(f32[1024]{0:T(1024)} %param.23) | copy-start | bytes 12292
  42.6 12.1 %collective-permute-start = (bf16[1024,128]{1,0:T(8,128)(2,1)S(1)}, bf16[1024,128]{1,0:T(8,128)(2,1)S(1)}, u32[]{:S(2)}, u32[]{:S(2)}) collective-permute-start(bf16[1024,128]{1,0:T(8,128)(2,1)S(1)} %bitcast.36), channel_id=1, source_target_pairs={{1,0},{2,1},{3,2},{4,3},{5,4},{6,5},{7,6},{8,7},{9,8},{10,9},{11,1... | collective-permute-start | bytes 786440 | tf_op jit(solution)/shard_map/ppermute | solution.py:33
  48.9 11.2 %collective-permute-start.1 = (bf16[1024,128]{1,0:T(8,128)(2,1)S(1)}, bf16[1024,128]{1,0:T(8,128)(2,1)S(1)}, u32[]{:S(2)}, u32[]{:S(2)}) collective-permute-start(bf16[1024,128]{1,0:T(8,128)(2,1)S(1)} %bitcast.37), channel_id=1, source_target_pairs={{2,0},{15,1},{4,2},{1,3},{6,4},{3,5},{8,6},{5,7},{10,8},{7,9},{12,... | collective-permute-start | bytes 786440 | tf_op jit(solution)/shard_map/ppermute | solution.py:282
  51.6 11.5 %collective-permute-start.2 = (bf16[1024,128]{1,0:T(8,128)(2,1)S(1)}, bf16[1024,128]{1,0:T(8,128)(2,1)S(1)}, u32[]{:S(2)}, u32[]{:S(2)}) collective-permute-start(bf16[1024,128]{1,0:T(8,128)(2,1)S(1)} %bitcast.38), channel_id=1, source_target_pairs={{15,0},{0,1},{1,2},{2,3},{3,4},{4,5},{5,6},{6,7},{7,8},{8,9},{9,10... | collective-permute-start | bytes 786440 | tf_op jit(solution)/shard_map/ppermute | solution.py:33
  91.6 18.8 %copy-start.1 = (bf16[1024,128]{1,0:T(8,128)(2,1)S(1)}, bf16[1024,128]{1,0:T(8,128)(2,1)}, u32[]{:S(2)}) copy-start(bf16[1024,128]{1,0:T(8,128)(2,1)} %w_project_ref.1) | copy-start | bytes 786436
  91.6 18.8 %copy-start.2 = (f32[1024]{0:T(1024)S(1)}, f32[1024]{0:T(1024)}, u32[]{:S(2)}) copy-start(f32[1024]{0:T(1024)} %param.26) | copy-start | bytes 12292
  97.1 13.3 %all-to-all-start.2 = ((bf16[8,32,1024]{2,1,0:T(8,128)(2,1)}), bf16[8,32,1024]{2,1,0:T(8,128)(2,1)S(1)}, u32[]{:S(2)}, u32[]{:S(2)}) async-start(bf16[8,32,1024]{2,1,0:T(8,128)(2,1)} %get-tuple-element.13), calls=%async_computation.2 | async-start | bytes 1048576 | tf_op jit(solution)/shard_map/all_to_all | solution.py:312
  111.6 13.3 %all-to-all-start.3 = ((bf16[32,32,128]{2,1,0:T(8,128)(2,1)}), bf16[32,32,128]{2,1,0:T(8,128)(2,1)S(1)}, u32[]{:S(2)}, u32[]{:S(2)}) async-start(bf16[32,32,128]{2,1,0:T(8,128)(2,1)} %embed.1), calls=%async_computation.3 | async-start | bytes 524288 | tf_op jit(solution)/shard_map/all_to_all | solution.py:317
  127.4 16.7 %all-to-all-start.4 = ((f32[32,16,128]{2,1,0:T(8,128)}), f32[32,16,128]{2,1,0:T(8,128)S(1)}, u32[]{:S(2)}, u32[]{:S(2)}) async-start(f32[32,16,128]{2,1,0:T(8,128)} %match.1), calls=%async_computation.4 | async-start | bytes 524288 | tf_op jit(solution)/shard_map/all_to_all | solution.py:333
Sparse Core Ops, SparseCore 0:
  10.2 38.5 all-gather.3
  50.9 61.9 all-gather.5

commit v11 on v10

--- a/solution.py
+++ b/solution.py
@@ -272,8 +272,7 @@
     query = jnp.dot(token_rows, w_query, preferred_element_type=F32).astype(BF) * BF(0.125)
     own_key = jnp.dot(token_rows, w_key, preferred_element_type=F32).astype(BF)
     own_value = jnp.dot(token_rows, w_value, preferred_element_type=F32).astype(BF)
-    ids = jnp.concatenate([candidates // 64, candidates % 64, request_group[:, None]], axis=1)
-    ids = jnp.pad(ids.astype(BF), ((0, 12), (0, 128 - 33)))
+    ids = jnp.pad(request_group.astype(BF)[:, None], ((0, 12), (0, 127)))
     rows = jnp.concatenate([query, own_key, own_value, ids], axis=0)
     rows = lax.all_gather(rows, "y", axis=0, tiled=True)
     pages_q, rows = lax.optimization_barrier((pages_q, rows))
@@ -288,9 +287,8 @@
     docs = lax.all_gather(doc_block, ("q", "r"), axis=0, tiled=True)
 
     rows = rows.reshape(4, XROW, 128)
-    got = rows[:, 3 * NROW : 3 * NROW + RQ, :33].reshape(16, 33).astype(jnp.int32)
-    groups = jnp.where(got[:, 32] // 4 == my_y, got[:, 32] % 4, -1)
-    pick = jnp.where(got[:, :16] == my_head * 4 + my_y, got[:, 16:32], -1)
+    got = rows[:, 3 * NROW : 3 * NROW + RQ, 0].reshape(16).astype(jnp.int32)
+    groups = jnp.where(got // 4 == my_y, got % 4, -1)
 
     table = lax.dynamic_slice(page_table, (my_y * 32,), (32,)).reshape(4, 8)
     lengths = lax.dynamic_slice(prompt_lengths, (my_y * 4,), (4,))
@@ -309,6 +307,9 @@
     context = jnp.sum(back.astype(F32), axis=0).astype(BF)
     context = lax.all_gather(context, HEAD, axis=0, tiled=False)
     first, terms = dense(context, token_rows, norm1_gain[None], [w_out_all, w_inner, w_outer])
+    candidates, terms = lax.optimization_barrier((candidates, terms))
+    asked = lax.all_gather(candidates, "y", axis=0, tiled=True)
+    pick = jnp.where(asked // 64 == my_head * 4 + my_y, asked % 64, -1)
     terms = lax.all_to_all(terms, HEAD, 0, 0, tiled=True)
     embed = vmem_call(embed_kernel, jax.ShapeDtypeStruct((32, 32, 128), BF), "embed", 1)(
         my_head.reshape(1), first, terms, norm2_gain[None], w_project

time: 152 us -> 155 us (1.020)
  blocking collectives: 39.1 us -> 51 us
  waiting for transfers between devices: 32.7 us -> 23.5 us
  starting transfers between devices: 42.9 us -> 46 us
  Pallas kernels: 12.2 us -> 9.91 us
    all_gather x0 -> x1, blocking collectives: none -> 8.68 us  [per_device(): asked = lax.all_gather(candidates, 'y', axis=0, tiled=True)]
    all_to_all x1, waiting for transfers between devices: 9.11 us -> 0.53 us  [per_device(): terms = lax.all_to_all(terms, HEAD, 0, 0, tiled=True)]
    all_to_all x1, starting transfers between devices: 4.41 us -> 7.99 us  [per_device(): queries = lax.all_to_all(embed, HEAD + ('y',), 0, 0, tiled=True)]
    all_to_all x1, blocking collectives: 8.92 us -> 12.2 us  [per_device(): back = lax.all_to_all(mixed, 'y', 0, 0, tiled=True)]
    all_to_all x1, starting transfers between devices: 7.91 us -> 5.99 us  [per_device(): terms = lax.all_to_all(terms, HEAD + ('y',), 0, 0, tiled=True)]
    pallas_call x1, Pallas kernels: 2.36 us -> 0.58 us  [attend(): pl.pallas_call(attend_kernel, out_shape=jax.ShapeDtypeStruct((4, NROW, 12...]
    ppermute x1, waiting for transfers between devices: 5.38 us -> 3.8 us  [per_device(): ahead_two = lax.ppermute(pages_q, ('q', 'r'), pairs)]
  transfers between devices with their start and end apart: 9 -> 9, of which waited for: 5 -> 5; matrix products, arithmetic and copies ran while one was open for 7% -> 6% of each run, Pallas kernels for 6% -> 5%
where the time goes in v11:
time: 155 us; the launch traced here: 154 us
  blocking collectives  51 us (33%)
  starting transfers between devices  46 us (30%)
  waiting for transfers between devices  23.5 us (15%)
  between operations  14.4 us (9%)
  Pallas kernels  9.91 us (6%)
  local copies, waits for them, and re-layouts  4.74 us (3%)
  other arithmetic  2.32 us (1%)
  matrix products  1.94 us (1%)
    all_gather x1, blocking collectives, per_device(): context = lax.all_gather(context, HEAD, axis=0, tiled=False)  17.2 us
    all_to_all x1, starting transfers between devices, spread(): lax.all_to_all(wide, axes, 0, 0, tiled=True)  15.6 us
    all_gather x1, blocking collectives, per_device(): rows = lax.all_gather(rows, 'y', axis=0, tiled=True)  12.9 us
    all_to_all x1, blocking collectives, per_device(): back = lax.all_to_all(mixed, 'y', 0, 0, tiled=True)  12.2 us
    ppermute x2, starting transfers between devices, from_ahead(): lax.ppermute(block, ('q', 'r'), [((i + step) % 16, i) for i in range(16)])  9.22 us
    all_gather x1, blocking collectives, per_device(): asked = lax.all_gather(candidates, 'y', axis=0, tiled=True)  8.68 us
    all_to_all x1, waiting for transfers between devices, per_device(): terms = lax.all_to_all(terms, HEAD + ('y',), 0, 0, tiled=True)  8.16 us
    all_to_all x1, starting transfers between devices, per_device(): queries = lax.all_to_all(embed, HEAD + ('y',), 0, 0, tiled=True)  7.99 us
  transfers between devices with their start and end apart: 9, of which 5 were waited for; matrix products, arithmetic and copies ran while one was open for 6% of the time, Pallas kernels for 5%

profile of v11, /device:TPU:1, one launch (start us, length us, event | category | flops | bytes accessed | tf_op | source)
XLA Modules:
  0.0 153.9 jit_solution(6197763326354550022)
XLA Ops:
  7.3 0.7 all-gather.5.cloned.1.call-update
  8.0 0.8 pad_maximum_fusion
  8.8 0.7 broadcast_in_dim.62
  9.5 15.6 %all-to-all-start = ((bf16[4,256,128]{2,1,0:T(8,128)(2,1)}), bf16[4,256,128]{2,1,0:T(8,128)(2,1)S(1)}, u32[]{:S(2)}, u32[]{:S(2)}) async-start(bf16[4,256,128]{2,1,0:T(8,128)(2,1)} %broadcast_in_dim.62), calls=%async_computation | async-start | bytes 524288 | tf_op jit(solution)/shard_map/all_to_all | solution.py:29
  25.1 1.4 convolution_convert_fusion
  26.5 0.3 convolution_convert_fusion.1
  26.8 0.3 fusion
  27.2 0.1 copy.43
  27.3 0.1 add.103
  27.4 0.1 dynamic_slice.10
  27.5 12.9 %all_gather.18 = bf16[3136,128]{1,0:T(8,128)(2,1)S(1)} all-gather(bf16[784,128]{1,0:T(8,128)(2,1)S(1)} %fusion.2), channel_id=1, replica_groups=mesh['x'=4,'c'=2,'y'=4,'q'=4,'r'=4] {'y'}, dimensions={0}, use_global_device_ids=true | all-gather | bytes 1003520 | tf_op jit(solution)/shard_map/all_gather | solution.py:277
  40.5 0.6 fusion.4
  41.2 6.3 %collective-permute-start = (bf16[1024,128]{1,0:T(8,128)(2,1)S(1)}, bf16[1024,128]{1,0:T(8,128)(2,1)S(1)}, u32[]{:S(2)}, u32[]{:S(2)}) collective-permute-start(bf16[1024,128]{1,0:T(8,128)(2,1)S(1)} %bitcast.37), channel_id=1, source_target_pairs={{1,0},{2,1},{3,2},{4,3},{5,4},{6,5},{7,6},{8,7},{9,8},{10,9},{11,1... | collective-permute-start | bytes 786440 | tf_op jit(solution)/shard_map/ppermute | solution.py:33
  47.5 3.3 %collective-permute-start.1 = (bf16[1024,128]{1,0:T(8,128)(2,1)S(1)}, bf16[1024,128]{1,0:T(8,128)(2,1)S(1)}, u32[]{:S(2)}, u32[]{:S(2)}) collective-permute-start(bf16[1024,128]{1,0:T(8,128)(2,1)S(1)} %bitcast.38), channel_id=1, source_target_pairs={{2,0},{15,1},{4,2},{1,3},{6,4},{3,5},{8,6},{5,7},{10,8},{7,9},{12,... | collective-permute-start | bytes 786440 | tf_op jit(solution)/shard_map/ppermute | solution.py:281
  50.8 2.9 %collective-permute-start.2 = (bf16[1024,128]{1,0:T(8,128)(2,1)S(1)}, bf16[1024,128]{1,0:T(8,128)(2,1)S(1)}, u32[]{:S(2)}, u32[]{:S(2)}) collective-permute-start(bf16[1024,128]{1,0:T(8,128)(2,1)S(1)} %bitcast.39), channel_id=1, source_target_pairs={{15,0},{0,1},{1,2},{2,3},{3,4},{4,5},{5,6},{6,7},{7,8},{8,9},{9,10... | collective-permute-start | bytes 786440 | tf_op jit(solution)/shard_map/ppermute | solution.py:33
  53.7 0.1 dynamic_slice.9
  53.8 0.1 eq.70
  53.9 0.2 select_reduce_fusion.1
  54.2 0.1 add.101
  54.3 0.1 fusion.8
  54.3 0.1 select_reduce_fusion
  54.5 0.1 convert_reduce_fusion
  54.6 0.1 reshape.131
  54.7 3.8 %collective-permute-done.1.refs_2_ = bf16[1024,128]{1,0:T(8,128)(2,1)S(1)} collective-permute-done((bf16[1024,128]{1,0:T(8,128)(2,1)S(1)}, bf16[1024,128]{1,0:T(8,128)(2,1)S(1)}, u32[]{:S(2)}, u32[]{:S(2)}) %collective-permute-start.1) | collective-permute-done | bytes 262176 | tf_op jit(solution)/shard_map/ppermute | solution.py:281
  58.5 4.2 %collective-permute-done.2.refs_3_ = bf16[1024,128]{1,0:T(8,128)(2,1)S(1)} collective-permute-done((bf16[1024,128]{1,0:T(8,128)(2,1)S(1)}, bf16[1024,128]{1,0:T(8,128)(2,1)S(1)}, u32[]{:S(2)}, u32[]{:S(2)}) %collective-permute-start.2) | collective-permute-done | bytes 262176 | tf_op jit(solution)/shard_map/ppermute | solution.py:33
  62.7 0.6 attend.1
  63.3 12.2 %all_to_all.25 = bf16[4,256,128]{2,1,0:T(8,128)(2,1)S(1)} all-to-all(bf16[4,256,128]{2,1,0:T(8,128)(2,1)S(1)} %attend.1), channel_id=1, replica_groups=mesh['x'=4,'c'=2,'y'=4,'q'=4,'r'=4] {'y'}, dimensions={0} | all-to-all | bytes 524288 | tf_op jit(solution)/shard_map/all_to_all | solution.py:306
  75.5 17.2 %all-gather = bf16[2048,128]{1,0:T(8,128)(2,1)S(1)} all-gather(bf16[256,128]{1,0:T(8,128)(2,1)S(1)} %reduce_sum.32), channel_id=2, replica_groups=mesh['x'=4,'c'=2,'y'=4,'q'=4,'r'=4] {'x','c'}, dimensions={0}, use_global_device_ids=true | all-gather | bytes 589824 | tf_op jit(solution)/shard_map/all_gather | solution.py:308
  92.7 5.4 %dense.1 = (bf16[256,1024]{1,0:T(8,128)(2,1)S(1)}, bf16[8,32,1024]{2,1,0:T(8,128)(2,1)}) custom-call(bf16[8,256,128]{2,1,0:T(8,128)(2,1)S(1)} %bitcast.34, bf16[256,1024]{1,0:T(8,128)(2,1)} %bitcast.45, f32[1,1024]{1,0:T(1,128)S(1)} %bitcast.43, bf16[1024,1024]{1,0:T(8,128)(2,1)} %all-gather.5.cloned.1.call-done.refs_0_, bf16[1024,512]{1,0:T(8,128)(2,1)} %refs_1_.1, ...), custom_call_target="tpu_custom_call" | custom-call | flops 1000 | bytes 1000 | tf_op jit(solution)/shard_map/dense/pallas_call | solution.py:218
  98.2 3.8 %all-to-all-start.2 = ((bf16[8,32,1024]{2,1,0:T(8,128)(2,1)}), bf16[8,32,1024]{2,1,0:T(8,128)(2,1)S(1)}, u32[]{:S(2)}, u32[]{:S(2)}) async-start(bf16[8,32,1024]{2,1,0:T(8,128)(2,1)} %get-tuple-element.16), calls=%async_computation.2 | async-start | bytes 1048576 | tf_op jit(solution)/shard_map/all_to_all | solution.py:313
  102.0 8.7 %all-gather.1 = s32[4,4,16]{2,1,0:T(4,128)S(1)} all-gather(s32[1,4,16]{2,1,0:T(4,128)S(1)} %bitcast.55), channel_id=1, replica_groups=mesh['x'=4,'c'=2,'y'=4,'q'=4,'r'=4] {'y'}, dimensions={0}, use_global_device_ids=true | all-gather | bytes 1280 | tf_op jit(solution)/shard_map/all_gather | solution.py:311
  110.9 0.1 eq.76
  111.0 0.5 all-to-all-done.2.terms_ref
  111.5 1.2 embed.1
  112.7 8.0 %all-to-all-start.3 = ((bf16[32,32,128]{2,1,0:T(8,128)(2,1)}), bf16[32,32,128]{2,1,0:T(8,128)(2,1)S(1)}, u32[]{:S(2)}, u32[]{:S(2)}) async-start(bf16[32,32,128]{2,1,0:T(8,128)(2,1)} %embed.1), calls=%async_computation.3 | async-start | bytes 524288 | tf_op jit(solution)/shard_map/all_to_all | solution.py:318
  120.7 0.1 fusion.5
  120.8 1.3 slice.14
  122.1 0.8 slice.13
  122.9 0.1 copy.50
  123.0 0.1 reshape.133
  123.1 0.1 copy.51
  123.2 0.1 reduce_window_sum.14.last_ref
  123.3 6.2 %all-to-all-done.3 = bf16[32,32,128]{2,1,0:T(8,128)(2,1)S(1)} async-done(((bf16[32,32,128]{2,1,0:T(8,128)(2,1)}), bf16[32,32,128]{2,1,0:T(8,128)(2,1)S(1)}, u32[]{:S(2)}, u32[]{:S(2)}) %all-to-all-start.3) | async-done | bytes 262176 | tf_op jit(solution)/shard_map/all_to_all | solution.py:318
  129.5 2.0 %match.1 = f32[32,16,128]{2,1,0:T(8,128)} custom-call(s32[64]{0:T(128)S(1)} %convert_element_type.48.need_ref, s32[64]{0:T(128)S(1)} %sub.16.first_ref, s32[64]{0:T(128)S(1)} %reduce_window_sum.14.last_ref, bf16[1024,128]{1,0:T(8,128)(2,1)S(1)} %bitcast.35, bf16[4096,128]{1,0:T(8,128)(2,1)S(1)} %bitcast.31, s32[16,128]{1,0:T(8,128)S(1)} %pad.14.pick_ref), custom_call_target="tpu_custom_call" | custom-call | flops 1000 | bytes 1000 | tf_op jit(solution)/shard_map/match/pallas_call | solution.py:157
  131.5 6.0 %all-to-all-start.4 = ((f32[32,16,128]{2,1,0:T(8,128)}), f32[32,16,128]{2,1,0:T(8,128)S(1)}, u32[]{:S(2)}, u32[]{:S(2)}) async-start(f32[32,16,128]{2,1,0:T(8,128)} %match.1), calls=%async_computation.4 | async-start | bytes 524288 | tf_op jit(solution)/shard_map/all_to_all | solution.py:334
  137.5 0.6 constant_dynamic-slice_fusion
  138.1 8.2 %all-to-all-done.4.terms_ref = f32[32,16,128]{2,1,0:T(8,128)S(1)} async-done(((f32[32,16,128]{2,1,0:T(8,128)}), f32[32,16,128]{2,1,0:T(8,128)S(1)}, u32[]{:S(2)}, u32[]{:S(2)}) %all-to-all-start.4) | async-done | bytes 262176 | tf_op jit(solution)/shard_map/all_to_all | solution.py:334
  146.3 0.7 total.1
  (53 shorter events, 0.6 us)
Async XLA Ops:
  7.2 18.0 %copy-start = (bf16[1024,128]{1,0:T(8,128)(2,1)S(1)}, bf16[1024,128]{1,0:T(8,128)(2,1)}, u32[]{:S(2)}) copy-start(bf16[1024,128]{1,0:T(8,128)(2,1)} %param.21) | copy-start | bytes 786436
  7.2 19.3 %copy-start.4 = (bf16[4,64,1024]{2,1,0:T(8,128)(2,1)S(1)}, bf16[4,64,1024]{2,1,0:T(8,128)(2,1)}, u32[]{:S(2)}) copy-start(bf16[4,64,1024]{2,1,0:T(8,128)(2,1)} %param.18) | copy-start | bytes 1572868
  7.2 19.3 %copy-start.5 = (bf16[1024,128]{1,0:T(8,128)(2,1)S(1)}, bf16[1024,128]{1,0:T(8,128)(2,1)}, u32[]{:S(2)}) copy-start(bf16[1024,128]{1,0:T(8,128)(2,1)} %param.20) | copy-start | bytes 786436
  7.2 19.6 %copy-start.6 = (bf16[1024,128]{1,0:T(8,128)(2,1)S(1)}, bf16[1024,128]{1,0:T(8,128)(2,1)}, u32[]{:S(2)}) copy-start(bf16[1024,128]{1,0:T(8,128)(2,1)} %param.19) | copy-start | bytes 786436
  7.2 19.9 %copy-start.9 = (s32[4]{0:T(128)S(1)}, s32[4]{0:T(128)}, u32[]{:S(2)}) copy-start(s32[4]{0:T(128)} %param.32) | copy-start | bytes 52
  7.2 20.1 %copy-start.10 = (s32[1,4]{1,0:T(1,128)S(1)}, s32[1,4]{1,0:T(1,128)}, u32[]{:S(2)}) copy-start(s32[1,4]{1,0:T(1,128)} %param.34) | copy-start | bytes 52
  7.2 20.1 %copy-start.11 = (s32[16]{0:T(128)S(1)}, s32[16]{0:T(128)}, u32[]{:S(2)}) copy-start(s32[16]{0:T(128)} %param.31) | copy-start | bytes 196
  7.2 85.5 %all-gather.5.cloned.1.call-start = ((), (), s32[]{:S(2)}) async-start(), calls=%async_computation.5 | async-start | bytes 2359296 | tf_op jit(solution)/shard_map/all_gather | solution.py:270
  9.5 31.0 %all-to-all-start = ((bf16[4,256,128]{2,1,0:T(8,128)(2,1)}), bf16[4,256,128]{2,1,0:T(8,128)(2,1)S(1)}, u32[]{:S(2)}, u32[]{:S(2)}) async-start(bf16[4,256,128]{2,1,0:T(8,128)(2,1)} %broadcast_in_dim.62), calls=%async_computation | async-start | bytes 524288 | tf_op jit(solution)/shard_map/all_to_all | solution.py:29
  25.1 15.4 %copy-start.7 = (bf16[256,128]{1,0:T(8,128)(2,1)S(1)}, bf16[256,128]{1,0:T(8,128)(2,1)}, u32[]{:S(2)}) copy-start(bf16[256,128]{1,0:T(8,128)(2,1)} %param.33) | copy-start | bytes 196612
  25.1 95.7 %all-gather.7.cloned.1.call-start = ((), (), s32[]{:S(2)}) async-start(), calls=%async_computation.6 | async-start | bytes 1183744 | tf_op jit(solution)/shard_map/all_gather | solution.py:287
  25.1 28.6 %copy-start.12 = (s32[128]{0:T(128)S(1)}, s32[128]{0:T(128)}, u32[]{:S(2)}) copy-start(s32[128]{0:T(128)} %param.30) | copy-start | bytes 1540
  40.5 52.2 %copy-start.3 = (f32[1024]{0:T(1024)S(1)}, f32[1024]{0:T(1024)}, u32[]{:S(2)}) copy-start(f32[1024]{0:T(1024)} %param.23) | copy-start | bytes 12292
  41.2 13.6 %collective-permute-start = (bf16[1024,128]{1,0:T(8,128)(2,1)S(1)}, bf16[1024,128]{1,0:T(8,128)(2,1)S(1)}, u32[]{:S(2)}, u32[]{:S(2)}) collective-permute-start(bf16[1024,128]{1,0:T(8,128)(2,1)S(1)} %bitcast.37), channel_id=1, source_target_pairs={{1,0},{2,1},{3,2},{4,3},{5,4},{6,5},{7,6},{8,7},{9,8},{10,9},{11,1... | collective-permute-start | bytes 786440 | tf_op jit(solution)/shard_map/ppermute | solution.py:33
  47.5 11.0 %collective-permute-start.1 = (bf16[1024,128]{1,0:T(8,128)(2,1)S(1)}, bf16[1024,128]{1,0:T(8,128)(2,1)S(1)}, u32[]{:S(2)}, u32[]{:S(2)}) collective-permute-start(bf16[1024,128]{1,0:T(8,128)(2,1)S(1)} %bitcast.38), channel_id=1, source_target_pairs={{2,0},{15,1},{4,2},{1,3},{6,4},{3,5},{8,6},{5,7},{10,8},{7,9},{12,... | collective-permute-start | bytes 786440 | tf_op jit(solution)/shard_map/ppermute | solution.py:281
  50.8 11.9 %collective-permute-start.2 = (bf16[1024,128]{1,0:T(8,128)(2,1)S(1)}, bf16[1024,128]{1,0:T(8,128)(2,1)S(1)}, u32[]{:S(2)}, u32[]{:S(2)}) collective-permute-start(bf16[1024,128]{1,0:T(8,128)(2,1)S(1)} %bitcast.39), channel_id=1, source_target_pairs={{15,0},{0,1},{1,2},{2,3},{3,4},{4,5},{5,6},{6,7},{7,8},{8,9},{9,10... | collective-permute-start | bytes 786440 | tf_op jit(solution)/shard_map/ppermute | solution.py:33
  92.7 9.3 %copy-start.8 = (s32[4,16]{1,0:T(4,128)S(1)}, s32[4,16]{1,0:T(4,128)}, u32[]{:S(2)}) copy-start(s32[4,16]{1,0:T(4,128)} %param.35) | copy-start | bytes 772
  92.7 18.8 %copy-start.1 = (bf16[1024,128]{1,0:T(8,128)(2,1)S(1)}, bf16[1024,128]{1,0:T(8,128)(2,1)}, u32[]{:S(2)}) copy-start(bf16[1024,128]{1,0:T(8,128)(2,1)} %w_project_ref.1) | copy-start | bytes 786436
  92.7 18.8 %copy-start.2 = (f32[1024]{0:T(1024)S(1)}, f32[1024]{0:T(1024)}, u32[]{:S(2)}) copy-start(f32[1024]{0:T(1024)} %param.26) | copy-start | bytes 12292
  98.2 13.3 %all-to-all-start.2 = ((bf16[8,32,1024]{2,1,0:T(8,128)(2,1)}), bf16[8,32,1024]{2,1,0:T(8,128)(2,1)S(1)}, u32[]{:S(2)}, u32[]{:S(2)}) async-start(bf16[8,32,1024]{2,1,0:T(8,128)(2,1)} %get-tuple-element.16), calls=%async_computation.2 | async-start | bytes 1048576 | tf_op jit(solution)/shard_map/all_to_all | solution.py:313
  112.7 16.8 %all-to-all-start.3 = ((bf16[32,32,128]{2,1,0:T(8,128)(2,1)}), bf16[32,32,128]{2,1,0:T(8,128)(2,1)S(1)}, u32[]{:S(2)}, u32[]{:S(2)}) async-start(bf16[32,32,128]{2,1,0:T(8,128)(2,1)} %embed.1), calls=%async_computation.3 | async-start | bytes 524288 | tf_op jit(solution)/shard_map/all_to_all | solution.py:318
  131.5 14.8 %all-to-all-start.4 = ((f32[32,16,128]{2,1,0:T(8,128)}), f32[32,16,128]{2,1,0:T(8,128)S(1)}, u32[]{:S(2)}, u32[]{:S(2)}) async-start(f32[32,16,128]{2,1,0:T(8,128)} %match.1), calls=%async_computation.4 | async-start | bytes 524288 | tf_op jit(solution)/shard_map/all_to_all | solution.py:334
Sparse Core Ops, SparseCore 0:
  10.2 38.5 all-gather.4
  50.9 61.8 all-gather.6

commit v12 on v9

--- a/solution.py
+++ b/solution.py
@@ -77,15 +77,15 @@
         mixed = mixed / total
         return jnp.where(low_half, mixed[:QL], mixed[QL:]).astype(BF)
 
-    def two_requests(step, carry):
-        i = order_ref[2 * step]
-        k = order_ref[jnp.where(2 * step + 1 < count, 2 * step + 1, 2 * step)]
-        results = [one_request(i), one_request(k)]
-        for j, result in zip((i, k), results):
+    def some_requests(step, carry):
+        places = [4 * step + j for j in range(4)]
+        picked = [order_ref[jnp.where(place < count, place, 4 * step)] for place in places]
+        results = [one_request(i) for i in picked]
+        for j, result in zip(picked, results):
             out_ref[j // RQ, pl.ds(pl.multiple_of((j % RQ) * QL, QL), QL), :] = result
         return carry
 
-    lax.fori_loop(0, (count + 1) // 2, two_requests, 0)
+    lax.fori_loop(0, (count + 3) // 4, some_requests, 0)
 
 
 def attend(groups, rows, prompt, bias):

time: 153 us -> 153 us (level)
  Pallas kernels: 14.5 us -> 12.3 us
where the time goes in v12:
time: 153 us; the launch traced here: 151 us
  blocking collectives  41 us (27%)
  starting transfers between devices  40.2 us (26%)
  waiting for transfers between devices  32.7 us (21%)
  between operations  14.3 us (9%)
  Pallas kernels  12.3 us (8%)
  local copies, waits for them, and re-layouts  4.98 us (3%)
  other arithmetic  3.61 us (2%)
  matrix products  1.92 us (1%)
    all_gather x1, blocking collectives, per_device(): context = lax.all_gather(context, HEAD, axis=0, tiled=False)  20.1 us
    all_to_all x1, starting transfers between devices, spread(): lax.all_to_all(wide, axes, 0, 0, tiled=True)  15.6 us
    all_gather x1, blocking collectives, per_device(): rows = lax.all_gather(rows, 'y', axis=0, tiled=True)  12.9 us
    ppermute x3, starting transfers between devices, from_ahead(): lax.ppermute(block, ('q', 'r'), [((i + step) % 16, i) for i in range(16)])  11.7 us
    all_to_all x1, waiting for transfers between devices, per_device(): terms = lax.all_to_all(terms, HEAD, 0, 0, tiled=True)  9.11 us
    ppermute x3, waiting for transfers between devices, from_ahead(): lax.ppermute(block, ('q', 'r'), [((i + step) % 16, i) for i in range(16)])  8.41 us
    all_to_all x1, waiting for transfers between devices, per_device(): terms = lax.all_to_all(terms, HEAD + ('y',), 0, 0, tiled=True)  8.16 us
    all_to_all x1, blocking collectives, per_device(): back = lax.all_to_all(mixed, 'y', 0, 0, tiled=True)  7.97 us
  transfers between devices with their start and end apart: 9, of which 4 were waited for; matrix products, arithmetic and copies ran while one was open for 7% of the time, Pallas kernels for 6%

profile of v12, /device:TPU:1, one launch (start us, length us, event | category | flops | bytes accessed | tf_op | source)
XLA Modules:
  0.0 151.0 jit_solution(16169835472762973065)
XLA Ops:
  7.3 0.7 all-gather.4.cloned.1.call-update
  8.0 0.8 pad_maximum_fusion.1
  8.7 0.7 broadcast_in_dim.65
  9.5 15.6 %all-to-all-start = ((bf16[4,256,128]{2,1,0:T(8,128)(2,1)}), bf16[4,256,128]{2,1,0:T(8,128)(2,1)S(1)}, u32[]{:S(2)}, u32[]{:S(2)}) async-start(bf16[4,256,128]{2,1,0:T(8,128)(2,1)} %broadcast_in_dim.65), calls=%async_computation | async-start | bytes 524288 | tf_op jit(solution)/shard_map/all_to_all | solution.py:29
  25.1 0.7 convert_bitcast_fusion
  25.8 0.7 fusion.14
  26.5 1.3 convolution_convert_fusion
  27.9 0.3 convolution_convert_fusion.1
  28.2 0.3 fusion
  28.5 0.1 copy.39
  28.6 0.1 add.104
  28.7 0.1 dynamic_slice.10
  28.8 0.1 fusion.13
  28.9 0.1 iota_compare_fusion.4
  29.0 12.9 %all_gather.15 = bf16[3136,128]{1,0:T(8,128)(2,1)S(1)} all-gather(bf16[784,128]{1,0:T(8,128)(2,1)S(1)} %pad_maximum_fusion), channel_id=1, replica_groups=mesh['x'=4,'c'=2,'y'=4,'q'=4,'r'=4] {'y'}, dimensions={0}, use_global_device_ids=true | all-gather | bytes 1003520 | tf_op jit(solution)/shard_map/all_gather | solution.py:278
  41.9 0.6 fusion.2
  42.6 6.3 %collective-permute-start = (bf16[1024,128]{1,0:T(8,128)(2,1)S(1)}, bf16[1024,128]{1,0:T(8,128)(2,1)S(1)}, u32[]{:S(2)}, u32[]{:S(2)}) collective-permute-start(bf16[1024,128]{1,0:T(8,128)(2,1)S(1)} %bitcast.36), channel_id=1, source_target_pairs={{1,0},{2,1},{3,2},{4,3},{5,4},{6,5},{7,6},{8,7},{9,8},{10,9},{11,1... | collective-permute-start | bytes 786440 | tf_op jit(solution)/shard_map/ppermute | solution.py:33
  48.9 2.7 %collective-permute-start.1 = (bf16[1024,128]{1,0:T(8,128)(2,1)S(1)}, bf16[1024,128]{1,0:T(8,128)(2,1)S(1)}, u32[]{:S(2)}, u32[]{:S(2)}) collective-permute-start(bf16[1024,128]{1,0:T(8,128)(2,1)S(1)} %bitcast.37), channel_id=1, source_target_pairs={{2,0},{3,1},{4,2},{5,3},{6,4},{7,5},{8,6},{9,7},{10,8},{11,9},{12,... | collective-permute-start | bytes 786440 | tf_op jit(solution)/shard_map/ppermute | solution.py:33
  51.6 2.7 %collective-permute-start.2 = (bf16[1024,128]{1,0:T(8,128)(2,1)S(1)}, bf16[1024,128]{1,0:T(8,128)(2,1)S(1)}, u32[]{:S(2)}, u32[]{:S(2)}) collective-permute-start(bf16[1024,128]{1,0:T(8,128)(2,1)S(1)} %bitcast.38), channel_id=1, source_target_pairs={{15,0},{0,1},{1,2},{2,3},{3,4},{4,5},{5,6},{6,7},{7,8},{8,9},{9,10... | collective-permute-start | bytes 786440 | tf_op jit(solution)/shard_map/ppermute | solution.py:33
  54.3 0.1 dynamic_slice.9
  54.4 0.1 eq.70
  54.5 0.2 select_reduce_fusion.1
  54.8 0.1 add.102
  54.9 0.1 select_reduce_fusion
  55.1 0.2 slice_reduce_fusion
  55.3 8.4 %collective-permute-done.1.refs_2_ = bf16[1024,128]{1,0:T(8,128)(2,1)S(1)} collective-permute-done((bf16[1024,128]{1,0:T(8,128)(2,1)S(1)}, bf16[1024,128]{1,0:T(8,128)(2,1)S(1)}, u32[]{:S(2)}, u32[]{:S(2)}) %collective-permute-start.1) | collective-permute-done | bytes 262176 | tf_op jit(solution)/shard_map/ppermute | solution.py:33
  63.7 2.1 %attend.1 = bf16[4,256,128]{2,1,0:T(8,128)(2,1)S(1)} custom-call(s32[16]{0:T(128)S(1)} %compare_select_fusion.3.group_ref, bf16[4,784,128]{2,1,0:T(8,128)(2,1)S(1)} %bitcast.32, f32[4,1,512]{2,1,0:T(1,128)S(1)} %bitcast.40, bf16[1024,128]{1,0:T(8,128)(2,1)S(1)} %bitcast.39, bf16[1024,128]{1,0:T(8,128)(2,1)S(1)} %collective-permute-done.refs_1_, ...), custom_call_target="tpu_custom_call" | custom-call | flops 1000 | bytes 1000 | tf_op jit(solution)/shard_map/attend/pallas_call | solution.py:92
  65.8 8.0 %all_to_all.25 = bf16[4,256,128]{2,1,0:T(8,128)(2,1)S(1)} all-to-all(bf16[4,256,128]{2,1,0:T(8,128)(2,1)S(1)} %attend.1), channel_id=1, replica_groups=mesh['x'=4,'c'=2,'y'=4,'q'=4,'r'=4] {'y'}, dimensions={0} | all-to-all | bytes 524288 | tf_op jit(solution)/shard_map/all_to_all | solution.py:307
  73.8 20.1 %all-gather = bf16[2048,128]{1,0:T(8,128)(2,1)S(1)} all-gather(bf16[256,128]{1,0:T(8,128)(2,1)S(1)} %reduce_sum.32), channel_id=2, replica_groups=mesh['x'=4,'c'=2,'y'=4,'q'=4,'r'=4] {'x','c'}, dimensions={0}, use_global_device_ids=true | all-gather | bytes 589824 | tf_op jit(solution)/shard_map/all_gather | solution.py:309
  93.9 5.4 %dense.1 = (bf16[256,1024]{1,0:T(8,128)(2,1)S(1)}, bf16[8,32,1024]{2,1,0:T(8,128)(2,1)}) custom-call(bf16[8,256,128]{2,1,0:T(8,128)(2,1)S(1)} %bitcast.33, bf16[256,1024]{1,0:T(8,128)(2,1)} %bitcast.44, f32[1,1024]{1,0:T(1,128)S(1)} %bitcast.42, bf16[1024,1024]{1,0:T(8,128)(2,1)} %all-gather.4.cloned.1.call-done.refs_0_, bf16[1024,512]{1,0:T(8,128)(2,1)} %refs_1_.1, ...), custom_call_target="tpu_custom_call" | custom-call | flops 1000 | bytes 1000 | tf_op jit(solution)/shard_map/dense/pallas_call | solution.py:218
  99.3 3.9 %all-to-all-start.2 = ((bf16[8,32,1024]{2,1,0:T(8,128)(2,1)}), bf16[8,32,1024]{2,1,0:T(8,128)(2,1)S(1)}, u32[]{:S(2)}, u32[]{:S(2)}) async-start(bf16[8,32,1024]{2,1,0:T(8,128)(2,1)} %get-tuple-element.13), calls=%async_computation.2 | async-start | bytes 1048576 | tf_op jit(solution)/shard_map/all_to_all | solution.py:311
  103.5 0.1 eq.76
  103.6 9.1 %all-to-all-done.2.terms_ref = bf16[8,32,1024]{2,1,0:T(8,128)(2,1)S(1)} async-done(((bf16[8,32,1024]{2,1,0:T(8,128)(2,1)}), bf16[8,32,1024]{2,1,0:T(8,128)(2,1)S(1)}, u32[]{:S(2)}, u32[]{:S(2)}) %all-to-all-start.2) | async-done | bytes 524320 | tf_op jit(solution)/shard_map/all_to_all | solution.py:311
  112.7 1.2 embed.1
  113.9 4.4 %all-to-all-start.3 = ((bf16[32,32,128]{2,1,0:T(8,128)(2,1)}), bf16[32,32,128]{2,1,0:T(8,128)(2,1)S(1)}, u32[]{:S(2)}, u32[]{:S(2)}) async-start(bf16[32,32,128]{2,1,0:T(8,128)(2,1)} %embed.1), calls=%async_computation.3 | async-start | bytes 524288 | tf_op jit(solution)/shard_map/all_to_all | solution.py:316
  118.3 0.1 fusion.3
  118.4 1.3 slice.30
  119.7 0.8 slice.29
  120.5 0.1 copy.44
  120.6 0.1 reshape.134
  120.7 0.1 copy.45
  120.8 0.1 reduce_window_sum.14.last_ref
  120.9 6.3 %all-to-all-done.3 = bf16[32,32,128]{2,1,0:T(8,128)(2,1)S(1)} async-done(((bf16[32,32,128]{2,1,0:T(8,128)(2,1)}), bf16[32,32,128]{2,1,0:T(8,128)(2,1)S(1)}, u32[]{:S(2)}, u32[]{:S(2)}) %all-to-all-start.3) | async-done | bytes 262176 | tf_op jit(solution)/shard_map/all_to_all | solution.py:316
  127.2 2.9 %match.1 = f32[32,16,128]{2,1,0:T(8,128)} custom-call(s32[64]{0:T(128)S(1)} %convert_element_type.45.need_ref, s32[64]{0:T(128)S(1)} %sub.16.first_ref, s32[64]{0:T(128)S(1)} %reduce_window_sum.14.last_ref, bf16[1024,128]{1,0:T(8,128)(2,1)S(1)} %bitcast.34, bf16[4096,128]{1,0:T(8,128)(2,1)S(1)} %bitcast.30, s32[16,128]{1,0:T(8,128)S(1)} %pad.14.pick_ref), custom_call_target="tpu_custom_call" | custom-call | flops 1000 | bytes 1000 | tf_op jit(solution)/shard_map/match/pallas_call | solution.py:157
  130.0 4.6 %all-to-all-start.4 = ((f32[32,16,128]{2,1,0:T(8,128)}), f32[32,16,128]{2,1,0:T(8,128)S(1)}, u32[]{:S(2)}, u32[]{:S(2)}) async-start(f32[32,16,128]{2,1,0:T(8,128)} %match.1), calls=%async_computation.4 | async-start | bytes 524288 | tf_op jit(solution)/shard_map/all_to_all | solution.py:332
  134.6 0.6 constant_dynamic-slice_fusion
  135.3 8.2 %all-to-all-done.4.terms_ref = f32[32,16,128]{2,1,0:T(8,128)S(1)} async-done(((f32[32,16,128]{2,1,0:T(8,128)}), f32[32,16,128]{2,1,0:T(8,128)S(1)}, u32[]{:S(2)}, u32[]{:S(2)}) %all-to-all-start.4) | async-done | bytes 262176 | tf_op jit(solution)/shard_map/all_to_all | solution.py:332
  143.4 0.7 total.1
  (52 shorter events, 0.8 us)
Async XLA Ops:
  7.2 19.3 %copy-start = (bf16[1024,128]{1,0:T(8,128)(2,1)S(1)}, bf16[1024,128]{1,0:T(8,128)(2,1)}, u32[]{:S(2)}) copy-start(bf16[1024,128]{1,0:T(8,128)(2,1)} %param.21) | copy-start | bytes 786436
  7.2 20.7 %copy-start.4 = (bf16[4,64,1024]{2,1,0:T(8,128)(2,1)S(1)}, bf16[4,64,1024]{2,1,0:T(8,128)(2,1)}, u32[]{:S(2)}) copy-start(bf16[4,64,1024]{2,1,0:T(8,128)(2,1)} %param.18) | copy-start | bytes 1572868
  7.2 20.7 %copy-start.5 = (bf16[1024,128]{1,0:T(8,128)(2,1)S(1)}, bf16[1024,128]{1,0:T(8,128)(2,1)}, u32[]{:S(2)}) copy-start(bf16[1024,128]{1,0:T(8,128)(2,1)} %param.20) | copy-start | bytes 786436
  7.2 21.0 %copy-start.6 = (bf16[1024,128]{1,0:T(8,128)(2,1)S(1)}, bf16[1024,128]{1,0:T(8,128)(2,1)}, u32[]{:S(2)}) copy-start(bf16[1024,128]{1,0:T(8,128)(2,1)} %param.19) | copy-start | bytes 786436
  7.2 21.5 %copy-start.8 = (s32[1,4]{1,0:T(1,128)S(1)}, s32[1,4]{1,0:T(1,128)}, u32[]{:S(2)}) copy-start(s32[1,4]{1,0:T(1,128)} %param.34) | copy-start | bytes 52
  7.2 21.5 %copy-start.9 = (s32[16]{0:T(128)S(1)}, s32[16]{0:T(128)}, u32[]{:S(2)}) copy-start(s32[16]{0:T(128)} %param.31) | copy-start | bytes 196
  7.2 86.7 %all-gather.4.cloned.1.call-start = ((), (), s32[]{:S(2)}) async-start(), calls=%async_computation.5 | async-start | bytes 2359296 | tf_op jit(solution)/shard_map/all_gather | solution.py:270
  9.5 32.4 %all-to-all-start = ((bf16[4,256,128]{2,1,0:T(8,128)(2,1)}), bf16[4,256,128]{2,1,0:T(8,128)(2,1)S(1)}, u32[]{:S(2)}, u32[]{:S(2)}) async-start(bf16[4,256,128]{2,1,0:T(8,128)(2,1)} %broadcast_in_dim.65), calls=%async_computation | async-start | bytes 524288 | tf_op jit(solution)/shard_map/all_to_all | solution.py:29
  25.1 16.8 %copy-start.7 = (bf16[256,128]{1,0:T(8,128)(2,1)S(1)}, bf16[256,128]{1,0:T(8,128)(2,1)}, u32[]{:S(2)}) copy-start(bf16[256,128]{1,0:T(8,128)(2,1)} %param.33) | copy-start | bytes 196612
  25.1 93.3 %all-gather.6.cloned.1.call-start = ((), (), s32[]{:S(2)}) async-start(), calls=%async_computation.6 | async-start | bytes 1183744 | tf_op jit(solution)/shard_map/all_gather | solution.py:287
  26.5 27.8 %copy-start.10 = (s32[128]{0:T(128)S(1)}, s32[128]{0:T(128)}, u32[]{:S(2)}) copy-start(s32[128]{0:T(128)} %param.30) | copy-start | bytes 1540
  41.9 52.0 %copy-start.3 = (f32[1024]{0:T(1024)S(1)}, f32[1024]{0:T(1024)}, u32[]{:S(2)}) copy-start(f32[1024]{0:T(1024)} %param.23) | copy-start | bytes 12292
  42.6 12.7 %collective-permute-start = (bf16[1024,128]{1,0:T(8,128)(2,1)S(1)}, bf16[1024,128]{1,0:T(8,128)(2,1)S(1)}, u32[]{:S(2)}, u32[]{:S(2)}) collective-permute-start(bf16[1024,128]{1,0:T(8,128)(2,1)S(1)} %bitcast.36), channel_id=1, source_target_pairs={{1,0},{2,1},{3,2},{4,3},{5,4},{6,5},{7,6},{8,7},{9,8},{10,9},{11,1... | collective-permute-start | bytes 786440 | tf_op jit(solution)/shard_map/ppermute | solution.py:33
  48.9 14.8 %collective-permute-start.1 = (bf16[1024,128]{1,0:T(8,128)(2,1)S(1)}, bf16[1024,128]{1,0:T(8,128)(2,1)S(1)}, u32[]{:S(2)}, u32[]{:S(2)}) collective-permute-start(bf16[1024,128]{1,0:T(8,128)(2,1)S(1)} %bitcast.37), channel_id=1, source_target_pairs={{2,0},{3,1},{4,2},{5,3},{6,4},{7,5},{8,6},{9,7},{10,8},{11,9},{12,... | collective-permute-start | bytes 786440 | tf_op jit(solution)/shard_map/ppermute | solution.py:33
  51.6 12.1 %collective-permute-start.2 = (bf16[1024,128]{1,0:T(8,128)(2,1)S(1)}, bf16[1024,128]{1,0:T(8,128)(2,1)S(1)}, u32[]{:S(2)}, u32[]{:S(2)}) collective-permute-start(bf16[1024,128]{1,0:T(8,128)(2,1)S(1)} %bitcast.38), channel_id=1, source_target_pairs={{15,0},{0,1},{1,2},{2,3},{3,4},{4,5},{5,6},{6,7},{7,8},{8,9},{9,10... | collective-permute-start | bytes 786440 | tf_op jit(solution)/shard_map/ppermute | solution.py:33
  93.9 18.8 %copy-start.1 = (bf16[1024,128]{1,0:T(8,128)(2,1)S(1)}, bf16[1024,128]{1,0:T(8,128)(2,1)}, u32[]{:S(2)}) copy-start(bf16[1024,128]{1,0:T(8,128)(2,1)} %w_project_ref.1) | copy-start | bytes 786436
  93.9 18.8 %copy-start.2 = (f32[1024]{0:T(1024)S(1)}, f32[1024]{0:T(1024)}, u32[]{:S(2)}) copy-start(f32[1024]{0:T(1024)} %param.26) | copy-start | bytes 12292
  99.3 13.3 %all-to-all-start.2 = ((bf16[8,32,1024]{2,1,0:T(8,128)(2,1)}), bf16[8,32,1024]{2,1,0:T(8,128)(2,1)S(1)}, u32[]{:S(2)}, u32[]{:S(2)}) async-start(bf16[8,32,1024]{2,1,0:T(8,128)(2,1)} %get-tuple-element.13), calls=%async_computation.2 | async-start | bytes 1048576 | tf_op jit(solution)/shard_map/all_to_all | solution.py:311
  113.9 13.3 %all-to-all-start.3 = ((bf16[32,32,128]{2,1,0:T(8,128)(2,1)}), bf16[32,32,128]{2,1,0:T(8,128)(2,1)S(1)}, u32[]{:S(2)}, u32[]{:S(2)}) async-start(bf16[32,32,128]{2,1,0:T(8,128)(2,1)} %embed.1), calls=%async_computation.3 | async-start | bytes 524288 | tf_op jit(solution)/shard_map/all_to_all | solution.py:316
  130.0 13.4 %all-to-all-start.4 = ((f32[32,16,128]{2,1,0:T(8,128)}), f32[32,16,128]{2,1,0:T(8,128)S(1)}, u32[]{:S(2)}, u32[]{:S(2)}) async-start(f32[32,16,128]{2,1,0:T(8,128)} %match.1), calls=%async_computation.4 | async-start | bytes 524288 | tf_op jit(solution)/shard_map/all_to_all | solution.py:332
Sparse Core Ops, SparseCore 0:
  10.2 38.5 all-gather.3
  50.9 61.7 all-gather.5

commit v13 on v12

--- a/solution.py
+++ b/solution.py
@@ -278,7 +278,8 @@
     rows = lax.all_gather(rows, "y", axis=0, tiled=True)
     pages_q, rows = lax.optimization_barrier((pages_q, rows))
     pages_q = pages_q.reshape(1024, 128)
-    ahead_two = from_ahead(pages_q, 2)
+    pairs = [((i + 2 if i % 2 == 0 else i - 2) % 16, i) for i in range(16)]
+    ahead_two = lax.ppermute(pages_q, ("q", "r"), pairs)
     prompt = [pages_q, from_ahead(pages_q, 1), ahead_two, from_ahead(pages_q, -1)]
 
     doc_vectors, page_table, pages_q = lax.optimization_barrier((doc_vectors, page_table, pages_q))

time: 153 us -> 153 us (level)
  blocking collectives: 41 us -> 37.7 us
  starting transfers between devices: 40.2 us -> 43.4 us
    ppermute x0 -> x1, waiting for transfers between devices: none -> 5.38 us  [per_device(): ahead_two = lax.ppermute(pages_q, ('q', 'r'), pairs)]
    ppermute x3 -> x2, waiting for transfers between devices: 8.41 us -> 3.04 us  [from_ahead(): lax.ppermute(block, ('q', 'r'), [((i + step) % 16, i) for i in range(16)])]
    all_to_all x1, starting transfers between devices: 4.56 us -> 8.31 us  [per_device(): terms = lax.all_to_all(terms, HEAD + ('y',), 0, 0, tiled=True)]
    ppermute x3 -> x2, starting transfers between devices: 11.7 us -> 8.42 us  [from_ahead(): lax.ppermute(block, ('q', 'r'), [((i + step) % 16, i) for i in range(16)])]
    all_gather x1, blocking collectives: 20.1 us -> 16.8 us  [per_device(): context = lax.all_gather(context, HEAD, axis=0, tiled=False)]
    ppermute x0 -> x1, starting transfers between devices: none -> 2.69 us  [per_device(): ahead_two = lax.ppermute(pages_q, ('q', 'r'), pairs)]
    pallas_call x1, Pallas kernels: 2.14 us -> 3.71 us  [attend(): pl.pallas_call(attend_kernel, out_shape=jax.ShapeDtypeStruct((4, NROW, 12...]
  transfers between devices with their start and end apart: 9 -> 9, of which waited for: 4 -> 5; matrix products, arithmetic and copies ran while one was open for 7% -> 7% of each run, Pallas kernels for 6% -> 7%
where the time goes in v13:
time: 153 us; the launch traced here: 152 us
  starting transfers between devices  43.4 us (28%)
  blocking collectives  37.7 us (25%)
  waiting for transfers between devices  32.7 us (21%)
  between operations  14.3 us (9%)
  Pallas kernels  13.5 us (9%)
  local copies, waits for them, and re-layouts  4.98 us (3%)
  other arithmetic  3.61 us (2%)
  matrix products  1.92 us (1%)
    all_gather x1, blocking collectives, per_device(): context = lax.all_gather(context, HEAD, axis=0, tiled=False)  16.8 us
    all_to_all x1, starting transfers between devices, spread(): lax.all_to_all(wide, axes, 0, 0, tiled=True)  15.6 us
    all_gather x1, blocking collectives, per_device(): rows = lax.all_gather(rows, 'y', axis=0, tiled=True)  12.9 us
    all_to_all x1, waiting for transfers between devices, per_device(): terms = lax.all_to_all(terms, HEAD, 0, 0, tiled=True)  9.11 us
    ppermute x2, starting transfers between devices, from_ahead(): lax.ppermute(block, ('q', 'r'), [((i + step) % 16, i) for i in range(16)])  8.42 us
    all_to_all x1, starting transfers between devices, per_device(): terms = lax.all_to_all(terms, HEAD + ('y',), 0, 0, tiled=True)  8.31 us
    all_to_all x1, waiting for transfers between devices, per_device(): terms = lax.all_to_all(terms, HEAD + ('y',), 0, 0, tiled=True)  8.16 us
    all_to_all x1, blocking collectives, per_device(): back = lax.all_to_all(mixed, 'y', 0, 0, tiled=True)  7.92 us
  transfers between devices with their start and end apart: 9, of which 5 were waited for; matrix products, arithmetic and copies ran while one was open for 7% of the time, Pallas kernels for 7%

profile of v13, /device:TPU:1, one launch (start us, length us, event | category | flops | bytes accessed | tf_op | source)
XLA Modules:
  0.0 152.0 jit_solution(10129372228374756024)
XLA Ops:
  7.3 0.7 all-gather.4.cloned.1.call-update
  8.0 0.8 pad_maximum_fusion.1
  8.7 0.7 broadcast_in_dim.65
  9.5 15.6 %all-to-all-start = ((bf16[4,256,128]{2,1,0:T(8,128)(2,1)}), bf16[4,256,128]{2,1,0:T(8,128)(2,1)S(1)}, u32[]{:S(2)}, u32[]{:S(2)}) async-start(bf16[4,256,128]{2,1,0:T(8,128)(2,1)} %broadcast_in_dim.65), calls=%async_computation | async-start | bytes 524288 | tf_op jit(solution)/shard_map/all_to_all | solution.py:29
  25.1 0.7 convert_bitcast_fusion
  25.8 0.7 fusion.14
  26.5 1.3 convolution_convert_fusion
  27.9 0.3 convolution_convert_fusion.1
  28.2 0.3 fusion
  28.5 0.1 copy.39
  28.6 0.1 add.104
  28.7 0.1 dynamic_slice.10
  28.8 0.1 fusion.13
  29.0 12.9 %all_gather.15 = bf16[3136,128]{1,0:T(8,128)(2,1)S(1)} all-gather(bf16[784,128]{1,0:T(8,128)(2,1)S(1)} %pad_maximum_fusion), channel_id=1, replica_groups=mesh['x'=4,'c'=2,'y'=4,'q'=4,'r'=4] {'y'}, dimensions={0}, use_global_device_ids=true | all-gather | bytes 1003520 | tf_op jit(solution)/shard_map/all_gather | solution.py:278
  41.9 0.6 fusion.2
  42.6 6.3 %collective-permute-start = (bf16[1024,128]{1,0:T(8,128)(2,1)S(1)}, bf16[1024,128]{1,0:T(8,128)(2,1)S(1)}, u32[]{:S(2)}, u32[]{:S(2)}) collective-permute-start(bf16[1024,128]{1,0:T(8,128)(2,1)S(1)} %bitcast.36), channel_id=1, source_target_pairs={{1,0},{2,1},{3,2},{4,3},{5,4},{6,5},{7,6},{8,7},{9,8},{10,9},{11,1... | collective-permute-start | bytes 786440 | tf_op jit(solution)/shard_map/ppermute | solution.py:33
  48.9 2.7 %collective-permute-start.1 = (bf16[1024,128]{1,0:T(8,128)(2,1)S(1)}, bf16[1024,128]{1,0:T(8,128)(2,1)S(1)}, u32[]{:S(2)}, u32[]{:S(2)}) collective-permute-start(bf16[1024,128]{1,0:T(8,128)(2,1)S(1)} %bitcast.37), channel_id=1, source_target_pairs={{2,0},{15,1},{4,2},{1,3},{6,4},{3,5},{8,6},{5,7},{10,8},{7,9},{12,... | collective-permute-start | bytes 786440 | tf_op jit(solution)/shard_map/ppermute | solution.py:282
  51.6 2.1 %collective-permute-start.2 = (bf16[1024,128]{1,0:T(8,128)(2,1)S(1)}, bf16[1024,128]{1,0:T(8,128)(2,1)S(1)}, u32[]{:S(2)}, u32[]{:S(2)}) collective-permute-start(bf16[1024,128]{1,0:T(8,128)(2,1)S(1)} %bitcast.38), channel_id=1, source_target_pairs={{15,0},{0,1},{1,2},{2,3},{3,4},{4,5},{5,6},{6,7},{7,8},{8,9},{9,10... | collective-permute-start | bytes 786440 | tf_op jit(solution)/shard_map/ppermute | solution.py:33
  53.7 0.1 dynamic_slice.9
  53.8 0.1 eq.70
  53.9 0.2 select_reduce_fusion.1
  54.2 0.1 add.102
  54.3 0.1 select_reduce_fusion
  54.5 0.2 slice_reduce_fusion
  54.7 5.4 %collective-permute-done.1.refs_2_ = bf16[1024,128]{1,0:T(8,128)(2,1)S(1)} collective-permute-done((bf16[1024,128]{1,0:T(8,128)(2,1)S(1)}, bf16[1024,128]{1,0:T(8,128)(2,1)S(1)}, u32[]{:S(2)}, u32[]{:S(2)}) %collective-permute-start.1) | collective-permute-done | bytes 262176 | tf_op jit(solution)/shard_map/ppermute | solution.py:282
  60.0 3.0 %collective-permute-done.2.refs_3_ = bf16[1024,128]{1,0:T(8,128)(2,1)S(1)} collective-permute-done((bf16[1024,128]{1,0:T(8,128)(2,1)S(1)}, bf16[1024,128]{1,0:T(8,128)(2,1)S(1)}, u32[]{:S(2)}, u32[]{:S(2)}) %collective-permute-start.2) | collective-permute-done | bytes 262176 | tf_op jit(solution)/shard_map/ppermute | solution.py:33
  63.1 3.7 %attend.1 = bf16[4,256,128]{2,1,0:T(8,128)(2,1)S(1)} custom-call(s32[16]{0:T(128)S(1)} %compare_select_fusion.3.group_ref, bf16[4,784,128]{2,1,0:T(8,128)(2,1)S(1)} %bitcast.32, f32[4,1,512]{2,1,0:T(1,128)S(1)} %bitcast.40, bf16[1024,128]{1,0:T(8,128)(2,1)S(1)} %bitcast.39, bf16[1024,128]{1,0:T(8,128)(2,1)S(1)} %collective-permute-done.refs_1_, ...), custom_call_target="tpu_custom_call" | custom-call | flops 1000 | bytes 1000 | tf_op jit(solution)/shard_map/attend/pallas_call | solution.py:92
  66.8 7.9 %all_to_all.25 = bf16[4,256,128]{2,1,0:T(8,128)(2,1)S(1)} all-to-all(bf16[4,256,128]{2,1,0:T(8,128)(2,1)S(1)} %attend.1), channel_id=1, replica_groups=mesh['x'=4,'c'=2,'y'=4,'q'=4,'r'=4] {'y'}, dimensions={0} | all-to-all | bytes 524288 | tf_op jit(solution)/shard_map/all_to_all | solution.py:308
  74.8 16.8 %all-gather = bf16[2048,128]{1,0:T(8,128)(2,1)S(1)} all-gather(bf16[256,128]{1,0:T(8,128)(2,1)S(1)} %reduce_sum.32), channel_id=2, replica_groups=mesh['x'=4,'c'=2,'y'=4,'q'=4,'r'=4] {'x','c'}, dimensions={0}, use_global_device_ids=true | all-gather | bytes 589824 | tf_op jit(solution)/shard_map/all_gather | solution.py:310
  91.6 5.4 %dense.1 = (bf16[256,1024]{1,0:T(8,128)(2,1)S(1)}, bf16[8,32,1024]{2,1,0:T(8,128)(2,1)}) custom-call(bf16[8,256,128]{2,1,0:T(8,128)(2,1)S(1)} %bitcast.33, bf16[256,1024]{1,0:T(8,128)(2,1)} %bitcast.44, f32[1,1024]{1,0:T(1,128)S(1)} %bitcast.42, bf16[1024,1024]{1,0:T(8,128)(2,1)} %all-gather.4.cloned.1.call-done.refs_0_, bf16[1024,512]{1,0:T(8,128)(2,1)} %refs_1_.1, ...), custom_call_target="tpu_custom_call" | custom-call | flops 1000 | bytes 1000 | tf_op jit(solution)/shard_map/dense/pallas_call | solution.py:218
  97.0 3.8 %all-to-all-start.2 = ((bf16[8,32,1024]{2,1,0:T(8,128)(2,1)}), bf16[8,32,1024]{2,1,0:T(8,128)(2,1)S(1)}, u32[]{:S(2)}, u32[]{:S(2)}) async-start(bf16[8,32,1024]{2,1,0:T(8,128)(2,1)} %get-tuple-element.13), calls=%async_computation.2 | async-start | bytes 1048576 | tf_op jit(solution)/shard_map/all_to_all | solution.py:312
  101.2 0.1 eq.76
  101.3 9.1 %all-to-all-done.2.terms_ref = bf16[8,32,1024]{2,1,0:T(8,128)(2,1)S(1)} async-done(((bf16[8,32,1024]{2,1,0:T(8,128)(2,1)}), bf16[8,32,1024]{2,1,0:T(8,128)(2,1)S(1)}, u32[]{:S(2)}, u32[]{:S(2)}) %all-to-all-start.2) | async-done | bytes 524320 | tf_op jit(solution)/shard_map/all_to_all | solution.py:312
  110.4 1.2 embed.1
  111.5 4.4 %all-to-all-start.3 = ((bf16[32,32,128]{2,1,0:T(8,128)(2,1)}), bf16[32,32,128]{2,1,0:T(8,128)(2,1)S(1)}, u32[]{:S(2)}, u32[]{:S(2)}) async-start(bf16[32,32,128]{2,1,0:T(8,128)(2,1)} %embed.1), calls=%async_computation.3 | async-start | bytes 524288 | tf_op jit(solution)/shard_map/all_to_all | solution.py:317
  116.0 0.1 fusion.3
  116.1 1.3 slice.30
  117.4 0.8 slice.29
  118.2 0.1 copy.44
  118.3 0.1 reshape.134
  118.4 0.1 copy.45
  118.5 0.1 reduce_window_sum.14.last_ref
  118.6 6.3 %all-to-all-done.3 = bf16[32,32,128]{2,1,0:T(8,128)(2,1)S(1)} async-done(((bf16[32,32,128]{2,1,0:T(8,128)(2,1)}), bf16[32,32,128]{2,1,0:T(8,128)(2,1)S(1)}, u32[]{:S(2)}, u32[]{:S(2)}) %all-to-all-start.3) | async-done | bytes 262176 | tf_op jit(solution)/shard_map/all_to_all | solution.py:317
  124.9 2.5 %match.1 = f32[32,16,128]{2,1,0:T(8,128)} custom-call(s32[64]{0:T(128)S(1)} %convert_element_type.45.need_ref, s32[64]{0:T(128)S(1)} %sub.16.first_ref, s32[64]{0:T(128)S(1)} %reduce_window_sum.14.last_ref, bf16[1024,128]{1,0:T(8,128)(2,1)S(1)} %bitcast.34, bf16[4096,128]{1,0:T(8,128)(2,1)S(1)} %bitcast.30, s32[16,128]{1,0:T(8,128)S(1)} %pad.14.pick_ref), custom_call_target="tpu_custom_call" | custom-call | flops 1000 | bytes 1000 | tf_op jit(solution)/shard_map/match/pallas_call | solution.py:157
  127.3 8.3 %all-to-all-start.4 = ((f32[32,16,128]{2,1,0:T(8,128)}), f32[32,16,128]{2,1,0:T(8,128)S(1)}, u32[]{:S(2)}, u32[]{:S(2)}) async-start(f32[32,16,128]{2,1,0:T(8,128)} %match.1), calls=%async_computation.4 | async-start | bytes 524288 | tf_op jit(solution)/shard_map/all_to_all | solution.py:333
  135.7 0.6 constant_dynamic-slice_fusion
  136.3 8.2 %all-to-all-done.4.terms_ref = f32[32,16,128]{2,1,0:T(8,128)S(1)} async-done(((f32[32,16,128]{2,1,0:T(8,128)}), f32[32,16,128]{2,1,0:T(8,128)S(1)}, u32[]{:S(2)}, u32[]{:S(2)}) %all-to-all-start.4) | async-done | bytes 262176 | tf_op jit(solution)/shard_map/all_to_all | solution.py:333
  144.5 0.7 total.1
  (52 shorter events, 0.8 us)
Async XLA Ops:
  7.2 19.3 %copy-start = (bf16[1024,128]{1,0:T(8,128)(2,1)S(1)}, bf16[1024,128]{1,0:T(8,128)(2,1)}, u32[]{:S(2)}) copy-start(bf16[1024,128]{1,0:T(8,128)(2,1)} %param.21) | copy-start | bytes 786436
  7.2 20.7 %copy-start.4 = (bf16[4,64,1024]{2,1,0:T(8,128)(2,1)S(1)}, bf16[4,64,1024]{2,1,0:T(8,128)(2,1)}, u32[]{:S(2)}) copy-start(bf16[4,64,1024]{2,1,0:T(8,128)(2,1)} %param.18) | copy-start | bytes 1572868
  7.2 20.7 %copy-start.5 = (bf16[1024,128]{1,0:T(8,128)(2,1)S(1)}, bf16[1024,128]{1,0:T(8,128)(2,1)}, u32[]{:S(2)}) copy-start(bf16[1024,128]{1,0:T(8,128)(2,1)} %param.20) | copy-start | bytes 786436
  7.2 21.0 %copy-start.6 = (bf16[1024,128]{1,0:T(8,128)(2,1)S(1)}, bf16[1024,128]{1,0:T(8,128)(2,1)}, u32[]{:S(2)}) copy-start(bf16[1024,128]{1,0:T(8,128)(2,1)} %param.19) | copy-start | bytes 786436
  7.2 21.5 %copy-start.8 = (s32[1,4]{1,0:T(1,128)S(1)}, s32[1,4]{1,0:T(1,128)}, u32[]{:S(2)}) copy-start(s32[1,4]{1,0:T(1,128)} %param.34) | copy-start | bytes 52
  7.2 21.5 %copy-start.9 = (s32[16]{0:T(128)S(1)}, s32[16]{0:T(128)}, u32[]{:S(2)}) copy-start(s32[16]{0:T(128)} %param.31) | copy-start | bytes 196
  7.2 84.4 %all-gather.4.cloned.1.call-start = ((), (), s32[]{:S(2)}) async-start(), calls=%async_computation.5 | async-start | bytes 2359296 | tf_op jit(solution)/shard_map/all_gather | solution.py:270
  9.5 32.4 %all-to-all-start = ((bf16[4,256,128]{2,1,0:T(8,128)(2,1)}), bf16[4,256,128]{2,1,0:T(8,128)(2,1)S(1)}, u32[]{:S(2)}, u32[]{:S(2)}) async-start(bf16[4,256,128]{2,1,0:T(8,128)(2,1)} %broadcast_in_dim.65), calls=%async_computation | async-start | bytes 524288 | tf_op jit(solution)/shard_map/all_to_all | solution.py:29
  25.1 16.8 %copy-start.7 = (bf16[256,128]{1,0:T(8,128)(2,1)S(1)}, bf16[256,128]{1,0:T(8,128)(2,1)}, u32[]{:S(2)}) copy-start(bf16[256,128]{1,0:T(8,128)(2,1)} %param.33) | copy-start | bytes 196612
  25.1 91.0 %all-gather.6.cloned.1.call-start = ((), (), s32[]{:S(2)}) async-start(), calls=%async_computation.6 | async-start | bytes 1183744 | tf_op jit(solution)/shard_map/all_gather | solution.py:288
  26.5 27.2 %copy-start.10 = (s32[128]{0:T(128)S(1)}, s32[128]{0:T(128)}, u32[]{:S(2)}) copy-start(s32[128]{0:T(128)} %param.30) | copy-start | bytes 1540
  41.9 49.7 %copy-start.3 = (f32[1024]{0:T(1024)S(1)}, f32[1024]{0:T(1024)}, u32[]{:S(2)}) copy-start(f32[1024]{0:T(1024)} %param.23) | copy-start | bytes 12292
  42.6 12.1 %collective-permute-start = (bf16[1024,128]{1,0:T(8,128)(2,1)S(1)}, bf16[1024,128]{1,0:T(8,128)(2,1)S(1)}, u32[]{:S(2)}, u32[]{:S(2)}) collective-permute-start(bf16[1024,128]{1,0:T(8,128)(2,1)S(1)} %bitcast.36), channel_id=1, source_target_pairs={{1,0},{2,1},{3,2},{4,3},{5,4},{6,5},{7,6},{8,7},{9,8},{10,9},{11,1... | collective-permute-start | bytes 786440 | tf_op jit(solution)/shard_map/ppermute | solution.py:33
  48.9 11.2 %collective-permute-start.1 = (bf16[1024,128]{1,0:T(8,128)(2,1)S(1)}, bf16[1024,128]{1,0:T(8,128)(2,1)S(1)}, u32[]{:S(2)}, u32[]{:S(2)}) collective-permute-start(bf16[1024,128]{1,0:T(8,128)(2,1)S(1)} %bitcast.37), channel_id=1, source_target_pairs={{2,0},{15,1},{4,2},{1,3},{6,4},{3,5},{8,6},{5,7},{10,8},{7,9},{12,... | collective-permute-start | bytes 786440 | tf_op jit(solution)/shard_map/ppermute | solution.py:282
  51.6 11.5 %collective-permute-start.2 = (bf16[1024,128]{1,0:T(8,128)(2,1)S(1)}, bf16[1024,128]{1,0:T(8,128)(2,1)S(1)}, u32[]{:S(2)}, u32[]{:S(2)}) collective-permute-start(bf16[1024,128]{1,0:T(8,128)(2,1)S(1)} %bitcast.38), channel_id=1, source_target_pairs={{15,0},{0,1},{1,2},{2,3},{3,4},{4,5},{5,6},{6,7},{7,8},{8,9},{9,10... | collective-permute-start | bytes 786440 | tf_op jit(solution)/shard_map/ppermute | solution.py:33
  91.6 18.8 %copy-start.1 = (bf16[1024,128]{1,0:T(8,128)(2,1)S(1)}, bf16[1024,128]{1,0:T(8,128)(2,1)}, u32[]{:S(2)}) copy-start(bf16[1024,128]{1,0:T(8,128)(2,1)} %w_project_ref.1) | copy-start | bytes 786436
  91.6 18.8 %copy-start.2 = (f32[1024]{0:T(1024)S(1)}, f32[1024]{0:T(1024)}, u32[]{:S(2)}) copy-start(f32[1024]{0:T(1024)} %param.26) | copy-start | bytes 12292
  97.0 13.3 %all-to-all-start.2 = ((bf16[8,32,1024]{2,1,0:T(8,128)(2,1)}), bf16[8,32,1024]{2,1,0:T(8,128)(2,1)S(1)}, u32[]{:S(2)}, u32[]{:S(2)}) async-start(bf16[8,32,1024]{2,1,0:T(8,128)(2,1)} %get-tuple-element.13), calls=%async_computation.2 | async-start | bytes 1048576 | tf_op jit(solution)/shard_map/all_to_all | solution.py:312
  111.5 13.3 %all-to-all-start.3 = ((bf16[32,32,128]{2,1,0:T(8,128)(2,1)}), bf16[32,32,128]{2,1,0:T(8,128)(2,1)S(1)}, u32[]{:S(2)}, u32[]{:S(2)}) async-start(bf16[32,32,128]{2,1,0:T(8,128)(2,1)} %embed.1), calls=%async_computation.3 | async-start | bytes 524288 | tf_op jit(solution)/shard_map/all_to_all | solution.py:317
  127.3 17.1 %all-to-all-start.4 = ((f32[32,16,128]{2,1,0:T(8,128)}), f32[32,16,128]{2,1,0:T(8,128)S(1)}, u32[]{:S(2)}, u32[]{:S(2)}) async-start(f32[32,16,128]{2,1,0:T(8,128)} %match.1), calls=%async_computation.4 | async-start | bytes 524288 | tf_op jit(solution)/shard_map/all_to_all | solution.py:333
Sparse Core Ops, SparseCore 0:
  10.2 38.5 all-gather.3
  50.9 61.8 all-gather.5
